TPU v7x, 32 devices: a whole 2x2x4 slice. The times are simulated.
32 devices in a mesh: groups: 2 (over x), gy: 8 (over z, y), gz: 2 (over core).
Axes of the slice: x: 2, y: 2, z: 4, core: 2. Of those that a mesh axis runs over, the one named last changes fastest.
Arguments:
- nodes: bfloat16 [32768, 512], P(('groups', 'gy', 'gz')), parts along dimension 0, may hold values from -6 to 6
- block_mask: int32 [256, 8], P(('groups', 'gy', 'gz')), parts along dimension 0, may hold values 0 or 1
- border_ids: int32 [4096], P(('groups', 'gy', 'gz')), parts along dimension 0, may hold values from 0 to 1023
- contact: bfloat16 [16384, 128], P(('groups', 'gy', 'gz')), parts along dimension 0, may hold values from -6 to 6
- edge_source: int32 [16384], P(('groups', 'gy', 'gz')), parts along dimension 0, may hold values from 0 to 1023
- edge_target: int32 [16384], P(('groups', 'gy', 'gz')), parts along dimension 0, may hold values from 0 to 1023
- edge_owner: int32 [16384, 1], P(('groups', 'gy', 'gz')), parts along dimension 0, may hold values from 0 to 15; in each aligned block of 512 rows (0 to 511, 512 to 1023, ...) at most 64 rows name the same one
- norm_gain: float32 [512], replicated, may hold values from 0.1 to 1.9
- w_qkv: bfloat16 [512, 1536], replicated, may hold values from -1 to 1
- w_attn_out: bfloat16 [512, 512], replicated, may hold values from -0.25 to 0.25
- w_source: bfloat16 [512, 512], replicated, may hold values from -0.25 to 0.25
- w_target: bfloat16 [512, 512], replicated, may hold values from -0.25 to 0.25
- w_contact: bfloat16 [128, 512], replicated, may hold values from -0.5 to 0.5
- w_score: float32 [512], replicated, may hold values from -0.25 to 0.25
Outputs:
- node_state: bfloat16 [32768, 512], P(('groups', 'gy', 'gz')), parts along dimension 0
- edge_scores: float32 [16384], P(('groups', 'gy', 'gz')), parts along dimension 0
There are 2 independent parts, one for each index of `groups`. A program takes and returns all parts, laid end to end along the dimension named above; an argument that names none is the same for every part. Nothing has to cross between parts.
Inputs may be any that keep to these rules, and one draw needn't show every extreme that they name: `edge_owner`: among the edges of one brick, no brick is named by more than 64 of them, a bound that some block reaches.
All inputs are finite; a program needn't handle non-finite values. No bound on the sum of `block_mask` on one device may be relied on, other than what follows from the above.
Results may differ from a plain program's by a relative error of at most 0.011.
Values may be sent and summed in bfloat16 or wider, within the bound.
No kernel may reach another device: no remote copies, remote signals or barrier semaphores. Data moves between devices by JAX's collectives and lax.ppermute only.
A program may use at most 128 MiB of HBM per device.

v0:
```python
import jax
import jax.numpy as jnp
from jax import lax
from jax.sharding import PartitionSpec as P

HEADS = 8
HEAD_DIM = 64
BLOCK = 128


def padded(block, sides, width):
    for axis, dim in sides:
        count = lax.axis_size(axis)
        forward = [(i, i + 1) for i in range(count - 1)]
        backward = [(target, source) for source, target in forward]
        low = lax.ppermute(
            lax.slice_in_dim(block, block.shape[dim] - width, None, axis=dim), axis, forward
        )
        high = lax.ppermute(lax.slice_in_dim(block, 0, width, axis=dim), axis, backward)
        block = jnp.concatenate([low, block, high], axis=dim)
    return block


def rms_norm(values, gain):
    wide = values.astype(jnp.float32)
    return wide * lax.rsqrt(jnp.mean(wide * wide, axis=-1, keepdims=True) + 1e-06) * gain


def attend(queries, keys, values, halo_keys, halo_values, blocks, valid):
    rows = queries.shape[0]
    width = queries.shape[1]
    span = min(512, rows)
    all_keys = jnp.concatenate([keys, halo_keys], 0)
    all_values = jnp.concatenate([values, halo_values], 0)
    count = all_keys.shape[0]
    key_heads = all_keys.reshape(count, HEADS, -1)
    value_heads = all_values.reshape(count, HEADS, -1)
    key_block = jnp.arange(rows) // BLOCK
    halo_allowed = jnp.repeat(valid, halo_keys.shape[0] // 4) > 0

    def attend_rows(start):
        query_rows = lax.dynamic_slice_in_dim(queries, start, span, 0).reshape(span, HEADS, -1)
        scores = jnp.einsum(
            "qhd,khd->hqk", query_rows, key_heads, preferred_element_type=jnp.float32
        ) * (1.0 / HEAD_DIM**0.5)
        row_block = (start + jnp.arange(span)) // BLOCK
        local_allowed = jnp.repeat(jnp.take(blocks, row_block, axis=0) > 0, BLOCK, axis=1)
        local_allowed = local_allowed | (row_block[:, None] == key_block[None, :])
        allowed = jnp.concatenate(
            [local_allowed, jnp.broadcast_to(halo_allowed[None, :], (span, halo_allowed.shape[0]))],
            1,
        )
        scores = jnp.where(allowed[None], scores, -1e30)
        row_max = jnp.max(scores, axis=-1, keepdims=True)
        weights = jnp.exp(scores - row_max)
        totals = jnp.sum(weights, axis=-1)
        weights_bf = weights.astype(jnp.bfloat16)
        mixed = (
            jnp.einsum("hqk,khd->qhd", weights_bf, value_heads, preferred_element_type=jnp.float32)
            / jnp.transpose(totals)[:, :, None]
        )
        return mixed.reshape(span, width).astype(jnp.bfloat16)

    starts = jnp.arange(rows // span) * span
    return lax.map(attend_rows, starts).reshape(rows, width)


def local(
    nodes,
    block_mask,
    border_ids,
    contact,
    edge_source,
    edge_target,
    edge_owner,
    norm_gain,
    w_qkv,
    w_attn_out,
    w_source,
    w_target,
    w_contact,
    w_score,
):
    width = nodes.shape[1]
    normed = rms_norm(nodes, norm_gain).astype(jnp.bfloat16)
    qkv = jnp.dot(normed, w_qkv, preferred_element_type=jnp.float32).astype(jnp.bfloat16)
    queries = qkv[:, :width]
    keys_values = qkv[:, width:]
    border = jnp.take(keys_values, border_ids, axis=0)
    beside_all = padded(border[None, None], (("gy", 0), ("gz", 1)), 1)
    halo = jnp.concatenate(
        [beside_all[0, 1], beside_all[2, 1], beside_all[1, 0], beside_all[1, 2]], 0
    )
    y_index = lax.axis_index("gy")
    z_index = lax.axis_index("gz")
    y_count = lax.axis_size("gy")
    z_count = lax.axis_size("gz")
    valid = jnp.stack(
        [y_index > 0, y_index < y_count - 1, z_index > 0, z_index < z_count - 1]
    ).astype(jnp.float32)
    attended = attend(
        queries,
        keys_values[:, :width],
        keys_values[:, width:],
        halo[:, :width],
        halo[:, width:],
        block_mask,
        valid,
    )
    state = nodes.astype(jnp.float32) + jnp.dot(
        attended, w_attn_out, preferred_element_type=jnp.float32
    )
    node_state = state.astype(jnp.bfloat16)
    source_table = jnp.dot(node_state, w_source, preferred_element_type=jnp.float32).astype(
        jnp.bfloat16
    )
    target_table = jnp.dot(node_state, w_target, preferred_element_type=jnp.float32).astype(
        jnp.bfloat16
    )
    bricks = y_count * z_count
    edge_count = edge_source.shape[0]
    capacity = max(2 * edge_count // bricks, 2)
    owner = edge_owner[:, 0]
    onehot = (owner[:, None] == jnp.arange(bricks, dtype=jnp.int32)[None, :]).astype(jnp.int32)
    slots = jnp.sum(jnp.cumsum(onehot, axis=0) * onehot, axis=1) - 1
    position = owner * capacity + slots
    placing = position[None, :] == jnp.arange(bricks * capacity, dtype=jnp.int32)[:, None]
    place_half = placing.astype(jnp.bfloat16)
    place_full = placing.astype(jnp.float32)
    target_float = jnp.dot(
        place_full, edge_target.astype(jnp.float32)[:, None], precision=lax.Precision.HIGHEST
    )
    target_slots = target_float[:, 0].astype(jnp.int32).reshape(bricks, capacity)
    hidden_units = source_table.shape[1]
    panel = contact.shape[1]
    source_rows = jnp.take(source_table, edge_source, axis=0)
    source_slots = (
        jnp.dot(place_half, source_rows, preferred_element_type=jnp.float32)
        .astype(jnp.bfloat16)
        .reshape(bricks, capacity, hidden_units)
    )
    contact_slots = (
        jnp.dot(place_half, contact, preferred_element_type=jnp.float32)
        .astype(jnp.bfloat16)
        .reshape(bricks, capacity, panel)
    )
    source_in = lax.all_to_all(source_slots, ("gy", "gz"), split_axis=0, concat_axis=0, tiled=True)
    contact_in = lax.all_to_all(
        contact_slots, ("gy", "gz"), split_axis=0, concat_axis=0, tiled=True
    )
    target_in = lax.all_to_all(target_slots, ("gy", "gz"), split_axis=0, concat_axis=0, tiled=True)
    target_rows = jnp.take(target_table, target_in, axis=0)
    pre = source_in.astype(jnp.float32) + target_rows.astype(jnp.float32)
    pre = pre + jnp.einsum("nmp,ph->nmh", contact_in, w_contact, preferred_element_type=jnp.float32)
    scores = jnp.einsum("nmh,h->nm", jax.nn.gelu(pre), w_score, precision=lax.Precision.HIGHEST)
    returned = lax.all_to_all(scores, ("gy", "gz"), split_axis=0, concat_axis=0, tiled=True)
    edge_scores = jnp.dot(
        returned.reshape(bricks * capacity), place_full, precision=lax.Precision.HIGHEST
    )
    return (node_state, edge_scores)


def solution(mesh):
    in_specs = (
        P(("groups", "gy", "gz"), None),
        P(("groups", "gy", "gz"), None),
        P(("groups", "gy", "gz")),
        P(("groups", "gy", "gz"), None),
        P(("groups", "gy", "gz")),
        P(("groups", "gy", "gz")),
        P(("groups", "gy", "gz"), None),
        P(),
        P(),
        P(),
        P(),
        P(),
        P(),
        P(),
    )
    out_specs = (P(("groups", "gy", "gz"), None), P(("groups", "gy", "gz")))
    return jax.shard_map(local, mesh=mesh, in_specs=in_specs, out_specs=out_specs, check_vma=False)
```

profile of v0, /device:TPU:9, one launch (start us, length us, event | category | flops | bytes accessed | tf_op | source)
XLA Modules:
  0.0 203.1 jit_solution(13762921980240081401)
XLA Ops:
  3.6 3.1 %convolution_convert_fusion = bf16[1024,1536]{1,0:T(8,128)(2,1)S(1)} fusion(bf16[512,1536]{1,0:T(8,128)(2,1)S(1)} %copy-done, bf16[1024,512]{1,0:T(8,128)(2,1)} %param.16, f32[512]{0:T(512)} %param.23, f32[1024]{0:T(1024)S(1)} %add_rsqrt_fusion), kind=kOutput, calls=%fused_computation.47 | convolution fusion | flops 1614282752 | bytes 5773312 | tf_op jit(solution)/shard_map/dot_general | solution.py:86
  6.7 1.6 copy-done.2
  8.3 1.6 slice.52
  10.0 2.9 %gather_fusion.1 = bf16[128,1024]{1,0:T(8,128)(2,1)S(1)} fusion(bf16[1024,1024]{1,0:T(8,128)(2,1)} %slice.52, s32[1024]{0:T(1024)S(1)} %pad_clamp_fusion.2), kind=kCustom, calls=%fused_computation.1 | custom fusion | bytes 524800 | tf_op jit(solution)/shard_map/jit(_take)/gather | solution.py:89
  13.0 3.1 %collective-permute-start = (bf16[1,1,128,1024]{3,2,1,0:T(8,128)(2,1)S(1)}, bf16[1,1,128,1024]{3,2,1,0:T(8,128)(2,1)S(1)}, u32[]{:S(2)}, u32[]{:S(2)}) collective-permute-start(bf16[1,1,128,1024]{3,2,1,0:T(8,128)(2,1)S(1)} %bitcast_select_fusion), channel_id=1, source_target_pairs={{0,2},{2,4},{4,6},{6,8},{8,10},{10,12},{12,14},{1,3},{3,5},{5,7},{... | collective-permute-start | bytes 786440 | tf_op jit(solution)/shard_map/ppermute | solution.py:16
  16.2 3.0 %collective-permute-start.1 = (bf16[1,1,128,1024]{3,2,1,0:T(8,128)(2,1)S(1)}, bf16[1,1,128,1024]{3,2,1,0:T(8,128)(2,1)S(1)}, u32[]{:S(2)}, u32[]{:S(2)}) collective-permute-start(bf16[1,1,128,1024]{3,2,1,0:T(8,128)(2,1)S(1)} %bitcast_select_fusion), channel_id=1, source_target_pairs={{2,0},{4,2},{6,4},{8,6},{10,8},{12,10},{14,12},{3,1},{5,3},{7,5},{... | collective-permute-start | bytes 786440 | tf_op jit(solution)/shard_map/ppermute | solution.py:19
  22.5 6.3 %all-to-all-start.1 = ((s32[16,1,64]{2,1,0:T(1,128)}), s32[16,1,64]{2,1,0:T(1,128)}, u32[]{:S(2)}, u32[]{:S(2)}) async-start(s32[16,1,64]{2,1,0:T(1,128)} %convert_element_type.91), calls=%async_computation.1 | async-start | bytes 16384 | tf_op jit(solution)/shard_map/all_to_all | solution.py:151
  29.8 2.4 %collective-permute-start.3 = (bf16[3,1,128,1024]{3,2,1,0:T(8,128)(2,1)S(1)}, bf16[3,1,128,1024]{3,2,1,0:T(8,128)(2,1)S(1)}, u32[]{:S(2)}, u32[]{:S(2)}) collective-permute-start(bf16[3,1,128,1024]{3,2,1,0:T(8,128)(2,1)S(1)} %pad_maximum_fusion.3), channel_id=1, source_target_pairs={{1,0},{3,2},{5,4},{7,6},{9,8},{11,10},{13,12},{15,14},{17,16},{19,... | collective-permute-start | bytes 2359304 | tf_op jit(solution)/shard_map/ppermute | solution.py:19
  35.4 3.0 %fusion.74 = (bf16[1024,512]{1,0:T(8,128)(2,1)S(1)}, bf16[1024,512]{1,0:T(8,128)(2,1)S(1)}, bf16[1024,512]{1,0:T(8,128)(2,1)}) fusion(bf16[1024,1536]{1,0:T(8,128)(2,1)} %copy-done.2), kind=kLoop, calls=%fused_computation.128 | loop fusion | bytes 6291456 | tf_op jit(solution)/shard_map/slice | solution.py:104
  40.0 2.6 %copy.24 = bf16[1536,512]{0,1:T(8,128)(2,1)} copy(bf16[1536,512]{1,0:T(8,128)(2,1)} %get-tuple-element.184) | data formatting | bytes 3145728 | tf_op jit(solution)/shard_map/concatenate | solution.py:33
  44.2 91.9 %while.13 = (s32[]{:T(128)}, bf16[2,512,512]{2,1,0:T(8,128)(2,1)}, s32[2]{0:T(128)S(1)}, s32[8,8]{1,0:T(8,128)S(1)}, bf16[1024,512]{1,0:T(8,128)(2,1)}, /*index=...) while((s32[]{:T(128)}, bf16[2,512,512]{2,1,0:T(8,128)(2,1)}, ...), condition=%wide.region_4.5_spmd.clone, body=%wide.region_1.4_spmd.clone.sunk | while | flops 1682216448 | bytes 95588056 | solution.py:65
  47.5 1.6 broadcast_in_dim.181
  54.3 12.0 %fusion.101 = (f32[8,512]{1,0:T(8,128)S(1)}, f32[8,512,1536]{2,1,0:T(8,128)}) fusion(pred[512,1536]{1,0:T(8,128)(4,1)S(1)} %pad_add_fusion.2, bf16[512,8,64]{0,2,1:T(8,128)(2,1)S(1)} %bitcast.104, bf16[1536,8,64]{0,2,1:T(8,128)(2,1)} %get-tuple-element.268), kind=kOutput, calls=%fused_computation.8.clone.1 | convolution fusion | flops 824176640 | bytes 28065792 | tf_op jit(solution)/shard_map/while/body/eval_jaxpr/qhd,khd->hqk/dot_general | solution.py:43
  66.2 11.8 %fusion.102 = f32[8,512]{1,0:T(8,128)S(1)} fusion(f32[8,512,1536]{2,1,0:T(8,128)} %get-tuple-element.237, f32[8,512]{1,0:T(8,128)S(1)} %get-tuple-element.238, pred[512,1536]{1,0:T(8,128)(4,1)S(1)} %pad_add_fusion.2), kind=kLoop, calls=%fused_computation.9.clone.1 | loop fusion | flops 25161728 | bytes 25985024 | tf_op jit(solution)/shard_map/while/body/eval_jaxpr/reduce_sum | solution.py:56
  78.0 11.1 %divide_convert_fusion.2 = bf16[512,8,64]{0,2,1:T(8,128)(2,1)S(1)} fusion(bf16[1536,8,64]{0,2,1:T(8,128)(2,1)S(1)} %copy-done.3, f32[8,512,1536]{2,1,0:T(8,128)} %get-tuple-element.237, f32[8,512]{1,0:T(8,128)S(1)} %get-tuple-element.238, pred[512,1536]{1,0:T(8,128)(4,1)S(1)} %pad_add_fusion.2, f32[512,8]{0,1:T(8,128)S(1)} %bitcast.111), kind=kOutput, calls=%fused_computation.16.clone.1 | convolution fusion | flops 830996480 | bytes 28082176 | tf_op jit(solution)/shard_map/while/body/eval_jaxpr/hqk,khd->qhd/dot_general | solution.py:59
  93.5 1.6 broadcast_in_dim.181
  100.2 12.0 %fusion.101 = (f32[8,512]{1,0:T(8,128)S(1)}, f32[8,512,1536]{2,1,0:T(8,128)}) fusion(pred[512,1536]{1,0:T(8,128)(4,1)S(1)} %pad_add_fusion.2, bf16[512,8,64]{0,2,1:T(8,128)(2,1)S(1)} %bitcast.104, bf16[1536,8,64]{0,2,1:T(8,128)(2,1)} %get-tuple-element.268), kind=kOutput, calls=%fused_computation.8.clone.1 | convolution fusion | flops 824176640 | bytes 28065792 | tf_op jit(solution)/shard_map/while/body/eval_jaxpr/qhd,khd->hqk/dot_general | solution.py:43
  112.2 11.8 %fusion.102 = f32[8,512]{1,0:T(8,128)S(1)} fusion(f32[8,512,1536]{2,1,0:T(8,128)} %get-tuple-element.237, f32[8,512]{1,0:T(8,128)S(1)} %get-tuple-element.238, pred[512,1536]{1,0:T(8,128)(4,1)S(1)} %pad_add_fusion.2), kind=kLoop, calls=%fused_computation.9.clone.1 | loop fusion | flops 25161728 | bytes 25985024 | tf_op jit(solution)/shard_map/while/body/eval_jaxpr/reduce_sum | solution.py:56
  124.0 11.1 %divide_convert_fusion.2 = bf16[512,8,64]{0,2,1:T(8,128)(2,1)S(1)} fusion(bf16[1536,8,64]{0,2,1:T(8,128)(2,1)S(1)} %copy-done.3, f32[8,512,1536]{2,1,0:T(8,128)} %get-tuple-element.237, f32[8,512]{1,0:T(8,128)S(1)} %get-tuple-element.238, pred[512,1536]{1,0:T(8,128)(4,1)S(1)} %pad_add_fusion.2, f32[512,8]{0,1:T(8,128)S(1)} %bitcast.111), kind=kOutput, calls=%fused_computation.16.clone.1 | convolution fusion | flops 830996480 | bytes 28082176 | tf_op jit(solution)/shard_map/while/body/eval_jaxpr/hqk,khd->qhd/dot_general | solution.py:59
  136.1 3.4 %fusion.26 = bf16[1024,512]{1,0:T(8,128)(2,1)} fusion(bf16[1024,512]{1,0:T(8,128)(2,1)} %param.16, bf16[1024,512]{1,0:T(8,128)(2,1)} %bitcast.118, bf16[512,512]{1,0:T(8,128)(2,1)} %param.25), kind=kOutput, calls=%fused_computation.55 | convolution fusion | flops 538443776 | bytes 3670016 | tf_op jit(solution)/shard_map/dot_general | solution.py:110
  139.6 6.6 %all-to-all-start.2 = ((bf16[16,64,128]{2,1,0:T(8,128)(2,1)}), bf16[16,64,128]{2,1,0:T(8,128)(2,1)S(1)}, u32[]{:S(2)}, u32[]{:S(2)}) async-start(bf16[16,64,128]{2,1,0:T(8,128)(2,1)} %bitcast.21), calls=%async_computation.2 | async-start | bytes 524288 | tf_op jit(solution)/shard_map/all_to_all | solution.py:148
  146.2 1.9 convolution_convert_fusion.2
  148.1 2.0 gather_fusion.2
  150.1 1.8 fusion.40
  151.9 2.9 %all-to-all-done.2 = bf16[16,64,128]{2,1,0:T(8,128)(2,1)S(1)} async-done(((bf16[16,64,128]{2,1,0:T(8,128)(2,1)}), bf16[16,64,128]{2,1,0:T(8,128)(2,1)S(1)}, u32[]{:S(2)}, u32[]{:S(2)}) %all-to-all-start.2) | async-done | bytes 262176 | tf_op jit(solution)/shard_map/all_to_all | solution.py:148
  154.8 5.6 %all-to-all-start = ((bf16[16,64,512]{2,1,0:T(8,128)(2,1)}), bf16[16,64,512]{2,1,0:T(8,128)(2,1)}, u32[]{:S(2)}, u32[]{:S(2)}) async-start(bf16[16,64,512]{2,1,0:T(8,128)(2,1)} %bitcast.15), calls=%async_computation | async-start | bytes 2097152 | tf_op jit(solution)/shard_map/all_to_all | solution.py:147
  161.9 1.8 fusion.62
  163.6 2.1 %convolution_convert_fusion.1 = bf16[1024,512]{1,0:T(8,128)(2,1)S(1)} fusion(bf16[1024,512]{1,0:T(8,128)(2,1)} %fusion.26, bf16[512,512]{1,0:T(8,128)(2,1)} %param.27), kind=kOutput, calls=%fused_computation.72 | convolution fusion | flops 537395200 | bytes 2621440 | tf_op jit(solution)/shard_map/dot_general | solution.py:117
  165.7 5.1 %gather_fusion.3 = bf16[1024,512]{1,0:T(8,128)(2,1)} fusion(bf16[1024,512]{1,0:T(8,128)(2,1)S(1)} %convolution_convert_fusion.1, s32[1024]{0:T(1024)S(1)} %broadcast_clamp_fusion), kind=kCustom, calls=%fused_computation.3 | custom fusion | bytes 2101248 | tf_op jit(solution)/shard_map/jit(_take)/gather | solution.py:152
  170.8 14.5 %all-to-all-done = bf16[16,64,512]{2,1,0:T(8,128)(2,1)} async-done(((bf16[16,64,512]{2,1,0:T(8,128)(2,1)}), bf16[16,64,512]{2,1,0:T(8,128)(2,1)}, u32[]{:S(2)}, u32[]{:S(2)}) %all-to-all-start) | async-done | bytes 1048608 | tf_op jit(solution)/shard_map/all_to_all | solution.py:147
  185.4 5.7 %fusion.42 = f32[16,1,64]{2,1,0:T(1,128)S(1)} fusion(f32[512,1,1]{0,1,2:T(1,128)S(1)} %bitcast.119, f32[16,64,512]{2,1,0:T(8,128)} %fusion.62, bf16[16,64,512]{2,1,0:T(8,128)(2,1)} %all-to-all-done, bf16[16,64,512]{2,1,0:T(8,128)(2,1)} %bitcast.110, pred[16,64]{1,0:T(8,128)(4,1)S(1)} %compare_and_fusion.1), kind=kOutput, calls=%fused_computation.75 | convolution fusion | flops 13107200 | bytes 4201472 | tf_op jit(solution)/shard_map/nmh,h->nm/dot_general | solution.py:155
  191.1 9.4 %all_to_all.31 = f32[16,1,64]{2,1,0:T(1,128)S(1)} all-to-all(f32[16,1,64]{2,1,0:T(1,128)S(1)} %fusion.42), channel_id=1, replica_groups=mesh['groups'=2,'gy'=8,'gz'=2] {'gy','gz'}, dimensions={0} | all-to-all | bytes 8192 | tf_op jit(solution)/shard_map/all_to_all | solution.py:156
  (108 shorter events, 32.2 us)
Async XLA Ops:
  0.6 3.0 %copy-start = (bf16[512,1536]{1,0:T(8,128)(2,1)S(1)}, bf16[512,1536]{1,0:T(8,128)(2,1)}, u32[]{:S(2)}) copy-start(bf16[512,1536]{1,0:T(8,128)(2,1)} %param.24) | copy-start | bytes 4718596
  6.7 1.7 copy-start.2
  9.9 9.3 %copy-start.5 = (s32[512,1]{0,1:T(1,128)S(1)}, s32[512,1]{0,1:T(1,128)}, u32[]{:S(2)}) copy-start(s32[512,1]{0,1:T(1,128)} %param.22) | copy-start | bytes 6148
  9.9 10.8 %copy-start.10 = (s32[512]{0:T(512)S(1)}, s32[512]{0:T(512)}, u32[]{:S(2)}) copy-start(s32[512]{0:T(512)} %param.21) | copy-start | bytes 6148
  9.9 18.9 %copy-start.7 = (s32[512]{0:T(512)S(1)}, s32[512]{0:T(512)}, u32[]{:S(2)}) copy-start(s32[512]{0:T(512)} %param.20) | copy-start | bytes 6148
  10.0 22.3 %copy-start.13 = (bf16[512,128]{1,0:T(8,128)(2,1)S(1)}, bf16[512,128]{1,0:T(8,128)(2,1)}, u32[]{:S(2)}) copy-start(bf16[512,128]{1,0:T(8,128)(2,1)} %param.19) | copy-start | bytes 393220
  13.0 16.5 %collective-permute-start = (bf16[1,1,128,1024]{3,2,1,0:T(8,128)(2,1)S(1)}, bf16[1,1,128,1024]{3,2,1,0:T(8,128)(2,1)S(1)}, u32[]{:S(2)}, u32[]{:S(2)}) collective-permute-start(bf16[1,1,128,1024]{3,2,1,0:T(8,128)(2,1)S(1)} %bitcast_select_fusion), channel_id=1, source_target_pairs={{0,2},{2,4},{4,6},{6,8},{8,10},{10,12},{12,14},{1,3},{3,5},{5,7},{... | collective-permute-start | bytes 786440 | tf_op jit(solution)/shard_map/ppermute | solution.py:16
  16.2 13.5 %collective-permute-start.1 = (bf16[1,1,128,1024]{3,2,1,0:T(8,128)(2,1)S(1)}, bf16[1,1,128,1024]{3,2,1,0:T(8,128)(2,1)S(1)}, u32[]{:S(2)}, u32[]{:S(2)}) collective-permute-start(bf16[1,1,128,1024]{3,2,1,0:T(8,128)(2,1)S(1)} %bitcast_select_fusion), channel_id=1, source_target_pairs={{2,0},{4,2},{6,4},{8,6},{10,8},{12,10},{14,12},{3,1},{5,3},{7,5},{... | collective-permute-start | bytes 786440 | tf_op jit(solution)/shard_map/ppermute | solution.py:19
  20.8 17.7 %copy-start.8 = (s32[512]{0:T(512)}, s32[512]{0:T(512)S(1)}, u32[]{:S(2)}) copy-start(s32[512]{0:T(512)S(1)} %add_add_fusion) | copy-start | bytes 6148
  22.5 117.1 %all-to-all-start.1 = ((s32[16,1,64]{2,1,0:T(1,128)}), s32[16,1,64]{2,1,0:T(1,128)}, u32[]{:S(2)}, u32[]{:S(2)}) async-start(s32[16,1,64]{2,1,0:T(1,128)} %convert_element_type.91), calls=%async_computation.1 | async-start | bytes 16384 | tf_op jit(solution)/shard_map/all_to_all | solution.py:151
  29.8 8.7 %collective-permute-start.3 = (bf16[3,1,128,1024]{3,2,1,0:T(8,128)(2,1)S(1)}, bf16[3,1,128,1024]{3,2,1,0:T(8,128)(2,1)S(1)}, u32[]{:S(2)}, u32[]{:S(2)}) collective-permute-start(bf16[3,1,128,1024]{3,2,1,0:T(8,128)(2,1)S(1)} %pad_maximum_fusion.3), channel_id=1, source_target_pairs={{1,0},{3,2},{5,4},{7,6},{9,8},{11,10},{13,12},{15,14},{17,16},{19,... | collective-permute-start | bytes 2359304 | tf_op jit(solution)/shard_map/ppermute | solution.py:19
  33.4 5.1 %collective-permute-start.2 = (bf16[3,1,128,1024]{3,2,1,0:T(8,128)(2,1)S(1)}, bf16[3,1,128,1024]{3,2,1,0:T(8,128)(2,1)S(1)}, u32[]{:S(2)}, u32[]{:S(2)}) collective-permute-start(bf16[3,1,128,1024]{3,2,1,0:T(8,128)(2,1)S(1)} %pad_maximum_fusion.3), channel_id=1, source_target_pairs={{0,1},{2,3},{4,5},{6,7},{8,9},{10,11},{12,13},{14,15},{16,17},{18,... | collective-permute-start | bytes 2359304 | tf_op jit(solution)/shard_map/ppermute | solution.py:16
  42.7 1.6 copy-start.1
  66.2 11.8 %copy-start.3 = (bf16[1536,8,64]{0,2,1:T(8,128)(2,1)S(1)}, bf16[1536,8,64]{0,2,1:T(8,128)(2,1)}, u32[]{:S(2)}) copy-start(bf16[1536,8,64]{0,2,1:T(8,128)(2,1)} %get-tuple-element.269) | copy-start | bytes 4718596 | tf_op jit(solution)/shard_map/while
  112.1 11.8 %copy-start.3 = (bf16[1536,8,64]{0,2,1:T(8,128)(2,1)S(1)}, bf16[1536,8,64]{0,2,1:T(8,128)(2,1)}, u32[]{:S(2)}) copy-start(bf16[1536,8,64]{0,2,1:T(8,128)(2,1)} %get-tuple-element.269) | copy-start | bytes 4718596 | tf_op jit(solution)/shard_map/while
  136.1 10.0 %copy-start.12 = (bf16[512,512]{1,0:T(8,128)(2,1)S(1)}, bf16[512,512]{1,0:T(8,128)(2,1)}, u32[]{:S(2)}) copy-start(bf16[512,512]{1,0:T(8,128)(2,1)} %param.26) | copy-start | bytes 1572868
  139.6 8.5 %copy-start.6 = (s32[1024]{0:T(1024)S(1)}, s32[1024]{0:T(1024)}, u32[]{:S(2)}) copy-start(s32[1024]{0:T(1024)} %pad_clamp_fusion.1) | copy-start | bytes 12292
  139.6 15.3 %all-to-all-start.2 = ((bf16[16,64,128]{2,1,0:T(8,128)(2,1)}), bf16[16,64,128]{2,1,0:T(8,128)(2,1)S(1)}, u32[]{:S(2)}, u32[]{:S(2)}) async-start(bf16[16,64,128]{2,1,0:T(8,128)(2,1)} %bitcast.21), calls=%async_computation.2 | async-start | bytes 524288 | tf_op jit(solution)/shard_map/all_to_all | solution.py:148
  148.1 2.0 copy-start.9
  148.1 2.0 copy-start.11
  150.1 11.8 %copy-start.4 = (bf16[128,512]{1,0:T(8,128)(2,1)S(1)}, bf16[128,512]{1,0:T(8,128)(2,1)}, u32[]{:S(2)}) copy-start(bf16[128,512]{1,0:T(8,128)(2,1)} %param.28) | copy-start | bytes 393220
  154.8 30.5 %all-to-all-start = ((bf16[16,64,512]{2,1,0:T(8,128)(2,1)}), bf16[16,64,512]{2,1,0:T(8,128)(2,1)}, u32[]{:S(2)}, u32[]{:S(2)}) async-start(bf16[16,64,512]{2,1,0:T(8,128)(2,1)} %bitcast.15), calls=%async_computation | async-start | bytes 2097152 | tf_op jit(solution)/shard_map/all_to_all | solution.py:147
  165.7 19.7 %copy-start.14 = (f32[512]{0:T(512)S(1)}, f32[512]{0:T(512)}, u32[]{:S(2)}) copy-start(f32[512]{0:T(512)} %param.29) | copy-start | bytes 6148
where the time goes:
time: 207 us; the launch traced here: 203 us
  matrix products  69.4 us (34%)
  other arithmetic  38.9 us (19%)
  local copies, waits for them, and re-layouts  33.9 us (16%)
  starting transfers between devices  28.5 us (14%)
  waiting for transfers between devices  17.6 us (9%)
  blocking collectives  9.43 us (5%)
  loops' own time  4.34 us (2%)
    dot_general x2, matrix products, attend_rows(): jnp.einsum('qhd,khd->hqk', query_rows, key_heads, preferred_element_type=...  23.9 us
    reduce_sum x2, other arithmetic, attend_rows(): totals = jnp.sum(weights, axis=-1)  23.6 us
    dot_general x2, matrix products, attend_rows(): jnp.einsum('hqk,khd->qhd', weights_bf, value_heads, preferred_element_typ...  22.2 us
    all_to_all x1, waiting for transfers between devices, local(): lax.all_to_all(source_slots, ('gy', 'gz'), split_axis=0, concat_axis=0, t...  14.5 us
    all_to_all x1, blocking collectives, local(): lax.all_to_all(scores, ('gy', 'gz'), split_axis=0, concat_axis=0, tiled=T...  9.43 us
    all_to_all x1, starting transfers between devices, local(): lax.all_to_all(contact_slots, ('gy', 'gz'), split_axis=0, concat_axis=0,...  6.58 us
    all_to_all x1, starting transfers between devices, local(): lax.all_to_all(target_slots, ('gy', 'gz'), split_axis=0, concat_axis=0, t...  6.28 us
    dot_general x1, matrix products, local(): jnp.einsum('nmh,h->nm', jax.nn.gelu(pre), w_score, precision=lax.Precisio...  5.71 us
  transfers between devices with their start and end apart: 7, of which 3 were waited for; matrix products, arithmetic and copies ran while one was open for 60% of the time, Pallas kernels for 0%

commit v1 on v0

v1 whole, which is shorter than its diff:
```python
import functools

import jax
import jax.numpy as jnp
from jax import lax
from jax.experimental import pallas as pl
from jax.experimental.pallas import tpu as pltpu
from jax.sharding import PartitionSpec as P

HEADS = 8
HEAD_DIM = 64
BLOCK = 128
PAIR = 2 * HEAD_DIM
SPAN = 256
F32 = jnp.float32
BF16 = jnp.bfloat16
NT = (((1,), (1,)), ((), ()))


def dot(lhs, rhs):
    return jnp.dot(lhs, rhs, preferred_element_type=F32)


def dot_nt(lhs, rhs):
    return lax.dot_general(lhs, rhs, NT, preferred_element_type=F32)


def ones_where(condition):
    return jnp.where(condition, 1.0, 0.0).astype(BF16)


def iota(shape, axis):
    return lax.broadcasted_iota(jnp.int32, shape, axis)


def columns_of(rows):
    count, lanes = rows.shape
    if count < 8:
        rows = jnp.concatenate([rows] * (8 // count), 0)
    return jnp.transpose(rows)


def picked(index_rows, table):
    count = index_rows.shape[0]
    columns = columns_of(index_rows)
    lanes = iota((128, table.shape[0]), 1)
    hot = [ones_where(columns[:, r : r + 1] == lanes) for r in range(count)]
    return dot(jnp.concatenate(hot, 0), table)


def normed_rows(values, gain):
    wide = values.astype(F32)
    mean = jnp.mean(wide * wide, axis=-1, keepdims=True)
    return (wide * lax.rsqrt(mean + 1e-06) * gain).astype(BF16)


def prepare(ids_ref, owner_ref, target_ref, nodes_ref, border_ref, request_ref, place_ref):
    bricks, capacity = request_ref.shape
    edges = owner_ref.shape[1]
    border_ref[...] = picked(ids_ref[...], nodes_ref[...]).astype(BF16)
    owner = owner_ref[...]
    target = target_ref[...]
    mine = iota((bricks, edges), 0) == owner
    mine_f = jnp.where(mine, 1.0, 0.0)
    before = ones_where(iota((edges, edges), 0) < iota((edges, edges), 1))
    counts = dot(mine_f.astype(BF16), before)
    slots = jnp.sum(counts * mine_f, axis=0, keepdims=True).astype(jnp.int32)
    place = owner * capacity + slots
    for r in range(edges // 128):
        place_ref[r : r + 1, :] = place[:, r * 128 : (r + 1) * 128]
    at_slot = ones_where(iota((capacity, edges), 0) == slots)
    high = (mine_f * (target >> 5).astype(F32)).astype(BF16)
    low = (mine_f * (target & 31).astype(F32)).astype(BF16)
    request = dot_nt(high, at_slot) * 32.0 + dot_nt(low, at_slot)
    request_ref[...] = request.astype(jnp.int32)


def project(nodes_ref, gain_ref, w_ref, qkv_ref):
    normed = normed_rows(nodes_ref[...], gain_ref[...])
    qkv_ref[...] = dot(normed, w_ref[...]).astype(BF16)


def attend(
    nodes_ref,
    q_ref,
    kv_ref,
    halo_ref,
    bias_ref,
    gain_ref,
    w_kv_ref,
    w_out_ref,
    w_source_ref,
    w_target_ref,
    state_ref,
    source_ref,
    target_ref,
    k_ref,
    v_ref,
):
    rows, width = kv_ref.shape[0], q_ref.shape[1]
    keys = k_ref.shape[0]
    span = q_ref.shape[0]
    step = pl.program_id(0)
    low_lanes = iota((keys, PAIR), 1) < HEAD_DIM

    @pl.when(step == 0)
    def _():
        halo = dot(normed_rows(halo_ref[...], gain_ref[...]), w_kv_ref[...]).astype(BF16)
        k_ref[:rows, :] = kv_ref[:, :width]
        k_ref[rows:, :] = halo[:, :width]
        for pair in range(width // PAIR):
            at = slice(pair * PAIR, (pair + 1) * PAIR)
            v_at = slice(width + pair * PAIR, width + (pair + 1) * PAIR)
            values = jnp.concatenate([kv_ref[:, v_at], halo[:, v_at]], 0)
            one = jnp.ones_like(values)
            v_ref[2 * pair] = jnp.where(low_lanes, values, one)
            v_ref[2 * pair + 1] = jnp.where(low_lanes, one, values)

    block = (step * span + iota((span, 128), 0)) // BLOCK
    q_block = ones_where(block == iota((span, 128), 1))
    bias = bias_ref[...]
    scale = 1.4426950408889634 / HEAD_DIM**0.5
    low = iota((span, PAIR), 1) < HEAD_DIM
    attended = []
    for pair in range(width // PAIR):
        at = slice(pair * PAIR, (pair + 1) * PAIR)
        q_pair = q_ref[:, at]
        k_pair = jnp.concatenate([k_ref[:, at], bias], 1)
        mixed = []
        for half in range(2):
            q_own = jnp.where(low if half == 0 else ~low, q_pair, jnp.zeros_like(q_pair))
            scores = dot_nt(jnp.concatenate([q_own, q_block], 1), k_pair)
            top = jnp.max(scores, axis=1, keepdims=True) * scale
            weights = jnp.exp2((scores * scale - top).astype(BF16))
            mixed.append(dot(weights, v_ref[2 * pair + half]))
        total = pltpu.roll(jnp.where(low, mixed[1], mixed[0]), HEAD_DIM, 1)
        attended.append((jnp.where(low, mixed[0], mixed[1]) / total).astype(BF16))
    state = nodes_ref[...].astype(F32) + dot(jnp.concatenate(attended, 1), w_out_ref[...])
    state = state.astype(BF16)
    state_ref[...] = state
    source_ref[...] = dot(state, w_source_ref[...]).astype(BF16)
    target_ref[...] = dot(state, w_target_ref[...]).astype(BF16)


def answer(request_ref, table_ref, out_ref):
    out_ref[...] = picked(request_ref[...], table_ref[...]).astype(BF16)


def own_part(index_ref, table_ref, contact_ref, w_ref, out_ref):
    out_ref[...] = picked(index_ref[...], table_ref[...]) + dot(contact_ref[...], w_ref[...])


def score(place_ref, answers_ref, part_ref, w_ref, out_ref):
    pre = part_ref[...] + picked(place_ref[...], answers_ref[...])
    weighted = jax.nn.gelu(pre) * w_ref[...]
    folded = weighted[:, :128]
    for at in range(128, weighted.shape[1], 128):
        folded = folded + weighted[:, at : at + 128]
    out_ref[...] = jnp.sum(jnp.transpose(folded), axis=0, keepdims=True)


def shape(dims, dtype):
    return jax.ShapeDtypeStruct(dims, dtype)


def neighbours(block):
    pieces, valid = [], []
    for axis in ("gy", "gz"):
        count = lax.axis_size(axis)
        index = lax.axis_index(axis)
        if count == 2:
            pieces.append(lax.ppermute(block, axis, [(0, 1), (1, 0)]))
            valid.append(jnp.bool_(True))
        elif count > 2:
            forward = [(i, i + 1) for i in range(count - 1)]
            backward = [(target, source) for source, target in forward]
            pieces.append(lax.ppermute(block, axis, forward))
            valid.append(index > 0)
            pieces.append(lax.ppermute(block, axis, backward))
            valid.append(index < count - 1)
    return jnp.concatenate(pieces, 0), jnp.stack(valid)


def local(
    nodes,
    block_mask,
    border_ids,
    contact,
    edge_source,
    edge_target,
    edge_owner,
    norm_gain,
    w_qkv,
    w_attn_out,
    w_source,
    w_target,
    w_contact,
    w_score,
):
    rows, width = nodes.shape
    edges = edge_source.shape[0]
    border_count = border_ids.shape[0]
    bricks = lax.axis_size("gy") * lax.axis_size("gz")
    capacity = max(2 * edges // bricks, 2)
    vmem = pltpu.CompilerParams(vmem_limit_bytes=60 * 1024 * 1024)

    border, request, place = pl.pallas_call(
        prepare,
        out_shape=(
            shape((border_count, width), BF16),
            shape((bricks, capacity), jnp.int32),
            shape((edges // 128, 128), jnp.int32),
        ),
        compiler_params=vmem,
    )(
        border_ids.reshape(border_count // 128, 128),
        edge_owner.reshape(1, edges),
        edge_target.reshape(1, edges),
        nodes,
    )
    halo, valid = neighbours(border)
    requests = lax.all_gather(request, ("gy", "gz"))
    me = lax.axis_index("gy") * lax.axis_size("gz") + lax.axis_index("gz")
    asked = lax.dynamic_index_in_dim(requests, me, 1, keepdims=False)
    asked = asked.reshape(bricks * capacity // 128, 128)

    gain = norm_gain.reshape(1, width)
    qkv = pl.pallas_call(
        project,
        out_shape=shape((rows, 3 * width), BF16),
        grid=(rows // SPAN,),
        in_specs=[
            pl.BlockSpec((SPAN, width), lambda i: (i, 0)),
            pl.BlockSpec((1, width), lambda i: (0, 0)),
            pl.BlockSpec((width, 3 * width), lambda i: (0, 0)),
        ],
        out_specs=pl.BlockSpec((SPAN, 3 * width), lambda i: (i, 0)),
        compiler_params=vmem,
    )(nodes, gain, w_qkv)

    blocks = rows // BLOCK
    seen = (block_mask > 0) | jnp.eye(blocks, dtype=jnp.bool_)
    seen = jnp.concatenate(
        [seen, jnp.broadcast_to(valid[None, :], (blocks, valid.shape[0]))], 1
    )
    seen = jnp.pad(seen.T, ((0, 0), (0, 128 - blocks)))
    bias = jnp.repeat(jnp.where(seen, 0.0, -1e30).astype(BF16), BLOCK, axis=0)
    keys = rows + halo.shape[0]

    def fixed(dims, at=(0, 0)):
        return pl.BlockSpec(dims, lambda i: at)

    def tiled(dims):
        return pl.BlockSpec(dims, lambda i: (i, 0))

    node_state, source_table, target_table = pl.pallas_call(
        attend,
        out_shape=(shape((rows, width), BF16),) * 3,
        grid=(rows // SPAN,),
        in_specs=[
            tiled((SPAN, width)),
            tiled((SPAN, width)),
            fixed((rows, 2 * width)),
            fixed((halo.shape[0], width)),
            fixed((keys, 128)),
            fixed((1, width)),
            fixed((width, 2 * width)),
            fixed((width, width)),
            fixed((width, width)),
            fixed((width, width)),
        ],
        out_specs=(tiled((SPAN, width)),) * 3,
        scratch_shapes=[
            pltpu.VMEM((keys, width), BF16),
            pltpu.VMEM((HEADS, keys, PAIR), BF16),
        ],
        compiler_params=vmem,
    )(
        nodes,
        qkv[:, :width],
        qkv[:, width:],
        halo,
        bias,
        gain,
        w_qkv[:, width:],
        w_attn_out,
        w_source,
        w_target,
    )

    hidden = w_target.shape[1]
    answers = pl.pallas_call(
        answer, out_shape=shape((bricks * capacity, hidden), BF16), compiler_params=vmem
    )(asked, target_table)
    answers = lax.all_to_all(
        answers.reshape(bricks, capacity, hidden),
        ("gy", "gz"),
        split_axis=0,
        concat_axis=0,
        tiled=True,
    ).reshape(bricks * capacity, hidden)
    part = pl.pallas_call(
        own_part, out_shape=shape((edges, hidden), F32), compiler_params=vmem
    )(edge_source.reshape(edges // 128, 128), source_table, contact, w_contact)
    scores = pl.pallas_call(score, out_shape=shape((1, edges), F32), compiler_params=vmem)(
        place, answers, part, w_score.reshape(1, hidden)
    )
    return (node_state, scores.reshape(edges))


def solution(mesh):
    split = ("groups", "gy", "gz")
    in_specs = (
        P(split, None),
        P(split, None),
        P(split),
        P(split, None),
        P(split),
        P(split),
        P(split, None),
        P(),
        P(),
        P(),
        P(),
        P(),
        P(),
        P(),
    )
    out_specs = (P(split, None), P(split))
    return jax.shard_map(local, mesh=mesh, in_specs=in_specs, out_specs=out_specs, check_vma=False)
```

time: 207 us -> 112 us (0.54); the launches traced: 203 us -> 112 us
  matrix products: 69.4 us -> 0 us
  Pallas kernels: 0 us -> 47 us
  other arithmetic: 38.9 us -> 0.94 us
  local copies, waits for them, and re-layouts: 33.9 us -> 11 us
  starting transfers between devices: 28.5 us -> 12.5 us
  blocking collectives: 9.43 us -> 17.9 us
  loops' own time: 4.34 us -> 0 us
  waiting for transfers between devices: 17.6 us -> 21.6 us
    dot_general x14 -> x0, matrix products: 69.4 us -> none  [the longest x2 23.9 us: attend_rows(): jnp.einsum('qhd,khd->hqk', query_rows, key_heads, preferred_element_type=...]
    pallas_call x0 -> x6, Pallas kernels: none -> 47 us  [the longest x1 28.7 us: local(): pl.pallas_call(attend, out_shape=(shape((rows, width), BF16),) * 3, grid=...]
    reduce_sum x4 -> x0, other arithmetic: 25.2 us -> none  [the longest x2 23.6 us: attend_rows(): totals = jnp.sum(weights, axis=-1)]
    all_gather x0 -> x1, blocking collectives: none -> 17.9 us  [local(): requests = lax.all_gather(request, ('gy', 'gz'))]
    gather x5 -> x0, local copies, waits for them, and re-layouts: 12.1 us -> none  [the longest x1 5.1 us: local(): target_rows = jnp.take(target_table, target_in, axis=0)]
    all_to_all x3 -> x1, starting transfers between devices: 18.4 us -> 6.54 us  [local(): lax.all_to_all(answers.reshape(bricks, capacity, hidden), ('gy', 'gz'), s...]
    all_to_all x1 -> x0, blocking collectives: 9.43 us -> none  [local(): lax.all_to_all(scores, ('gy', 'gz'), split_axis=0, concat_axis=0, tiled=T...]
    select_n x10 -> x0, other arithmetic: 4.39 us -> none  [the longest x2 1.41 us: attend_rows(): jnp.take(blocks, row_block, axis=0) > 0]
  transfers between devices with their start and end apart: 7 -> 4, of which waited for: 3 -> 1; matrix products, arithmetic and copies ran while one was open for 60% -> 8% of each run, Pallas kernels for 0% -> 8%
where the time goes in v1:
time: 112 us
  Pallas kernels  47 us (42%)
  waiting for transfers between devices  21.6 us (19%)
  blocking collectives  17.9 us (16%)
  starting transfers between devices  12.5 us (11%)
  local copies, waits for them, and re-layouts  11 us (10%)
    pallas_call x1, Pallas kernels, local(): pl.pallas_call(attend, out_shape=(shape((rows, width), BF16),) * 3, grid=...  28.7 us
    all_to_all x1, waiting for transfers between devices, local(): lax.all_to_all(answers.reshape(bricks, capacity, hidden), ('gy', 'gz'), s...  21.6 us
    all_gather x1, blocking collectives, local(): requests = lax.all_gather(request, ('gy', 'gz'))  17.9 us
    all_to_all x1, starting transfers between devices, local(): lax.all_to_all(answers.reshape(bricks, capacity, hidden), ('gy', 'gz'), s...  6.54 us
    pallas_call x1, Pallas kernels, local(): pl.pallas_call(project, out_shape=shape((rows, 3 * width), BF16), grid=(r...  5.6 us
    pallas_call x1, Pallas kernels, local(): pl.pallas_call(answer, out_shape=shape((bricks * capacity, hidden), BF16)...  3.58 us
    pallas_call x1, Pallas kernels, local(): pl.pallas_call(score, out_shape=shape((1, edges), F32), compiler_params=v...  3.38 us
    pallas_call x1, Pallas kernels, local(): pl.pallas_call(own_part, out_shape=shape((edges, hidden), F32), compiler_...  3.25 us
  transfers between devices with their start and end apart: 4, of which 1 were waited for; matrix products, arithmetic and copies ran while one was open for 8% of the time, Pallas kernels for 8%

profile of v1, /device:TPU:9, one launch (start us, length us, event | category | flops | bytes accessed | tf_op | source)
XLA Modules:
  0.0 111.6 jit_solution(9961994363741710856)
XLA Ops:
  0.6 2.5 %shard_map.150 = (bf16[128,512]{1,0:T(8,128)(2,1)}, s32[16,64]{1,0:T(8,128)}, s32[4,128]{1,0:T(4,128)}) custom-call(s32[1,128]{1,0:T(1,128)} %bitcast.30, s32[1,512]{1,0:T(1,128)} %bitcast.25, s32[1,512]{1,0:T(1,128)} %bitcast.26, bf16[1024,512]{1,0:T(8,128)(2,1)} %nodes_ref.5), custom_call_target="tpu_custom_call" | custom-call | tf_op jit(solution)/shard_map/pallas_call | solution.py:207
  3.1 0.7 collective-permute-start.2
  3.8 3.0 %collective-permute-start.1 = (bf16[128,512]{1,0:T(8,128)(2,1)}, bf16[128,512]{1,0:T(8,128)(2,1)S(1)}, u32[]{:S(2)}, u32[]{:S(2)}) collective-permute-start(bf16[128,512]{1,0:T(8,128)(2,1)} %get-tuple-element.8), channel_id=1, source_target_pairs={{2,0},{4,2},{6,4},{8,6},{10,8},{12,10},{14,12},{3,1},{5,3},{7,5},{... | collective-permute-start | bytes 393224 | tf_op jit(solution)/shard_map/ppermute | solution.py:179
  6.8 2.2 %collective-permute-start = (bf16[128,512]{1,0:T(8,128)(2,1)}, bf16[128,512]{1,0:T(8,128)(2,1)S(1)}, u32[]{:S(2)}, u32[]{:S(2)}) collective-permute-start(bf16[128,512]{1,0:T(8,128)(2,1)} %get-tuple-element.8), channel_id=1, source_target_pairs={{0,2},{2,4},{4,6},{6,8},{8,10},{10,12},{12,14},{1,3},{3,5},{5,7},{... | collective-permute-start | bytes 393224 | tf_op jit(solution)/shard_map/ppermute | solution.py:177
  9.1 0.8 copy.18
  9.9 17.9 %all-gather = s32[256,64]{1,0:T(8,128)S(1)} all-gather(s32[16,64]{1,0:T(8,128)} %get-tuple-element.11), channel_id=2, replica_groups=mesh['groups'=2,'gy'=8,'gz'=2] {'gy','gz'}, dimensions={0}, use_global_device_ids=true | all-gather | bytes 69632 | tf_op jit(solution)/shard_map/all_gather | solution.py:222
  27.7 0.1 pad_add_fusion
  27.8 0.1 pad.6.clone
  27.9 0.1 add_bitcast_fusion
  28.0 2.3 %slice.11.w_kv_ref = bf16[512,1024]{1,0:T(8,128)(2,1)} slice(bf16[512,1536]{1,0:T(8,128)(2,1)} %w_ref.2), slice={[0:512], [512:1536]} | slice | bytes 2097152 | tf_op jit(solution)/shard_map/slice | solution.py:285
  30.3 5.6 %shard_map.149 = bf16[1024,1536]{1,0:T(8,128)(2,1)} custom-call(bf16[1024,512]{1,0:T(8,128)(2,1)} %nodes_ref.5, f32[1,512]{1,0:T(1,128)} %bitcast.23, bf16[512,1536]{1,0:T(8,128)(2,1)} %w_ref.2), custom_call_target="tpu_custom_call" | custom-call | tf_op jit(solution)/shard_map/pallas_call | solution.py:228
  35.9 2.3 %slice.12.q_ref = bf16[1024,512]{1,0:T(8,128)(2,1)} slice(bf16[1024,1536]{1,0:T(8,128)(2,1)} %shard_map.149), slice={[0:1024], [0:512]} | slice | bytes 2097152 | tf_op jit(solution)/shard_map/slice | solution.py:280
  38.2 3.1 %slice.13.kv_ref = bf16[1024,1024]{1,0:T(8,128)(2,1)} slice(bf16[1024,1536]{1,0:T(8,128)(2,1)} %shard_map.149), slice={[0:1024], [512:1536]} | slice | bytes 4194304 | tf_op jit(solution)/shard_map/slice | solution.py:281
  41.3 0.7 reshape.44.request_ref
  42.0 0.0 collective-permute-done.2
  42.0 0.0 collective-permute-done.1
  42.0 0.0 collective-permute-done
  42.0 0.8 pad_maximum_fusion.halo_ref
  42.8 0.8 broadcast_in_dim.20
  43.5 28.7 %shard_map.151 = (bf16[1024,512]{1,0:T(8,128)(2,1)}, bf16[1024,512]{1,0:T(8,128)(2,1)}, bf16[1024,512]{1,0:T(8,128)(2,1)}) custom-call(bf16[1024,512]{1,0:T(8,128)(2,1)} %nodes_ref.5, bf16[1024,512]{1,0:T(8,128)(2,1)} %slice.12.q_ref, bf16[1024,1024]{1,0:T(8,128)(2,1)} %slice.13.kv_ref, bf16[384,512]{1,0:T(8,128)(2,1)} %pad_maximum_fusion.halo_ref, ...), custom_call_target="tpu_custom_call" | custom-call | tf_op jit(solution)/shard_map/pallas_call | solution.py:256
  72.2 3.6 %shard_map.152 = bf16[1024,512]{1,0:T(8,128)(2,1)} custom-call(s32[8,128]{1,0:T(8,128)} %reshape.44.request_ref, bf16[1024,512]{1,0:T(8,128)(2,1)} %get-tuple-element.12.table_ref), custom_call_target="tpu_custom_call" | custom-call | tf_op jit(solution)/shard_map/pallas_call | solution.py:292
  75.8 6.5 %all-to-all-start = ((bf16[16,64,512]{2,1,0:T(8,128)(2,1)}), bf16[16,64,512]{2,1,0:T(8,128)(2,1)S(1)}, u32[]{:S(2)}, u32[]{:S(2)}) async-start(bf16[16,64,512]{2,1,0:T(8,128)(2,1)} %bitcast.19), calls=%async_computation | async-start | bytes 2097152 | tf_op jit(solution)/shard_map/all_to_all | solution.py:295
  82.3 3.3 %shard_map.153.part_ref = f32[512,512]{1,0:T(8,128)} custom-call(s32[4,128]{1,0:T(4,128)} %bitcast.29, bf16[1024,512]{1,0:T(8,128)(2,1)} %get-tuple-element.13.table_ref, bf16[512,128]{1,0:T(8,128)(2,1)} %contact_ref.1, bf16[128,512]{1,0:T(8,128)(2,1)} %w_ref.3), custom_call_target="tpu_custom_call" | custom-call | tf_op jit(solution)/shard_map/pallas_call | solution.py:302
  85.6 21.6 %all-to-all-done = bf16[16,64,512]{2,1,0:T(8,128)(2,1)S(1)} async-done(((bf16[16,64,512]{2,1,0:T(8,128)(2,1)}), bf16[16,64,512]{2,1,0:T(8,128)(2,1)S(1)}, u32[]{:S(2)}, u32[]{:S(2)}) %all-to-all-start) | async-done | bytes 1048608 | tf_op jit(solution)/shard_map/all_to_all | solution.py:295
  107.2 0.0 copy-start
  107.2 1.0 copy-done
  108.2 3.4 %shard_map.154 = f32[1,512]{1,0:T(1,128)} custom-call(s32[4,128]{1,0:T(4,128)} %get-tuple-element.10.place_ref, bf16[1024,512]{1,0:T(8,128)(2,1)} %bitcast.18, f32[512,512]{1,0:T(8,128)} %shard_map.153.part_ref, f32[1,512]{1,0:T(1,128)} %bitcast.27), custom_call_target="tpu_custom_call" | custom-call | tf_op jit(solution)/shard_map/pallas_call | solution.py:305
  (3 shorter events, 0.0 us)
Async XLA Ops:
  3.1 38.8 %collective-permute-start.2 = (bf16[128,512]{1,0:T(8,128)(2,1)}, bf16[128,512]{1,0:T(8,128)(2,1)S(1)}, u32[]{:S(2)}, u32[]{:S(2)}) collective-permute-start(bf16[128,512]{1,0:T(8,128)(2,1)} %get-tuple-element.8), channel_id=1, source_target_pairs={{0,1},{1,0},{2,3},{3,2},{4,5},{5,4},{6,7},{7,6},{8,9},{9,8},{10,11... | collective-permute-start | bytes 393224 | tf_op jit(solution)/shard_map/ppermute | solution.py:172
  3.8 38.2 %collective-permute-start.1 = (bf16[128,512]{1,0:T(8,128)(2,1)}, bf16[128,512]{1,0:T(8,128)(2,1)S(1)}, u32[]{:S(2)}, u32[]{:S(2)}) collective-permute-start(bf16[128,512]{1,0:T(8,128)(2,1)} %get-tuple-element.8), channel_id=1, source_target_pairs={{2,0},{4,2},{6,4},{8,6},{10,8},{12,10},{14,12},{3,1},{5,3},{7,5},{... | collective-permute-start | bytes 393224 | tf_op jit(solution)/shard_map/ppermute | solution.py:179
  6.8 35.1 %collective-permute-start = (bf16[128,512]{1,0:T(8,128)(2,1)}, bf16[128,512]{1,0:T(8,128)(2,1)S(1)}, u32[]{:S(2)}, u32[]{:S(2)}) collective-permute-start(bf16[128,512]{1,0:T(8,128)(2,1)} %get-tuple-element.8), channel_id=1, source_target_pairs={{0,2},{2,4},{4,6},{6,8},{8,10},{10,12},{12,14},{1,3},{3,5},{5,7},{... | collective-permute-start | bytes 393224 | tf_op jit(solution)/shard_map/ppermute | solution.py:177
  75.8 31.4 %all-to-all-start = ((bf16[16,64,512]{2,1,0:T(8,128)(2,1)}), bf16[16,64,512]{2,1,0:T(8,128)(2,1)S(1)}, u32[]{:S(2)}, u32[]{:S(2)}) async-start(bf16[16,64,512]{2,1,0:T(8,128)(2,1)} %bitcast.19), calls=%async_computation | async-start | bytes 2097152 | tf_op jit(solution)/shard_map/all_to_all | solution.py:295
  107.2 1.0 copy-start

commit v2 on v1

v2 whole, which is shorter than its diff:
```python
import functools

import jax
import jax.numpy as jnp
from jax import lax
from jax.experimental import pallas as pl
from jax.experimental.pallas import tpu as pltpu
from jax.sharding import PartitionSpec as P

HEADS = 8
HEAD_DIM = 64
BLOCK = 128
PAIR = 2 * HEAD_DIM
SPAN = 256
F32 = jnp.float32
BF16 = jnp.bfloat16
NT = (((1,), (1,)), ((), ()))


def dot(lhs, rhs):
    return jnp.dot(lhs, rhs, preferred_element_type=F32)


def dot_nt(lhs, rhs):
    return lax.dot_general(lhs, rhs, NT, preferred_element_type=F32)


def ones_where(condition):
    return jnp.where(condition, 1.0, 0.0).astype(BF16)


def iota(shape, axis):
    return lax.broadcasted_iota(jnp.int32, shape, axis)


def columns_of(rows):
    count, lanes = rows.shape
    if count < 8:
        rows = jnp.concatenate([rows] * (8 // count), 0)
    return jnp.transpose(rows)


def picked(index_rows, table):
    count = index_rows.shape[0]
    columns = columns_of(index_rows)
    lanes = iota((128, table.shape[0]), 1)
    hot = [ones_where(columns[:, r : r + 1] == lanes) for r in range(count)]
    return dot(jnp.concatenate(hot, 0), table)


def normed_rows(values, gain):
    wide = values.astype(F32)
    mean = jnp.mean(wide * wide, axis=-1, keepdims=True)
    return (wide * lax.rsqrt(mean + 1e-06) * gain).astype(BF16)


def prepare(ids_ref, owner_ref, target_ref, nodes_ref, border_ref, request_ref, place_ref, *, dims):
    bricks, capacity = dims
    edges = owner_ref.shape[1]
    border_ref[...] = picked(ids_ref[...], nodes_ref[...]).astype(BF16)
    owner = owner_ref[...]
    target = target_ref[...]
    mine = iota((bricks, edges), 0) == owner
    mine_f = jnp.where(mine, 1.0, 0.0)
    before = ones_where(iota((edges, edges), 0) < iota((edges, edges), 1))
    counts = dot(mine_f.astype(BF16), before)
    slots = jnp.sum(counts * mine_f, axis=0, keepdims=True).astype(jnp.int32)
    place = owner * capacity + slots
    for r in range(edges // 128):
        place_ref[r : r + 1, :] = place[:, r * 128 : (r + 1) * 128]
    at_slot = ones_where(iota((128, edges), 0) == slots)
    high = (mine_f * (target >> 5).astype(F32)).astype(BF16)
    low = (mine_f * (target & 31).astype(F32)).astype(BF16)
    request = dot_nt(high, at_slot) * 32.0 + dot_nt(low, at_slot)
    request_ref[:bricks, :] = request.astype(jnp.int32)
    if request_ref.shape[0] > bricks:
        request_ref[bricks:, :] = jnp.zeros_like(request_ref[bricks:, :])


def project(nodes_ref, gain_ref, w_ref, q_ref, kv_ref):
    width = nodes_ref.shape[1]
    normed = normed_rows(nodes_ref[...], gain_ref[...])
    scale = 1.4426950408889634 / HEAD_DIM**0.5
    q_ref[...] = (dot(normed, w_ref[:, :width]) * scale).astype(BF16)
    kv_ref[...] = dot(normed, w_ref[:, width:]).astype(BF16)


def attend(*refs, pieces):
    valid_ref, nodes_ref, q_ref, kv_ref = refs[:4]
    halo_refs = refs[4 : 4 + pieces]
    (
        mask_ref,
        gain_ref,
        w_qkv_ref,
        w_out_ref,
        w_target_ref,
        request_ref,
        state_ref,
        answer_ref,
        v_ref,
    ) = refs[4 + pieces :]
    rows, width = q_ref.shape
    blocks = rows // BLOCK
    keys = v_ref.shape[1]
    border = halo_refs[0].shape[0]
    halo_nodes = jnp.concatenate([ref[...] for ref in halo_refs], 0)
    halo = dot(normed_rows(halo_nodes, gain_ref[...]), w_qkv_ref[:, width:]).astype(BF16)
    low_keys = iota((keys, PAIR), 1) < HEAD_DIM
    low = iota((rows, PAIR), 1) < HEAD_DIM

    lane = iota((blocks, 128), 1)
    row = iota((blocks, 128), 0)
    seen = dot(mask_ref[...].astype(F32).astype(BF16), ones_where(row == lane))
    seen = jnp.where(row == lane, 1.0, seen)
    for h in range(pieces):
        seen = jnp.where(lane == blocks + h, valid_ref[h].astype(F32), seen)
    bias = jnp.where(seen > 0.5, 0.0, -1e30).astype(BF16)
    bias = jnp.concatenate(
        [jnp.broadcast_to(bias[b : b + 1, :], (BLOCK, 128)) for b in range(blocks)], 0
    )
    own = iota((rows, 128), 0) // BLOCK
    far = blocks + iota((keys - rows, 128), 0) // border
    key_block = jnp.concatenate(
        [ones_where(own == iota(own.shape, 1)), ones_where(far == iota(far.shape, 1))], 0
    )

    attended = []
    for pair in range(width // PAIR):
        at = slice(pair * PAIR, (pair + 1) * PAIR)
        v_at = slice(width + pair * PAIR, width + (pair + 1) * PAIR)
        values = jnp.concatenate([kv_ref[:, v_at], halo[:, v_at]], 0)
        one = jnp.ones_like(values)
        v_ref[2 * pair] = jnp.where(low_keys, values, one)
        v_ref[2 * pair + 1] = jnp.where(low_keys, one, values)
        q_pair = q_ref[:, at]
        k_pair = jnp.concatenate([kv_ref[:, at], halo[:, at]], 0)
        k_pair = jnp.concatenate([k_pair, key_block], 1)
        mixed = []
        for half in range(2):
            q_own = jnp.where(low if half == 0 else ~low, q_pair, jnp.zeros_like(q_pair))
            scores = dot_nt(jnp.concatenate([q_own, bias], 1), k_pair)
            fold = scores[:, :128]
            for c in range(128, keys, 128):
                fold = jnp.maximum(fold, scores[:, c : c + 128])
            top = jnp.max(fold, axis=1, keepdims=True)
            weights = jnp.exp2((scores - top).astype(BF16))
            mixed.append(dot(weights, v_ref[2 * pair + half]))
        total = pltpu.roll(jnp.where(low, mixed[1], mixed[0]), HEAD_DIM, 1)
        attended.append((jnp.where(low, mixed[0], mixed[1]) / total).astype(BF16))
    state = nodes_ref[...].astype(F32) + dot(jnp.concatenate(attended, 1), w_out_ref[...])
    state = state.astype(BF16)
    state_ref[...] = state
    table = dot(state, w_target_ref[...]).astype(BF16)
    answer_ref[...] = picked(request_ref[...], table).astype(BF16)


def own_part(index_ref, state_ref, w_source_ref, contact_ref, w_ref, out_ref):
    rows = picked(index_ref[...], state_ref[...]).astype(BF16)
    rows = dot(rows, w_source_ref[...]).astype(BF16).astype(F32)
    out_ref[...] = rows + dot(contact_ref[...], w_ref[...])


def score(place_ref, answers_ref, part_ref, w_ref, out_ref):
    pre = part_ref[...] + picked(place_ref[...], answers_ref[...])
    weighted = jax.nn.gelu(pre) * w_ref[...]
    folded = weighted[:, :128]
    for at in range(128, weighted.shape[1], 128):
        folded = folded + weighted[:, at : at + 128]
    out_ref[...] = jnp.sum(jnp.transpose(folded), axis=0, keepdims=True)


def shape(dims, dtype):
    return jax.ShapeDtypeStruct(dims, dtype)


def neighbours(block):
    pieces, valid = [], []
    for axis in ("gy", "gz"):
        count = lax.axis_size(axis)
        index = lax.axis_index(axis)
        for first in range(min(2, count - 1)):
            swaps = []
            for i in range(first, count - 1, 2):
                swaps += [(i, i + 1), (i + 1, i)]
            pieces.append(lax.ppermute(block, axis, swaps))
            beside = jnp.where((index - first) % 2 == 0, index + 1, index - 1)
            valid.append((beside >= 0) & (beside < count))
    return pieces, jnp.stack(valid).astype(jnp.int32)


def local(
    nodes,
    block_mask,
    border_ids,
    contact,
    edge_source,
    edge_target,
    edge_owner,
    norm_gain,
    w_qkv,
    w_attn_out,
    w_source,
    w_target,
    w_contact,
    w_score,
):
    rows, width = nodes.shape
    edges = edge_source.shape[0]
    border_count = border_ids.shape[0]
    bricks = lax.axis_size("gy") * lax.axis_size("gz")
    capacity = max(2 * edges // bricks, 2)
    vmem = pltpu.CompilerParams(vmem_limit_bytes=60 * 1024 * 1024)

    border, request, place = pl.pallas_call(
        functools.partial(prepare, dims=(bricks, capacity)),
        out_shape=(
            shape((border_count, width), BF16),
            shape((max(256, bricks), 128), jnp.int32),
            shape((edges // 128, 128), jnp.int32),
        ),
        compiler_params=vmem,
    )(
        border_ids.reshape(border_count // 128, 128),
        edge_owner.reshape(1, edges),
        edge_target.reshape(1, edges),
        nodes,
    )
    halo, valid = neighbours(border)
    requests = lax.all_gather(request, ("gy", "gz"))
    me = lax.axis_index("gy") * lax.axis_size("gz") + lax.axis_index("gz")
    asked = lax.dynamic_index_in_dim(requests, me, 1, keepdims=False)[:, :capacity]
    asked = asked.reshape(bricks * capacity // 128, 128)

    gain = norm_gain.reshape(1, width)
    q, kv = pl.pallas_call(
        project,
        out_shape=(shape((rows, width), BF16), shape((rows, 2 * width), BF16)),
        grid=(rows // SPAN,),
        in_specs=[
            pl.BlockSpec((SPAN, width), lambda i: (i, 0)),
            pl.BlockSpec((1, width), lambda i: (0, 0)),
            pl.BlockSpec((width, 3 * width), lambda i: (0, 0)),
        ],
        out_specs=(
            pl.BlockSpec((SPAN, width), lambda i: (i, 0)),
            pl.BlockSpec((SPAN, 2 * width), lambda i: (i, 0)),
        ),
        compiler_params=vmem,
    )(nodes, gain, w_qkv)

    keys = rows + len(halo) * border_count
    in_vmem = pl.BlockSpec(memory_space=pltpu.VMEM)
    node_state, answers = pl.pallas_call(
        functools.partial(attend, pieces=len(halo)),
        out_shape=(
            shape((rows, width), BF16),
            shape((bricks * capacity, w_target.shape[1]), BF16),
        ),
        in_specs=[pl.BlockSpec(memory_space=pltpu.SMEM)] + [in_vmem] * (9 + len(halo)),
        out_specs=(in_vmem, in_vmem),
        scratch_shapes=[pltpu.VMEM((HEADS, keys, PAIR), BF16)],
        compiler_params=vmem,
    )(valid, nodes, q, kv, *halo, block_mask, gain, w_qkv, w_attn_out, w_target, asked)

    hidden = w_target.shape[1]
    answers = lax.all_to_all(
        answers.reshape(bricks, capacity, hidden),
        ("gy", "gz"),
        split_axis=0,
        concat_axis=0,
        tiled=True,
    ).reshape(bricks * capacity, hidden)
    part = pl.pallas_call(
        own_part, out_shape=shape((edges, hidden), F32), compiler_params=vmem
    )(edge_source.reshape(edges // 128, 128), node_state, w_source, contact, w_contact)
    scores = pl.pallas_call(score, out_shape=shape((1, edges), F32), compiler_params=vmem)(
        place, answers, part, w_score.reshape(1, hidden)
    )
    return (node_state, scores.reshape(edges))


def solution(mesh):
    split = ("groups", "gy", "gz")
    in_specs = (
        P(split, None),
        P(split, None),
        P(split),
        P(split, None),
        P(split),
        P(split),
        P(split, None),
        P(),
        P(),
        P(),
        P(),
        P(),
        P(),
        P(),
    )
    out_specs = (P(split, None), P(split))
    return jax.shard_map(local, mesh=mesh, in_specs=in_specs, out_specs=out_specs, check_vma=False)
```

time: 112 us -> 118 us (1.054)
  waiting for transfers between devices: 21.6 us -> 52.2 us
  blocking collectives: 17.9 us -> 0 us
  between operations: 0.69 us -> 14.1 us
  Pallas kernels: 47 us -> 37.1 us
  local copies, waits for them, and re-layouts: 11 us -> 3.22 us
  starting transfers between devices: 12.5 us -> 10.1 us
    all_gather x0 -> x1, waiting for transfers between devices: none -> 31 us  [local(): requests = lax.all_gather(request, ('gy', 'gz'))]
    all_gather x1 -> x0, blocking collectives: 17.9 us -> none  [local(): requests = lax.all_gather(request, ('gy', 'gz'))]
    pallas_call x4 -> x3, Pallas kernels: 40.3 us -> 30 us  [the longest x1 22 us: local(): pl.pallas_call(functools.partial(attend, pieces=len(halo)), out_shape=(sh...]
    slice x3 -> x0, local copies, waits for them, and re-layouts: 7.7 us -> none  [the longest x1 3.11 us: local(): qkv[:, width:]]
    all_to_all x1, starting transfers between devices: 6.54 us -> 4.86 us  [local(): lax.all_to_all(answers.reshape(bricks, capacity, hidden), ('gy', 'gz'), s...]
  transfers between devices with their start and end apart: 4 -> 5, of which waited for: 1 -> 2; matrix products, arithmetic and copies ran while one was open for 8% -> 2% of each run, Pallas kernels for 8% -> 8%
where the time goes in v2:
time: 118 us; the launch traced here: 117 us
  waiting for transfers between devices  52.2 us (44%)
  Pallas kernels  37.1 us (31%)
  between operations  14.1 us (12%)
  starting transfers between devices  10.1 us (9%)
  local copies, waits for them, and re-layouts  3.22 us (3%)
    all_gather x1, waiting for transfers between devices, local(): requests = lax.all_gather(request, ('gy', 'gz'))  31 us
    pallas_call x1, Pallas kernels, local(): pl.pallas_call(functools.partial(attend, pieces=len(halo)), out_shape=(sh...  22 us
    all_to_all x1, waiting for transfers between devices, local(): lax.all_to_all(answers.reshape(bricks, capacity, hidden), ('gy', 'gz'), s...  21.1 us
    pallas_call x1, Pallas kernels, local(): pl.pallas_call(project, out_shape=(shape((rows, width), BF16), shape((row...  5.43 us
    ppermute x3, starting transfers between devices, neighbours(): pieces.append(lax.ppermute(block, axis, swaps))  5.18 us
    all_to_all x1, starting transfers between devices, local(): lax.all_to_all(answers.reshape(bricks, capacity, hidden), ('gy', 'gz'), s...  4.86 us
    pallas_call x1, Pallas kernels, local(): pl.pallas_call(own_part, out_shape=shape((edges, hidden), F32), compiler_...  3.74 us
    pallas_call x1, Pallas kernels, local(): pl.pallas_call(score, out_shape=shape((1, edges), F32), compiler_params=v...  3.38 us
  transfers between devices with their start and end apart: 5, of which 2 were waited for; matrix products, arithmetic and copies ran while one was open for 2% of the time, Pallas kernels for 8%

profile of v2, /device:TPU:9, one launch (start us, length us, event | category | flops | bytes accessed | tf_op | source)
XLA Modules:
  0.0 117.3 jit_solution(10145749237304695845)
XLA Ops:
  7.2 0.0 all-gather.3.cloned.1.call-start
  7.2 2.6 %shard_map.150 = (bf16[128,512]{1,0:T(8,128)(2,1)}, s32[256,128]{1,0:T(8,128)}, s32[4,128]{1,0:T(4,128)}) custom-call(s32[1,128]{1,0:T(1,128)} %bitcast.25, s32[1,512]{1,0:T(1,128)} %bitcast.20, s32[1,512]{1,0:T(1,128)} %bitcast.21, bf16[1024,512]{1,0:T(8,128)(2,1)} %refs_1_.1), custom_call_target="tpu_custom_call" | custom-call | tf_op jit(solution)/shard_map/pallas_call | solution.py:214
  9.8 0.0 all-gather.3.cloned.1.call-update
  9.8 0.7 collective-permute-start.2
  10.5 3.0 %collective-permute-start.1 = (bf16[128,512]{1,0:T(8,128)(2,1)}, bf16[128,512]{1,0:T(8,128)(2,1)S(1)}, u32[]{:S(2)}, u32[]{:S(2)}) collective-permute-start(bf16[128,512]{1,0:T(8,128)(2,1)} %get-tuple-element.11), channel_id=1, source_target_pairs={{2,4},{4,2},{6,8},{8,6},{10,12},{12,10},{3,5},{5,3},{7,9},{9,7},{1... | collective-permute-start | bytes 393224 | tf_op jit(solution)/shard_map/ppermute | solution.py:185
  13.6 1.4 %collective-permute-start = (bf16[128,512]{1,0:T(8,128)(2,1)}, bf16[128,512]{1,0:T(8,128)(2,1)S(1)}, u32[]{:S(2)}, u32[]{:S(2)}) collective-permute-start(bf16[128,512]{1,0:T(8,128)(2,1)} %get-tuple-element.11), channel_id=1, source_target_pairs={{0,2},{2,0},{4,6},{6,4},{8,10},{10,8},{12,14},{14,12},{1,3},{3,1},... | collective-permute-start | bytes 393224 | tf_op jit(solution)/shard_map/ppermute | solution.py:185
  15.0 0.7 add_convert_fusion.refs_0_
  15.7 5.4 %shard_map.149 = (bf16[1024,512]{1,0:T(8,128)(2,1)}, bf16[1024,1024]{1,0:T(8,128)(2,1)}) custom-call(bf16[1024,512]{1,0:T(8,128)(2,1)} %refs_1_.1, f32[1,512]{1,0:T(1,128)} %bitcast.18, bf16[512,1536]{1,0:T(8,128)(2,1)} %refs_9_.1), custom_call_target="tpu_custom_call" | custom-call | tf_op jit(solution)/shard_map/pallas_call | solution.py:235
  21.1 31.0 %all-gather.3.cloned.1.call-done = s32[4096,128]{1,0:T(8,128)} async-done(((s32[256,128]{1,0:T(8,128)}), s32[4096,128]{1,0:T(8,128)}) %all-gather.3.cloned.1.call-update) | async-done | bytes 2097168 | tf_op jit(solution)/shard_map/all_gather | solution.py:229
  52.1 0.8 constant_dynamic-slice_fusion
  53.0 0.7 reshape.38.refs_12_
  53.6 0.0 collective-permute-done.2.refs_6_
  53.6 0.0 copy-start.1
  53.7 0.0 collective-permute-done.1.refs_5_
  53.7 0.0 copy-start.2
  53.7 0.0 collective-permute-done.refs_4_
  53.7 0.0 copy-start.3
  53.7 0.6 copy-done.1
  54.3 0.1 copy-done.2
  54.4 0.0 copy-done.3
  54.4 22.0 %shard_map.151 = (bf16[1024,512]{1,0:T(8,128)(2,1)}, bf16[1024,512]{1,0:T(8,128)(2,1)}) custom-call(s32[3]{0:T(128)} %add_convert_fusion.refs_0_, bf16[1024,512]{1,0:T(8,128)(2,1)} %refs_1_.1, bf16[1024,512]{1,0:T(8,128)(2,1)} %get-tuple-element.9.refs_2_, bf16[1024,1024]{1,0:T(8,128)(2,1)} %get-tuple-element.10.refs_3_, bf16[128,512]{1,0:T(8,128)(2,1)} %copy-done.3, ...), custom_call_target="tpu_custom_call" | custom-call | tf_op jit(solution)/shard_map/pallas_call | solution.py:253
  76.4 4.9 %all-to-all-start = ((bf16[16,64,512]{2,1,0:T(8,128)(2,1)}), bf16[16,64,512]{2,1,0:T(8,128)(2,1)S(1)}, u32[]{:S(2)}, u32[]{:S(2)}) async-start(bf16[16,64,512]{2,1,0:T(8,128)(2,1)} %bitcast.16), calls=%async_computation | async-start | bytes 2097152 | tf_op jit(solution)/shard_map/all_to_all | solution.py:266
  81.2 3.7 %shard_map.152.part_ref = f32[512,512]{1,0:T(8,128)} custom-call(s32[4,128]{1,0:T(4,128)} %bitcast.22, bf16[1024,512]{1,0:T(8,128)(2,1)} %get-tuple-element.7.state_ref, bf16[512,512]{1,0:T(8,128)(2,1)} %w_source_ref.1, bf16[512,128]{1,0:T(8,128)(2,1)} %contact_ref.1, bf16[128,512]{1,0:T(8,128)(2,1)} %w_ref.3), custom_call_target="tpu_custom_call" | custom-call | tf_op jit(solution)/shard_map/pallas_call | solution.py:273
  85.0 21.1 %all-to-all-done = bf16[16,64,512]{2,1,0:T(8,128)(2,1)S(1)} async-done(((bf16[16,64,512]{2,1,0:T(8,128)(2,1)}), bf16[16,64,512]{2,1,0:T(8,128)(2,1)S(1)}, u32[]{:S(2)}, u32[]{:S(2)}) %all-to-all-start) | async-done | bytes 1048608 | tf_op jit(solution)/shard_map/all_to_all | solution.py:266
  106.1 0.0 copy-start
  106.1 1.0 copy-done
  107.1 3.4 %shard_map.153 = f32[1,512]{1,0:T(1,128)} custom-call(s32[4,128]{1,0:T(4,128)} %get-tuple-element.14.place_ref, bf16[1024,512]{1,0:T(8,128)(2,1)} %bitcast.15, f32[512,512]{1,0:T(8,128)} %shard_map.152.part_ref, f32[1,512]{1,0:T(1,128)} %bitcast.23), custom_call_target="tpu_custom_call" | custom-call | tf_op jit(solution)/shard_map/pallas_call | solution.py:276
Async XLA Ops:
  7.2 45.0 %all-gather.3.cloned.1.call-start = ((), (), s32[]{:S(2)}) async-start(), calls=%async_computation.1 | async-start | bytes 2228224 | tf_op jit(solution)/shard_map/all_gather | solution.py:229
  9.8 43.8 %collective-permute-start.2 = (bf16[128,512]{1,0:T(8,128)(2,1)}, bf16[128,512]{1,0:T(8,128)(2,1)S(1)}, u32[]{:S(2)}, u32[]{:S(2)}) collective-permute-start(bf16[128,512]{1,0:T(8,128)(2,1)} %get-tuple-element.11), channel_id=1, source_target_pairs={{0,1},{1,0},{2,3},{3,2},{4,5},{5,4},{6,7},{7,6},{8,9},{9,8},{10,11... | collective-permute-start | bytes 393224 | tf_op jit(solution)/shard_map/ppermute | solution.py:185
  10.5 43.1 %collective-permute-start.1 = (bf16[128,512]{1,0:T(8,128)(2,1)}, bf16[128,512]{1,0:T(8,128)(2,1)S(1)}, u32[]{:S(2)}, u32[]{:S(2)}) collective-permute-start(bf16[128,512]{1,0:T(8,128)(2,1)} %get-tuple-element.11), channel_id=1, source_target_pairs={{2,4},{4,2},{6,8},{8,6},{10,12},{12,10},{3,5},{5,3},{7,9},{9,7},{1... | collective-permute-start | bytes 393224 | tf_op jit(solution)/shard_map/ppermute | solution.py:185
  13.6 40.1 %collective-permute-start = (bf16[128,512]{1,0:T(8,128)(2,1)}, bf16[128,512]{1,0:T(8,128)(2,1)S(1)}, u32[]{:S(2)}, u32[]{:S(2)}) collective-permute-start(bf16[128,512]{1,0:T(8,128)(2,1)} %get-tuple-element.11), channel_id=1, source_target_pairs={{0,2},{2,0},{4,6},{6,4},{8,10},{10,8},{12,14},{14,12},{1,3},{3,1},... | collective-permute-start | bytes 393224 | tf_op jit(solution)/shard_map/ppermute | solution.py:185
  53.6 0.6 copy-start.1
  53.7 0.7 copy-start.2
  53.7 0.7 copy-start.3
  76.4 29.7 %all-to-all-start = ((bf16[16,64,512]{2,1,0:T(8,128)(2,1)}), bf16[16,64,512]{2,1,0:T(8,128)(2,1)S(1)}, u32[]{:S(2)}, u32[]{:S(2)}) async-start(bf16[16,64,512]{2,1,0:T(8,128)(2,1)} %bitcast.16), calls=%async_computation | async-start | bytes 2097152 | tf_op jit(solution)/shard_map/all_to_all | solution.py:266
  106.1 1.0 copy-start
Sparse Core Ops, SparseCore 0:
  10.2 41.9 all-gather.2

commit v3 on v2

--- a/solution.py
+++ b/solution.py
@@ -57,7 +57,9 @@
 def prepare(ids_ref, owner_ref, target_ref, nodes_ref, border_ref, request_ref, place_ref, *, dims):
     bricks, capacity = dims
     edges = owner_ref.shape[1]
-    border_ref[...] = picked(ids_ref[...], nodes_ref[...]).astype(BF16)
+    border = ids_ref.shape[0] * 128
+    border_ref[:border, :] = picked(ids_ref[...], nodes_ref[...]).astype(BF16)
+    border_ref[border:, :] = jnp.ones_like(border_ref[border:, :])
     owner = owner_ref[...]
     target = target_ref[...]
     mine = iota((bricks, edges), 0) == owner
@@ -72,9 +74,7 @@
     high = (mine_f * (target >> 5).astype(F32)).astype(BF16)
     low = (mine_f * (target & 31).astype(F32)).astype(BF16)
     request = dot_nt(high, at_slot) * 32.0 + dot_nt(low, at_slot)
-    request_ref[:bricks, :] = request.astype(jnp.int32)
-    if request_ref.shape[0] > bricks:
-        request_ref[bricks:, :] = jnp.zeros_like(request_ref[bricks:, :])
+    request_ref[...] = request.astype(jnp.int32)
 
 
 def project(nodes_ref, gain_ref, w_ref, q_ref, kv_ref):
@@ -86,8 +86,8 @@
 
 
 def attend(*refs, pieces):
-    valid_ref, nodes_ref, q_ref, kv_ref = refs[:4]
-    halo_refs = refs[4 : 4 + pieces]
+    nodes_ref, q_ref, kv_ref = refs[:3]
+    halo_refs = refs[3 : 3 + pieces]
     (
         mask_ref,
         gain_ref,
@@ -98,12 +98,12 @@
         state_ref,
         answer_ref,
         v_ref,
-    ) = refs[4 + pieces :]
+    ) = refs[3 + pieces :]
     rows, width = q_ref.shape
     blocks = rows // BLOCK
     keys = v_ref.shape[1]
-    border = halo_refs[0].shape[0]
-    halo_nodes = jnp.concatenate([ref[...] for ref in halo_refs], 0)
+    border = (keys - rows) // pieces
+    halo_nodes = jnp.concatenate([ref[:border, :] for ref in halo_refs], 0)
     halo = dot(normed_rows(halo_nodes, gain_ref[...]), w_qkv_ref[:, width:]).astype(BF16)
     low_keys = iota((keys, PAIR), 1) < HEAD_DIM
     low = iota((rows, PAIR), 1) < HEAD_DIM
@@ -113,7 +113,8 @@
     seen = dot(mask_ref[...].astype(F32).astype(BF16), ones_where(row == lane))
     seen = jnp.where(row == lane, 1.0, seen)
     for h in range(pieces):
-        seen = jnp.where(lane == blocks + h, valid_ref[h].astype(F32), seen)
+        sent = halo_refs[h][border : border + 1, :128].astype(F32)
+        seen = jnp.where(lane == blocks + h, sent, seen)
     bias = jnp.where(seen > 0.5, 0.0, -1e30).astype(BF16)
     bias = jnp.concatenate(
         [jnp.broadcast_to(bias[b : b + 1, :], (BLOCK, 128)) for b in range(blocks)], 0
@@ -151,7 +152,12 @@
     state = state.astype(BF16)
     state_ref[...] = state
     table = dot(state, w_target_ref[...]).astype(BF16)
-    answer_ref[...] = picked(request_ref[...], table).astype(BF16)
+    bricks = request_ref.shape[0]
+    capacity = answer_ref.shape[0] // bricks
+    columns = jnp.transpose(request_ref[...])
+    lanes = iota((capacity, rows), 1)
+    hot = [ones_where(columns[:capacity, b : b + 1] == lanes) for b in range(bricks)]
+    answer_ref[...] = dot(jnp.concatenate(hot, 0), table).astype(BF16)
 
 
 def own_part(index_ref, state_ref, w_source_ref, contact_ref, w_ref, out_ref):
@@ -174,18 +180,15 @@
 
 
 def neighbours(block):
-    pieces, valid = [], []
+    pieces = []
     for axis in ("gy", "gz"):
         count = lax.axis_size(axis)
-        index = lax.axis_index(axis)
         for first in range(min(2, count - 1)):
             swaps = []
             for i in range(first, count - 1, 2):
                 swaps += [(i, i + 1), (i + 1, i)]
             pieces.append(lax.ppermute(block, axis, swaps))
-            beside = jnp.where((index - first) % 2 == 0, index + 1, index - 1)
-            valid.append((beside >= 0) & (beside < count))
-    return pieces, jnp.stack(valid).astype(jnp.int32)
+    return pieces
 
 
 def local(
@@ -214,8 +217,8 @@
     border, request, place = pl.pallas_call(
         functools.partial(prepare, dims=(bricks, capacity)),
         out_shape=(
-            shape((border_count, width), BF16),
-            shape((max(256, bricks), 128), jnp.int32),
+            shape((border_count + 16, width), BF16),
+            shape((bricks, 128), jnp.int32),
             shape((edges // 128, 128), jnp.int32),
         ),
         compiler_params=vmem,
@@ -225,11 +228,8 @@
         edge_target.reshape(1, edges),
         nodes,
     )
-    halo, valid = neighbours(border)
-    requests = lax.all_gather(request, ("gy", "gz"))
-    me = lax.axis_index("gy") * lax.axis_size("gz") + lax.axis_index("gz")
-    asked = lax.dynamic_index_in_dim(requests, me, 1, keepdims=False)[:, :capacity]
-    asked = asked.reshape(bricks * capacity // 128, 128)
+    asked = lax.all_to_all(request, ("gy", "gz"), split_axis=0, concat_axis=0, tiled=True)
+    halo = neighbours(border)
 
     gain = norm_gain.reshape(1, width)
     q, kv = pl.pallas_call(
@@ -256,11 +256,11 @@
             shape((rows, width), BF16),
             shape((bricks * capacity, w_target.shape[1]), BF16),
         ),
-        in_specs=[pl.BlockSpec(memory_space=pltpu.SMEM)] + [in_vmem] * (9 + len(halo)),
+        in_specs=[in_vmem] * (9 + len(halo)),
         out_specs=(in_vmem, in_vmem),
         scratch_shapes=[pltpu.VMEM((HEADS, keys, PAIR), BF16)],
         compiler_params=vmem,
-    )(valid, nodes, q, kv, *halo, block_mask, gain, w_qkv, w_attn_out, w_target, asked)
+    )(nodes, q, kv, *halo, block_mask, gain, w_qkv, w_attn_out, w_target, asked)
 
     hidden = w_target.shape[1]
     answers = lax.all_to_all(

time: 118 us -> 77.5 us (0.66)
  waiting for transfers between devices: 52.2 us -> 21.1 us
  between operations: 14.1 us -> 0.7 us
  starting transfers between devices: 10.1 us -> 16.5 us
  local copies, waits for them, and re-layouts: 3.22 us -> 1.73 us
    all_gather x1 -> x0, waiting for transfers between devices: 31 us -> none  [local(): requests = lax.all_gather(request, ('gy', 'gz'))]
    all_to_all x0 -> x1, starting transfers between devices: none -> 5.38 us  [local(): lax.all_to_all(request, ('gy', 'gz'), split_axis=0, concat_axis=0, tiled=...]
  transfers between devices with their start and end apart: 5 -> 5, of which waited for: 2 -> 1; matrix products, arithmetic and copies ran while one was open for 2% -> 0% of each run, Pallas kernels for 8% -> 12%
where the time goes in v3:
time: 77.5 us; the launch traced here: 77.1 us
  Pallas kernels  37 us (48%)
  waiting for transfers between devices  21.1 us (27%)
  starting transfers between devices  16.5 us (21%)
  local copies, waits for them, and re-layouts  1.73 us (2%)
    pallas_call x1, Pallas kernels, local(): pl.pallas_call(functools.partial(attend, pieces=len(halo)), out_shape=(sh...  21.9 us
    all_to_all x1, waiting for transfers between devices, local(): lax.all_to_all(answers.reshape(bricks, capacity, hidden), ('gy', 'gz'), s...  21.1 us
    all_to_all x1, starting transfers between devices, local(): lax.all_to_all(answers.reshape(bricks, capacity, hidden), ('gy', 'gz'), s...  6.02 us
    pallas_call x1, Pallas kernels, local(): pl.pallas_call(project, out_shape=(shape((rows, width), BF16), shape((row...  5.44 us
    all_to_all x1, starting transfers between devices, local(): lax.all_to_all(request, ('gy', 'gz'), split_axis=0, concat_axis=0, tiled=...  5.38 us
    ppermute x3, starting transfers between devices, neighbours(): pieces.append(lax.ppermute(block, axis, swaps))  5.11 us
    pallas_call x1, Pallas kernels, local(): pl.pallas_call(own_part, out_shape=shape((edges, hidden), F32), compiler_...  3.74 us
    pallas_call x1, Pallas kernels, local(): pl.pallas_call(score, out_shape=shape((1, edges), F32), compiler_params=v...  3.38 us
  transfers between devices with their start and end apart: 5, of which 1 were waited for; matrix products, arithmetic and copies ran while one was open for 0% of the time, Pallas kernels for 12%

profile of v3, /device:TPU:9, one launch (start us, length us, event | category | flops | bytes accessed | tf_op | source)
XLA Modules:
  0.0 77.1 jit_solution(13401031751161340876)
XLA Ops:
  0.6 2.5 %shard_map.150 = (bf16[144,512]{1,0:T(8,128)(2,1)}, s32[16,128]{1,0:T(8,128)}, s32[4,128]{1,0:T(4,128)}) custom-call(s32[1,128]{1,0:T(1,128)} %bitcast.24, s32[1,512]{1,0:T(1,128)} %bitcast.19, s32[1,512]{1,0:T(1,128)} %bitcast.20, bf16[1024,512]{1,0:T(8,128)(2,1)} %refs_0_.1), custom_call_target="tpu_custom_call" | custom-call | tf_op jit(solution)/shard_map/pallas_call | solution.py:217
  3.1 0.7 collective-permute-start.2
  3.8 3.0 %collective-permute-start.1 = (bf16[144,512]{1,0:T(8,128)(2,1)}, bf16[144,512]{1,0:T(8,128)(2,1)S(1)}, u32[]{:S(2)}, u32[]{:S(2)}) collective-permute-start(bf16[144,512]{1,0:T(8,128)(2,1)} %get-tuple-element.11), channel_id=1, source_target_pairs={{2,4},{4,2},{6,8},{8,6},{10,12},{12,10},{3,5},{5,3},{7,9},{9,7},{1... | collective-permute-start | bytes 442376 | tf_op jit(solution)/shard_map/ppermute | solution.py:190
  6.8 1.4 %collective-permute-start = (bf16[144,512]{1,0:T(8,128)(2,1)}, bf16[144,512]{1,0:T(8,128)(2,1)S(1)}, u32[]{:S(2)}, u32[]{:S(2)}) collective-permute-start(bf16[144,512]{1,0:T(8,128)(2,1)} %get-tuple-element.11), channel_id=1, source_target_pairs={{0,2},{2,0},{4,6},{6,4},{8,10},{10,8},{12,14},{14,12},{1,3},{3,1},... | collective-permute-start | bytes 442376 | tf_op jit(solution)/shard_map/ppermute | solution.py:190
  8.3 5.4 %all-to-all-start = ((s32[16,1,128]{2,1,0:T(1,128)}), s32[16,1,128]{2,1,0:T(1,128)S(1)}, u32[]{:S(2)}, u32[]{:S(2)}) async-start(s32[16,1,128]{2,1,0:T(1,128)} %bitcast.16), calls=%async_computation | async-start | bytes 16384 | tf_op jit(solution)/shard_map/all_to_all | solution.py:231
  13.6 5.4 %shard_map.149 = (bf16[1024,512]{1,0:T(8,128)(2,1)}, bf16[1024,1024]{1,0:T(8,128)(2,1)}) custom-call(bf16[1024,512]{1,0:T(8,128)(2,1)} %refs_0_.1, f32[1,512]{1,0:T(1,128)} %bitcast.17, bf16[512,1536]{1,0:T(8,128)(2,1)} %refs_8_.1), custom_call_target="tpu_custom_call" | custom-call | tf_op jit(solution)/shard_map/pallas_call | solution.py:235
  19.1 0.0 all-to-all-done
  19.1 0.0 copy-start.4
  19.1 0.0 collective-permute-done.2.refs_5_
  19.1 0.0 copy-start.1
  19.1 0.0 collective-permute-done.1.refs_4_
  19.1 0.0 copy-start.2
  19.1 0.0 collective-permute-done.refs_3_
  19.1 0.0 copy-start.3
  19.2 0.5 copy-done.4
  19.7 0.1 copy-done.1
  19.8 0.0 copy-done.2
  19.8 0.1 copy-done.3
  19.9 21.9 %shard_map.151 = (bf16[1024,512]{1,0:T(8,128)(2,1)}, bf16[1024,512]{1,0:T(8,128)(2,1)}) custom-call(bf16[1024,512]{1,0:T(8,128)(2,1)} %refs_0_.1, bf16[1024,512]{1,0:T(8,128)(2,1)} %get-tuple-element.9.refs_1_, bf16[1024,1024]{1,0:T(8,128)(2,1)} %get-tuple-element.10.refs_2_, bf16[144,512]{1,0:T(8,128)(2,1)} %copy-done.3, bf16[144,512]{1,0:T(8,128)(2,1)} %copy-done.2, ...), custom_call_target="tpu_custom_call" | custom-call | tf_op jit(solution)/shard_map/pallas_call | solution.py:253
  41.8 6.0 %all-to-all-start.1 = ((bf16[16,64,512]{2,1,0:T(8,128)(2,1)}), bf16[16,64,512]{2,1,0:T(8,128)(2,1)S(1)}, u32[]{:S(2)}, u32[]{:S(2)}) async-start(bf16[16,64,512]{2,1,0:T(8,128)(2,1)} %bitcast.14), calls=%async_computation.1 | async-start | bytes 2097152 | tf_op jit(solution)/shard_map/all_to_all | solution.py:266
  47.8 3.7 %shard_map.152.part_ref = f32[512,512]{1,0:T(8,128)} custom-call(s32[4,128]{1,0:T(4,128)} %bitcast.21, bf16[1024,512]{1,0:T(8,128)(2,1)} %get-tuple-element.7.state_ref, bf16[512,512]{1,0:T(8,128)(2,1)} %w_source_ref.1, bf16[512,128]{1,0:T(8,128)(2,1)} %contact_ref.1, bf16[128,512]{1,0:T(8,128)(2,1)} %w_ref.3), custom_call_target="tpu_custom_call" | custom-call | tf_op jit(solution)/shard_map/pallas_call | solution.py:273
  51.6 21.1 %all-to-all-done.1 = bf16[16,64,512]{2,1,0:T(8,128)(2,1)S(1)} async-done(((bf16[16,64,512]{2,1,0:T(8,128)(2,1)}), bf16[16,64,512]{2,1,0:T(8,128)(2,1)S(1)}, u32[]{:S(2)}, u32[]{:S(2)}) %all-to-all-start.1) | async-done | bytes 1048608 | tf_op jit(solution)/shard_map/all_to_all | solution.py:266
  72.7 0.0 copy-start
  72.7 1.0 %copy-done = bf16[16,64,512]{2,1,0:T(8,128)(2,1)} copy-done((bf16[16,64,512]{2,1,0:T(8,128)(2,1)}, bf16[16,64,512]{2,1,0:T(8,128)(2,1)S(1)}, u32[]{:S(2)}) %copy-start) | copy-done | bytes 1048600
  73.7 3.4 %shard_map.153 = f32[1,512]{1,0:T(1,128)} custom-call(s32[4,128]{1,0:T(4,128)} %get-tuple-element.14.place_ref, bf16[1024,512]{1,0:T(8,128)(2,1)} %bitcast.13, f32[512,512]{1,0:T(8,128)} %shard_map.152.part_ref, f32[1,512]{1,0:T(1,128)} %bitcast.22), custom_call_target="tpu_custom_call" | custom-call | tf_op jit(solution)/shard_map/pallas_call | solution.py:276
Async XLA Ops:
  3.1 16.0 %collective-permute-start.2 = (bf16[144,512]{1,0:T(8,128)(2,1)}, bf16[144,512]{1,0:T(8,128)(2,1)S(1)}, u32[]{:S(2)}, u32[]{:S(2)}) collective-permute-start(bf16[144,512]{1,0:T(8,128)(2,1)} %get-tuple-element.11), channel_id=1, source_target_pairs={{0,1},{1,0},{2,3},{3,2},{4,5},{5,4},{6,7},{7,6},{8,9},{9,8},{10,11... | collective-permute-start | bytes 442376 | tf_op jit(solution)/shard_map/ppermute | solution.py:190
  3.8 15.3 %collective-permute-start.1 = (bf16[144,512]{1,0:T(8,128)(2,1)}, bf16[144,512]{1,0:T(8,128)(2,1)S(1)}, u32[]{:S(2)}, u32[]{:S(2)}) collective-permute-start(bf16[144,512]{1,0:T(8,128)(2,1)} %get-tuple-element.11), channel_id=1, source_target_pairs={{2,4},{4,2},{6,8},{8,6},{10,12},{12,10},{3,5},{5,3},{7,9},{9,7},{1... | collective-permute-start | bytes 442376 | tf_op jit(solution)/shard_map/ppermute | solution.py:190
  6.8 12.3 %collective-permute-start = (bf16[144,512]{1,0:T(8,128)(2,1)}, bf16[144,512]{1,0:T(8,128)(2,1)S(1)}, u32[]{:S(2)}, u32[]{:S(2)}) collective-permute-start(bf16[144,512]{1,0:T(8,128)(2,1)} %get-tuple-element.11), channel_id=1, source_target_pairs={{0,2},{2,0},{4,6},{6,4},{8,10},{10,8},{12,14},{14,12},{1,3},{3,1},... | collective-permute-start | bytes 442376 | tf_op jit(solution)/shard_map/ppermute | solution.py:190
  8.3 10.8 %all-to-all-start = ((s32[16,1,128]{2,1,0:T(1,128)}), s32[16,1,128]{2,1,0:T(1,128)S(1)}, u32[]{:S(2)}, u32[]{:S(2)}) async-start(s32[16,1,128]{2,1,0:T(1,128)} %bitcast.16), calls=%async_computation | async-start | bytes 16384 | tf_op jit(solution)/shard_map/all_to_all | solution.py:231
  19.1 0.6 copy-start.4
  19.1 0.7 copy-start.1
  19.1 0.7 copy-start.2
  19.1 0.7 copy-start.3
  41.8 30.9 %all-to-all-start.1 = ((bf16[16,64,512]{2,1,0:T(8,128)(2,1)}), bf16[16,64,512]{2,1,0:T(8,128)(2,1)S(1)}, u32[]{:S(2)}, u32[]{:S(2)}) async-start(bf16[16,64,512]{2,1,0:T(8,128)(2,1)} %bitcast.14), calls=%async_computation.1 | async-start | bytes 2097152 | tf_op jit(solution)/shard_map/all_to_all | solution.py:266
  72.7 1.0 %copy-start = (bf16[16,64,512]{2,1,0:T(8,128)(2,1)}, bf16[16,64,512]{2,1,0:T(8,128)(2,1)S(1)}, u32[]{:S(2)}) copy-start(bf16[16,64,512]{2,1,0:T(8,128)(2,1)S(1)} %all-to-all-done.1) | copy-start | bytes 3145732

commit v4 on v3

--- a/solution.py
+++ b/solution.py
@@ -11,7 +11,6 @@
 HEAD_DIM = 64
 BLOCK = 128
 PAIR = 2 * HEAD_DIM
-SPAN = 256
 F32 = jnp.float32
 BF16 = jnp.bfloat16
 NT = (((1,), (1,)), ((), ()))
@@ -40,12 +39,15 @@
     return jnp.transpose(rows)
 
 
-def picked(index_rows, table):
+def hot_rows(index_rows, size):
     count = index_rows.shape[0]
     columns = columns_of(index_rows)
-    lanes = iota((128, table.shape[0]), 1)
-    hot = [ones_where(columns[:, r : r + 1] == lanes) for r in range(count)]
-    return dot(jnp.concatenate(hot, 0), table)
+    lanes = iota((128, size), 1)
+    return jnp.concatenate([ones_where(columns[:, r : r + 1] == lanes) for r in range(count)], 0)
+
+
+def picked(index_rows, table):
+    return dot(hot_rows(index_rows, table.shape[0]), table)
 
 
 def normed_rows(values, gain):
@@ -77,12 +79,13 @@
     request_ref[...] = request.astype(jnp.int32)
 
 
-def project(nodes_ref, gain_ref, w_ref, q_ref, kv_ref):
+def project(nodes_ref, gain_ref, w_ref, request_ref, q_ref, kv_ref, column_ref):
     width = nodes_ref.shape[1]
     normed = normed_rows(nodes_ref[...], gain_ref[...])
     scale = 1.4426950408889634 / HEAD_DIM**0.5
     q_ref[...] = (dot(normed, w_ref[:, :width]) * scale).astype(BF16)
     kv_ref[...] = dot(normed, w_ref[:, width:]).astype(BF16)
+    column_ref[...] = jnp.transpose(request_ref[...])
 
 
 def attend(*refs, pieces):
@@ -94,7 +97,7 @@
         w_qkv_ref,
         w_out_ref,
         w_target_ref,
-        request_ref,
+        column_ref,
         state_ref,
         answer_ref,
         v_ref,
@@ -152,18 +155,20 @@
     state = state.astype(BF16)
     state_ref[...] = state
     table = dot(state, w_target_ref[...]).astype(BF16)
-    bricks = request_ref.shape[0]
+    bricks = column_ref.shape[1]
     capacity = answer_ref.shape[0] // bricks
-    columns = jnp.transpose(request_ref[...])
+    columns = column_ref[...]
     lanes = iota((capacity, rows), 1)
     hot = [ones_where(columns[:capacity, b : b + 1] == lanes) for b in range(bricks)]
     answer_ref[...] = dot(jnp.concatenate(hot, 0), table).astype(BF16)
 
 
-def own_part(index_ref, state_ref, w_source_ref, contact_ref, w_ref, out_ref):
+def own_part(
+    index_ref, state_ref, w_source_ref, contact_ref, w_ref, part_ref
+):
     rows = picked(index_ref[...], state_ref[...]).astype(BF16)
     rows = dot(rows, w_source_ref[...]).astype(BF16).astype(F32)
-    out_ref[...] = rows + dot(contact_ref[...], w_ref[...])
+    part_ref[...] = rows + dot(contact_ref[...], w_ref[...])
 
 
 def score(place_ref, answers_ref, part_ref, w_ref, out_ref):
@@ -173,6 +178,22 @@
     for at in range(128, weighted.shape[1], 128):
         folded = folded + weighted[:, at : at + 128]
     out_ref[...] = jnp.sum(jnp.transpose(folded), axis=0, keepdims=True)
+
+
+def near(array):
+    return pltpu.with_memory_space_constraint(array, pltpu.VMEM)
+
+
+def run(kernel, outs, *args, scratch=(), mib=16):
+    space = pl.BlockSpec(memory_space=pltpu.VMEM)
+    return pl.pallas_call(
+        kernel,
+        out_shape=tuple(outs),
+        in_specs=[space] * len(args),
+        out_specs=(space,) * len(outs),
+        scratch_shapes=scratch,
+        compiler_params=pltpu.CompilerParams(vmem_limit_bytes=mib * 1024 * 1024),
+    )(*args)
 
 
 def shape(dims, dtype):
@@ -212,57 +233,53 @@
     border_count = border_ids.shape[0]
     bricks = lax.axis_size("gy") * lax.axis_size("gz")
     capacity = max(2 * edges // bricks, 2)
-    vmem = pltpu.CompilerParams(vmem_limit_bytes=60 * 1024 * 1024)
-
-    border, request, place = pl.pallas_call(
+    hidden = w_target.shape[1]
+    nodes_near = near(nodes)
+    border, request, place = run(
         functools.partial(prepare, dims=(bricks, capacity)),
-        out_shape=(
+        (
             shape((border_count + 16, width), BF16),
             shape((bricks, 128), jnp.int32),
             shape((edges // 128, 128), jnp.int32),
         ),
-        compiler_params=vmem,
-    )(
         border_ids.reshape(border_count // 128, 128),
         edge_owner.reshape(1, edges),
         edge_target.reshape(1, edges),
-        nodes,
-    )
+        nodes_near,
+    )
+    halo = neighbours(border)
     asked = lax.all_to_all(request, ("gy", "gz"), split_axis=0, concat_axis=0, tiled=True)
-    halo = neighbours(border)
 
     gain = norm_gain.reshape(1, width)
-    q, kv = pl.pallas_call(
+    w_qkv_near = near(w_qkv)
+    q, kv, columns = run(
         project,
-        out_shape=(shape((rows, width), BF16), shape((rows, 2 * width), BF16)),
-        grid=(rows // SPAN,),
-        in_specs=[
-            pl.BlockSpec((SPAN, width), lambda i: (i, 0)),
-            pl.BlockSpec((1, width), lambda i: (0, 0)),
-            pl.BlockSpec((width, 3 * width), lambda i: (0, 0)),
-        ],
-        out_specs=(
-            pl.BlockSpec((SPAN, width), lambda i: (i, 0)),
-            pl.BlockSpec((SPAN, 2 * width), lambda i: (i, 0)),
+        (
+            pltpu.VMEM((rows, width), BF16),
+            pltpu.VMEM((rows, 2 * width), BF16),
+            pltpu.VMEM((128, bricks), jnp.int32),
         ),
-        compiler_params=vmem,
-    )(nodes, gain, w_qkv)
-
-    keys = rows + len(halo) * border_count
-    in_vmem = pl.BlockSpec(memory_space=pltpu.VMEM)
-    node_state, answers = pl.pallas_call(
+        nodes_near,
+        gain,
+        w_qkv_near,
+        near(asked),
+    )
+    node_state, answers = run(
         functools.partial(attend, pieces=len(halo)),
-        out_shape=(
-            shape((rows, width), BF16),
-            shape((bricks * capacity, w_target.shape[1]), BF16),
-        ),
-        in_specs=[in_vmem] * (9 + len(halo)),
-        out_specs=(in_vmem, in_vmem),
-        scratch_shapes=[pltpu.VMEM((HEADS, keys, PAIR), BF16)],
-        compiler_params=vmem,
-    )(nodes, q, kv, *halo, block_mask, gain, w_qkv, w_attn_out, w_target, asked)
-
-    hidden = w_target.shape[1]
+        (shape((rows, width), BF16), shape((bricks * capacity, hidden), BF16)),
+        nodes_near,
+        q,
+        kv,
+        *[near(piece) for piece in halo],
+        block_mask,
+        gain,
+        w_qkv_near,
+        near(w_attn_out),
+        near(w_target),
+        columns,
+        mib=32,
+        scratch=[pltpu.VMEM((HEADS, rows + len(halo) * border_count, PAIR), BF16)],
+    )
     answers = lax.all_to_all(
         answers.reshape(bricks, capacity, hidden),
         ("gy", "gz"),
@@ -270,11 +287,17 @@
         concat_axis=0,
         tiled=True,
     ).reshape(bricks * capacity, hidden)
-    part = pl.pallas_call(
-        own_part, out_shape=shape((edges, hidden), F32), compiler_params=vmem
-    )(edge_source.reshape(edges // 128, 128), node_state, w_source, contact, w_contact)
-    scores = pl.pallas_call(score, out_shape=shape((1, edges), F32), compiler_params=vmem)(
-        place, answers, part, w_score.reshape(1, hidden)
+    (part,) = run(
+        own_part,
+        (shape((edges, hidden), F32),),
+        edge_source.reshape(edges // 128, 128),
+        node_state,
+        w_source,
+        contact,
+        w_contact,
+    )
+    (scores,) = run(
+        score, (shape((1, edges), F32),), place, near(answers), part, w_score.reshape(1, hidden)
     )
     return (node_state, scores.reshape(edges))
 

time: 77.5 us -> 76.6 us (0.988)
  Pallas kernels: 37 us -> 24.8 us
  blocking collectives: 0 us -> 9.85 us
  local copies, waits for them, and re-layouts: 1.73 us -> 7.64 us
  starting transfers between devices: 16.5 us -> 10.6 us
  waiting for transfers between devices: 21.1 us -> 22.5 us
    pallas_call x5, Pallas kernels: 37 us -> 24.8 us  [run(): pl.pallas_call(kernel, out_shape=tuple(outs), in_specs=[space] * len(args...]
    all_to_all x0 -> x1, blocking collectives: none -> 9.85 us  [local(): lax.all_to_all(request, ('gy', 'gz'), split_axis=0, concat_axis=0, tiled=...]
    unnamed x10 -> x38, local copies, waits for them, and re-layouts: 1.73 us -> 7.64 us
    all_to_all x1 -> x0, starting transfers between devices: 5.38 us -> none  [local(): lax.all_to_all(request, ('gy', 'gz'), split_axis=0, concat_axis=0, tiled=...]
    all_to_all x1, waiting for transfers between devices: 21.1 us -> 22.5 us  [local(): lax.all_to_all(answers.reshape(bricks, capacity, hidden), ('gy', 'gz'), s...]
  transfers between devices with their start and end apart: 5 -> 4, of which waited for: 1 -> 1; matrix products, arithmetic and copies ran while one was open for 0% -> 0% of each run, Pallas kernels for 12% -> 4%
where the time goes in v4:
time: 76.6 us; the launch traced here: 76.1 us
  Pallas kernels  24.8 us (32%)
  waiting for transfers between devices  22.5 us (29%)
  starting transfers between devices  10.6 us (14%)
  blocking collectives  9.85 us (13%)
  local copies, waits for them, and re-layouts  7.64 us (10%)
  between operations  0.8 us (1%)
    pallas_call x5, Pallas kernels, run(): pl.pallas_call(kernel, out_shape=tuple(outs), in_specs=[space] * len(args...  24.8 us
    all_to_all x1, waiting for transfers between devices, local(): lax.all_to_all(answers.reshape(bricks, capacity, hidden), ('gy', 'gz'), s...  22.5 us
    all_to_all x1, blocking collectives, local(): lax.all_to_all(request, ('gy', 'gz'), split_axis=0, concat_axis=0, tiled=...  9.85 us
    unnamed x38, local copies, waits for them, and re-layouts  7.64 us
    all_to_all x1, starting transfers between devices, local(): lax.all_to_all(answers.reshape(bricks, capacity, hidden), ('gy', 'gz'), s...  5.41 us
    ppermute x3, starting transfers between devices, neighbours(): pieces.append(lax.ppermute(block, axis, swaps))  5.18 us
  transfers between devices with their start and end apart: 4, of which 1 were waited for; matrix products, arithmetic and copies ran while one was open for 0% of the time, Pallas kernels for 4%

profile of v4, /device:TPU:9, one launch (start us, length us, event | category | flops | bytes accessed | tf_op | source)
XLA Modules:
  0.0 76.1 jit_solution(13562905726865362998)
XLA Ops:
  0.6 0.0 copy-start.12
  0.6 0.0 copy-start
  0.7 1.2 %copy-done = bf16[1024,512]{1,0:T(8,128)(2,1)S(1)} copy-done((bf16[1024,512]{1,0:T(8,128)(2,1)S(1)}, bf16[1024,512]{1,0:T(8,128)(2,1)}, u32[]{:S(2)}) %copy-start) | copy-done | bytes 1048600
  1.9 0.7 copy-done.14
  2.6 0.7 copy-done.15
  3.2 0.7 copy-done.18
  3.9 0.6 shard_map.149
  4.5 0.7 collective-permute-start.2
  5.2 3.0 %collective-permute-start.1 = (bf16[144,512]{1,0:T(8,128)(2,1)S(1)}, bf16[144,512]{1,0:T(8,128)(2,1)S(1)}, u32[]{:S(2)}, u32[]{:S(2)}) collective-permute-start(bf16[144,512]{1,0:T(8,128)(2,1)S(1)} %get-tuple-element.13), channel_id=1, source_target_pairs={{2,4},{4,2},{6,8},{8,6},{10,12},{12,10},{3,5},{5,3},{7,9},{9,7},{1... | collective-permute-start | bytes 442376 | tf_op jit(solution)/shard_map/ppermute | solution.py:211
  8.2 1.4 %collective-permute-start = (bf16[144,512]{1,0:T(8,128)(2,1)S(1)}, bf16[144,512]{1,0:T(8,128)(2,1)S(1)}, u32[]{:S(2)}, u32[]{:S(2)}) collective-permute-start(bf16[144,512]{1,0:T(8,128)(2,1)S(1)} %get-tuple-element.13), channel_id=1, source_target_pairs={{0,2},{2,0},{4,6},{6,4},{8,10},{10,8},{12,14},{14,12},{1,3},{3,1},... | collective-permute-start | bytes 442376 | tf_op jit(solution)/shard_map/ppermute | solution.py:211
  9.7 9.8 %all_to_all.16 = s32[16,1,128]{2,1,0:T(1,128)S(1)} all-to-all(s32[16,1,128]{2,1,0:T(1,128)S(1)} %bitcast.15), channel_id=1, replica_groups=mesh['groups'=2,'gy'=8,'gz'=2] {'gy','gz'}, dimensions={0} | all-to-all | bytes 16384 | tf_op jit(solution)/shard_map/all_to_all | solution.py:251
  19.5 1.2 %copy-done.1 = bf16[1024,512]{1,0:T(8,128)(2,1)S(1)} copy-done((bf16[1024,512]{1,0:T(8,128)(2,1)S(1)}, bf16[1024,512]{1,0:T(8,128)(2,1)}, u32[]{:S(2)}) %copy-start.1) | copy-done | bytes 1048600
  20.7 1.4 %copy-done.3 = bf16[512,1536]{1,0:T(8,128)(2,1)S(1)} copy-done((bf16[512,1536]{1,0:T(8,128)(2,1)S(1)}, bf16[512,1536]{1,0:T(8,128)(2,1)}, u32[]{:S(2)}) %copy-start.3) | copy-done | bytes 1572888
  22.1 0.7 copy-done.11
  22.8 1.9 %shard_map.150 = (bf16[1024,512]{1,0:T(8,128)(2,1)S(1)}, bf16[1024,1024]{1,0:T(8,128)(2,1)S(1)}, s32[128,16]{1,0:T(8,128)S(1)}) custom-call(bf16[1024,512]{1,0:T(8,128)(2,1)S(1)} %copy-done.1, f32[1,512]{1,0:T(1,128)S(1)} %bitcast.16, bf16[512,1536]{1,0:T(8,128)(2,1)S(1)} %copy-done.3, s32[16,128]{1,0:T(8,128)S(1)} %bitcast.14), custom_call_target="tpu_custom_call" | custom-call | tf_op jit(solution)/shard_map/pallas_call | solution.py:189
  24.7 0.0 collective-permute-done.2.refs_5_
  24.7 0.0 collective-permute-done.1.refs_4_
  24.8 0.0 collective-permute-done.refs_3_
  24.8 0.0 copy-done.12
  24.8 19.1 %shard_map.151 = (bf16[1024,512]{1,0:T(8,128)(2,1)}, bf16[1024,512]{1,0:T(8,128)(2,1)}) custom-call(bf16[1024,512]{1,0:T(8,128)(2,1)S(1)} %copy-done.2, bf16[1024,512]{1,0:T(8,128)(2,1)S(1)} %get-tuple-element.11.refs_1_, bf16[1024,1024]{1,0:T(8,128)(2,1)S(1)} %get-tuple-element.12.refs_2_, bf16[144,512]{1,0:T(8,128)(2,1)S(1)} %collective-permute-done.refs_3_, ...), custom_call_target="tpu_custom_call" | custom-call | tf_op jit(solution)/shard_map/pallas_call | solution.py:189
  43.9 0.0 copy-start.17
  44.0 5.4 %all-to-all-start.1 = ((bf16[16,64,512]{2,1,0:T(8,128)(2,1)}), bf16[16,64,512]{2,1,0:T(8,128)(2,1)S(1)}, u32[]{:S(2)}, u32[]{:S(2)}) async-start(bf16[16,64,512]{2,1,0:T(8,128)(2,1)} %bitcast.7), calls=%async_computation.1 | async-start | bytes 2097152 | tf_op jit(solution)/shard_map/all_to_all | solution.py:283
  49.4 0.0 copy-done.5
  49.4 0.0 copy-done.9
  49.4 0.0 copy-done.10
  49.4 0.0 copy-done.16
  49.4 0.0 copy-start.6
  49.4 1.0 %copy-done.6 = bf16[512,512]{1,0:T(8,128)(2,1)S(1)} copy-done((bf16[512,512]{1,0:T(8,128)(2,1)S(1)}, bf16[512,512]{1,0:T(8,128)(2,1)}, u32[]{:S(2)}) %copy-start.6) | copy-done | bytes 524312
  50.5 1.3 %shard_map.152.part_ref = f32[512,512]{1,0:T(8,128)S(1)} custom-call(s32[4,128]{1,0:T(4,128)S(1)} %bitcast.20, bf16[1024,512]{1,0:T(8,128)(2,1)S(1)} %copy-done.5, bf16[512,512]{1,0:T(8,128)(2,1)S(1)} %copy-done.6, bf16[512,128]{1,0:T(8,128)(2,1)S(1)} %copy-done.9, bf16[128,512]{1,0:T(8,128)(2,1)S(1)} %copy-done.10), custom_call_target="tpu_custom_call" | custom-call | tf_op jit(solution)/shard_map/pallas_call | solution.py:189
  51.8 22.5 %all-to-all-done.1 = bf16[16,64,512]{2,1,0:T(8,128)(2,1)S(1)} async-done(((bf16[16,64,512]{2,1,0:T(8,128)(2,1)}), bf16[16,64,512]{2,1,0:T(8,128)(2,1)S(1)}, u32[]{:S(2)}, u32[]{:S(2)}) %all-to-all-start.1) | async-done | bytes 1048608 | tf_op jit(solution)/shard_map/all_to_all | solution.py:283
  74.2 0.0 copy-done.17
  74.2 1.8 %shard_map.153 = f32[1,512]{1,0:T(1,128)} custom-call(s32[4,128]{1,0:T(4,128)S(1)} %get-tuple-element.16.place_ref, bf16[1024,512]{1,0:T(8,128)(2,1)S(1)} %bitcast.13, f32[512,512]{1,0:T(8,128)S(1)} %shard_map.152.part_ref, f32[1,512]{1,0:T(1,128)S(1)} %bitcast.21), custom_call_target="tpu_custom_call" | custom-call | tf_op jit(solution)/shard_map/pallas_call | solution.py:189
  (20 shorter events, 0.0 us)
Async XLA Ops:
  0.6 24.1 %copy-start.12 = (f32[512]{0:T(512)S(1)}, f32[512]{0:T(512)}, u32[]{:S(2)}) copy-start(f32[512]{0:T(512)} %param.21) | copy-start | bytes 6148
  0.6 1.2 %copy-start = (bf16[1024,512]{1,0:T(8,128)(2,1)S(1)}, bf16[1024,512]{1,0:T(8,128)(2,1)}, u32[]{:S(2)}) copy-start(bf16[1024,512]{1,0:T(8,128)(2,1)} %refs_0_.1) | copy-start | bytes 3145732
  1.9 0.7 copy-start.14
  2.6 0.7 copy-start.15
  3.2 0.7 copy-start.18
  3.9 20.9 %copy-start.2 = (bf16[1024,512]{1,0:T(8,128)(2,1)S(1)}, bf16[1024,512]{1,0:T(8,128)(2,1)}, u32[]{:S(2)}) copy-start(bf16[1024,512]{1,0:T(8,128)(2,1)} %refs_0_.1) | copy-start | bytes 3145732
  3.9 20.9 %copy-start.13 = (s32[8,8]{1,0:T(8,128)S(1)}, s32[8,8]{1,0:T(8,128)}, u32[]{:S(2)}) copy-start(s32[8,8]{1,0:T(8,128)} %refs_6_.1) | copy-start | bytes 772
  4.5 20.3 %collective-permute-start.2 = (bf16[144,512]{1,0:T(8,128)(2,1)S(1)}, bf16[144,512]{1,0:T(8,128)(2,1)S(1)}, u32[]{:S(2)}, u32[]{:S(2)}) collective-permute-start(bf16[144,512]{1,0:T(8,128)(2,1)S(1)} %get-tuple-element.13), channel_id=1, source_target_pairs={{0,1},{1,0},{2,3},{3,2},{4,5},{5,4},{6,7},{7,6},{8,9},{9,8},{10,11... | collective-permute-start | bytes 442376 | tf_op jit(solution)/shard_map/ppermute | solution.py:211
  5.2 19.5 %collective-permute-start.1 = (bf16[144,512]{1,0:T(8,128)(2,1)S(1)}, bf16[144,512]{1,0:T(8,128)(2,1)S(1)}, u32[]{:S(2)}, u32[]{:S(2)}) collective-permute-start(bf16[144,512]{1,0:T(8,128)(2,1)S(1)} %get-tuple-element.13), channel_id=1, source_target_pairs={{2,4},{4,2},{6,8},{8,6},{10,12},{12,10},{3,5},{5,3},{7,9},{9,7},{1... | collective-permute-start | bytes 442376 | tf_op jit(solution)/shard_map/ppermute | solution.py:211
  8.2 16.5 %collective-permute-start = (bf16[144,512]{1,0:T(8,128)(2,1)S(1)}, bf16[144,512]{1,0:T(8,128)(2,1)S(1)}, u32[]{:S(2)}, u32[]{:S(2)}) collective-permute-start(bf16[144,512]{1,0:T(8,128)(2,1)S(1)} %get-tuple-element.13), channel_id=1, source_target_pairs={{0,2},{2,0},{4,6},{6,4},{8,10},{10,8},{12,14},{14,12},{1,3},{3,1},... | collective-permute-start | bytes 442376 | tf_op jit(solution)/shard_map/ppermute | solution.py:211
  19.5 1.2 %copy-start.1 = (bf16[1024,512]{1,0:T(8,128)(2,1)S(1)}, bf16[1024,512]{1,0:T(8,128)(2,1)}, u32[]{:S(2)}) copy-start(bf16[1024,512]{1,0:T(8,128)(2,1)} %refs_0_.1) | copy-start | bytes 3145732
  20.7 1.4 %copy-start.3 = (bf16[512,1536]{1,0:T(8,128)(2,1)S(1)}, bf16[512,1536]{1,0:T(8,128)(2,1)}, u32[]{:S(2)}) copy-start(bf16[512,1536]{1,0:T(8,128)(2,1)} %refs_8_.1) | copy-start | bytes 4718596
  22.1 0.7 copy-start.11
  22.8 2.0 %copy-start.4 = (bf16[512,1536]{1,0:T(8,128)(2,1)S(1)}, bf16[512,1536]{1,0:T(8,128)(2,1)}, u32[]{:S(2)}) copy-start(bf16[512,1536]{1,0:T(8,128)(2,1)} %refs_8_.1) | copy-start | bytes 4718596
  22.8 2.0 %copy-start.7 = (bf16[512,512]{1,0:T(8,128)(2,1)S(1)}, bf16[512,512]{1,0:T(8,128)(2,1)}, u32[]{:S(2)}) copy-start(bf16[512,512]{1,0:T(8,128)(2,1)} %refs_9_.1) | copy-start | bytes 1572868
  22.8 2.0 %copy-start.8 = (bf16[512,512]{1,0:T(8,128)(2,1)S(1)}, bf16[512,512]{1,0:T(8,128)(2,1)}, u32[]{:S(2)}) copy-start(bf16[512,512]{1,0:T(8,128)(2,1)} %refs_10_.1) | copy-start | bytes 1572868
  43.9 5.4 %copy-start.5 = (bf16[1024,512]{1,0:T(8,128)(2,1)S(1)}, bf16[1024,512]{1,0:T(8,128)(2,1)}, u32[]{:S(2)}) copy-start(bf16[1024,512]{1,0:T(8,128)(2,1)} %get-tuple-element.8.state_ref) | copy-start | bytes 3145732
  43.9 5.4 %copy-start.9 = (bf16[512,128]{1,0:T(8,128)(2,1)S(1)}, bf16[512,128]{1,0:T(8,128)(2,1)}, u32[]{:S(2)}) copy-start(bf16[512,128]{1,0:T(8,128)(2,1)} %contact_ref.1) | copy-start | bytes 393220
  43.9 5.4 %copy-start.10 = (bf16[128,512]{1,0:T(8,128)(2,1)S(1)}, bf16[128,512]{1,0:T(8,128)(2,1)}, u32[]{:S(2)}) copy-start(bf16[128,512]{1,0:T(8,128)(2,1)} %w_ref.3) | copy-start | bytes 393220
  43.9 5.5 %copy-start.16 = (s32[512]{0:T(512)S(1)}, s32[512]{0:T(512)}, u32[]{:S(2)}) copy-start(s32[512]{0:T(512)} %param.18) | copy-start | bytes 6148
  43.9 30.3 %copy-start.17 = (f32[512]{0:T(512)S(1)}, f32[512]{0:T(512)}, u32[]{:S(2)}) copy-start(f32[512]{0:T(512)} %param.27) | copy-start | bytes 6148
  44.0 30.3 %all-to-all-start.1 = ((bf16[16,64,512]{2,1,0:T(8,128)(2,1)}), bf16[16,64,512]{2,1,0:T(8,128)(2,1)S(1)}, u32[]{:S(2)}, u32[]{:S(2)}) async-start(bf16[16,64,512]{2,1,0:T(8,128)(2,1)} %bitcast.7), calls=%async_computation.1 | async-start | bytes 2097152 | tf_op jit(solution)/shard_map/all_to_all | solution.py:283
  49.4 1.0 %copy-start.6 = (bf16[512,512]{1,0:T(8,128)(2,1)S(1)}, bf16[512,512]{1,0:T(8,128)(2,1)}, u32[]{:S(2)}) copy-start(bf16[512,512]{1,0:T(8,128)(2,1)} %w_source_ref.1) | copy-start | bytes 1572868

commit v5 on v4

--- a/solution.py
+++ b/solution.py
@@ -13,6 +13,7 @@
 PAIR = 2 * HEAD_DIM
 F32 = jnp.float32
 BF16 = jnp.bfloat16
+FAR = pltpu.HBM
 NT = (((1,), (1,)), ((), ()))
 
 
@@ -56,12 +57,23 @@
     return (wide * lax.rsqrt(mean + 1e-06) * gain).astype(BF16)
 
 
-def prepare(ids_ref, owner_ref, target_ref, nodes_ref, border_ref, request_ref, place_ref, *, dims):
+def fetch(sources, places, signals):
+    copies = [
+        pltpu.make_async_copy(source, place, signals.at[i])
+        for i, (source, place) in enumerate(zip(sources, places))
+    ]
+    for copy in copies:
+        copy.start()
+    return copies
+
+
+def prepare(*refs, dims):
+    border_ref, request_ref, place_ref, ids_ref, owner_ref, target_ref, nodes_ref, signals = refs[4:]
+    copies = fetch(refs[:4], (ids_ref, owner_ref, target_ref, nodes_ref), signals)
+    for copy in copies[:3]:
+        copy.wait()
     bricks, capacity = dims
     edges = owner_ref.shape[1]
-    border = ids_ref.shape[0] * 128
-    border_ref[:border, :] = picked(ids_ref[...], nodes_ref[...]).astype(BF16)
-    border_ref[border:, :] = jnp.ones_like(border_ref[border:, :])
     owner = owner_ref[...]
     target = target_ref[...]
     mine = iota((bricks, edges), 0) == owner
@@ -77,37 +89,45 @@
     low = (mine_f * (target & 31).astype(F32)).astype(BF16)
     request = dot_nt(high, at_slot) * 32.0 + dot_nt(low, at_slot)
     request_ref[...] = request.astype(jnp.int32)
-
-
-def project(nodes_ref, gain_ref, w_ref, request_ref, q_ref, kv_ref, column_ref):
+    border = ids_ref.shape[0] * 128
+    hot = hot_rows(ids_ref[...], nodes_ref.shape[0])
+    copies[3].wait()
+    border_ref[:border, :] = dot(hot, nodes_ref[...]).astype(BF16)
+    border_ref[border:, :] = jnp.ones_like(border_ref[border:, :])
+
+
+def project(*refs):
+    q_ref, kv_ref, nodes_ref, gain_ref, w_ref, signals = refs[3:]
+    copies = fetch(refs[:3], (nodes_ref, gain_ref, w_ref), signals)
     width = nodes_ref.shape[1]
+    copies[0].wait()
+    copies[1].wait()
     normed = normed_rows(nodes_ref[...], gain_ref[...])
     scale = 1.4426950408889634 / HEAD_DIM**0.5
+    copies[2].wait()
     q_ref[...] = (dot(normed, w_ref[:, :width]) * scale).astype(BF16)
     kv_ref[...] = dot(normed, w_ref[:, width:]).astype(BF16)
-    column_ref[...] = jnp.transpose(request_ref[...])
 
 
 def attend(*refs, pieces):
-    nodes_ref, q_ref, kv_ref = refs[:3]
-    halo_refs = refs[3 : 3 + pieces]
-    (
-        mask_ref,
-        gain_ref,
-        w_qkv_ref,
-        w_out_ref,
-        w_target_ref,
-        column_ref,
-        state_ref,
-        answer_ref,
-        v_ref,
-    ) = refs[3 + pieces :]
+    far_refs = refs[:6]
+    q_ref, kv_ref, request_ref = refs[6:9]
+    halo_refs = refs[9 : 9 + pieces]
+    state_ref, answer_ref, v_ref = refs[9 + pieces : 12 + pieces]
+    mask_ref, gain_ref, w_kv_ref, nodes_ref, w_out_ref, w_target_ref, signals = refs[12 + pieces :]
     rows, width = q_ref.shape
+    sources = list(far_refs)
+    sources[2] = far_refs[2].at[:, width:]
+    copies = fetch(
+        sources, (mask_ref, gain_ref, w_kv_ref, nodes_ref, w_out_ref, w_target_ref), signals
+    )
+    for copy in copies[:3]:
+        copy.wait()
     blocks = rows // BLOCK
     keys = v_ref.shape[1]
     border = (keys - rows) // pieces
     halo_nodes = jnp.concatenate([ref[:border, :] for ref in halo_refs], 0)
-    halo = dot(normed_rows(halo_nodes, gain_ref[...]), w_qkv_ref[:, width:]).astype(BF16)
+    halo = dot(normed_rows(halo_nodes, gain_ref[...]), w_kv_ref[...]).astype(BF16)
     low_keys = iota((keys, PAIR), 1) < HEAD_DIM
     low = iota((rows, PAIR), 1) < HEAD_DIM
 
@@ -151,13 +171,15 @@
             mixed.append(dot(weights, v_ref[2 * pair + half]))
         total = pltpu.roll(jnp.where(low, mixed[1], mixed[0]), HEAD_DIM, 1)
         attended.append((jnp.where(low, mixed[0], mixed[1]) / total).astype(BF16))
+    for copy in copies[3:]:
+        copy.wait()
     state = nodes_ref[...].astype(F32) + dot(jnp.concatenate(attended, 1), w_out_ref[...])
     state = state.astype(BF16)
     state_ref[...] = state
     table = dot(state, w_target_ref[...]).astype(BF16)
-    bricks = column_ref.shape[1]
+    bricks = request_ref.shape[0]
     capacity = answer_ref.shape[0] // bricks
-    columns = column_ref[...]
+    columns = jnp.transpose(request_ref[...])
     lanes = iota((capacity, rows), 1)
     hot = [ones_where(columns[:capacity, b : b + 1] == lanes) for b in range(bricks)]
     answer_ref[...] = dot(jnp.concatenate(hot, 0), table).astype(BF16)
@@ -184,12 +206,18 @@
     return pltpu.with_memory_space_constraint(array, pltpu.VMEM)
 
 
-def run(kernel, outs, *args, scratch=(), mib=16):
+def away(array):
+    return pltpu.with_memory_space_constraint(array, pltpu.HBM)
+
+
+def run(kernel, outs, *args, scratch=(), mib=16, far=0):
     space = pl.BlockSpec(memory_space=pltpu.VMEM)
+    left = pl.BlockSpec(memory_space=FAR)
+    args = [away(arg) for arg in args[:far]] + list(args[far:])
     return pl.pallas_call(
         kernel,
         out_shape=tuple(outs),
-        in_specs=[space] * len(args),
+        in_specs=[left] * far + [space] * (len(args) - far),
         out_specs=(space,) * len(outs),
         scratch_shapes=scratch,
         compiler_params=pltpu.CompilerParams(vmem_limit_bytes=mib * 1024 * 1024),
@@ -201,15 +229,15 @@
 
 
 def neighbours(block):
-    pieces = []
+    steps = []
     for axis in ("gy", "gz"):
         count = lax.axis_size(axis)
         for first in range(min(2, count - 1)):
             swaps = []
             for i in range(first, count - 1, 2):
                 swaps += [(i, i + 1), (i + 1, i)]
-            pieces.append(lax.ppermute(block, axis, swaps))
-    return pieces
+            steps.append((axis, swaps))
+    return [lax.ppermute(block, axis, swaps) for axis, swaps in reversed(steps)]
 
 
 def local(
@@ -234,51 +262,70 @@
     bricks = lax.axis_size("gy") * lax.axis_size("gz")
     capacity = max(2 * edges // bricks, 2)
     hidden = w_target.shape[1]
-    nodes_near = near(nodes)
+    integer = jnp.int32
     border, request, place = run(
         functools.partial(prepare, dims=(bricks, capacity)),
         (
             shape((border_count + 16, width), BF16),
-            shape((bricks, 128), jnp.int32),
-            shape((edges // 128, 128), jnp.int32),
+            shape((bricks, 128), integer),
+            shape((edges // 128, 128), integer),
         ),
         border_ids.reshape(border_count // 128, 128),
         edge_owner.reshape(1, edges),
         edge_target.reshape(1, edges),
-        nodes_near,
-    )
+        nodes,
+        far=4,
+        scratch=[
+            pltpu.VMEM((border_count // 128, 128), integer),
+            pltpu.VMEM((1, edges), integer),
+            pltpu.VMEM((1, edges), integer),
+            pltpu.VMEM((rows, width), BF16),
+            pltpu.SemaphoreType.DMA((4,)),
+        ],
+    )
+    asked = lax.all_to_all(request, ("gy", "gz"), split_axis=0, concat_axis=0, tiled=True)
     halo = neighbours(border)
-    asked = lax.all_to_all(request, ("gy", "gz"), split_axis=0, concat_axis=0, tiled=True)
 
     gain = norm_gain.reshape(1, width)
-    w_qkv_near = near(w_qkv)
-    q, kv, columns = run(
+    q, kv = run(
         project,
-        (
+        (pltpu.VMEM((rows, width), BF16), pltpu.VMEM((rows, 2 * width), BF16)),
+        nodes,
+        gain,
+        w_qkv,
+        far=3,
+        scratch=[
             pltpu.VMEM((rows, width), BF16),
-            pltpu.VMEM((rows, 2 * width), BF16),
-            pltpu.VMEM((128, bricks), jnp.int32),
-        ),
-        nodes_near,
-        gain,
-        w_qkv_near,
-        near(asked),
+            pltpu.VMEM((1, width), F32),
+            pltpu.VMEM((width, 3 * width), BF16),
+            pltpu.SemaphoreType.DMA((3,)),
+        ],
     )
     node_state, answers = run(
         functools.partial(attend, pieces=len(halo)),
         (shape((rows, width), BF16), shape((bricks * capacity, hidden), BF16)),
-        nodes_near,
+        block_mask,
+        gain,
+        w_qkv,
+        nodes,
+        w_attn_out,
+        w_target,
         q,
         kv,
+        near(asked),
         *[near(piece) for piece in halo],
-        block_mask,
-        gain,
-        w_qkv_near,
-        near(w_attn_out),
-        near(w_target),
-        columns,
+        far=6,
         mib=32,
-        scratch=[pltpu.VMEM((HEADS, rows + len(halo) * border_count, PAIR), BF16)],
+        scratch=[
+            pltpu.VMEM((HEADS, rows + len(halo) * border_count, PAIR), BF16),
+            pltpu.VMEM(block_mask.shape, integer),
+            pltpu.VMEM((1, width), F32),
+            pltpu.VMEM((width, 2 * width), BF16),
+            pltpu.VMEM((rows, width), BF16),
+            pltpu.VMEM((width, width), BF16),
+            pltpu.VMEM((width, hidden), BF16),
+            pltpu.SemaphoreType.DMA((6,)),
+        ],
     )
     answers = lax.all_to_all(
         answers.reshape(bricks, capacity, hidden),

time: 76.6 us -> 72.7 us (0.949)
  blocking collectives: 9.85 us -> 0 us
  local copies, waits for them, and re-layouts: 7.64 us -> 1.07 us
  Pallas kernels: 24.8 us -> 30.7 us
  starting transfers between devices: 10.6 us -> 16.2 us
  waiting for transfers between devices: 22.5 us -> 23.6 us
    all_to_all x1 -> x0, blocking collectives: 9.85 us -> none  [local(): lax.all_to_all(request, ('gy', 'gz'), split_axis=0, concat_axis=0, tiled=...]
    unnamed x38 -> x12, local copies, waits for them, and re-layouts: 7.64 us -> 1.07 us
    all_to_all x0 -> x1, starting transfers between devices: none -> 6.54 us  [local(): lax.all_to_all(request, ('gy', 'gz'), split_axis=0, concat_axis=0, tiled=...]
    pallas_call x5, Pallas kernels: 24.8 us -> 30.7 us  [run(): pl.pallas_call(kernel, out_shape=tuple(outs), in_specs=[left] * far + [sp...]
    all_to_all x0 -> x1, waiting for transfers between devices: none -> 1.12 us  [local(): lax.all_to_all(request, ('gy', 'gz'), split_axis=0, concat_axis=0, tiled=...]
    ppermute x3, starting transfers between devices: 5.18 us -> 4.23 us  [neighbours(): return [lax.ppermute(block, axis, swaps) for axis, swaps in reversed(steps)]]
  transfers between devices with their start and end apart: 4 -> 5, of which waited for: 1 -> 2; matrix products, arithmetic and copies ran while one was open for 0% -> 0% of each run, Pallas kernels for 4% -> 7%
where the time goes in v5:
time: 72.7 us; the launch traced here: 72.3 us
  Pallas kernels  30.7 us (42%)
  waiting for transfers between devices  23.6 us (32%)
  starting transfers between devices  16.2 us (22%)
  local copies, waits for them, and re-layouts  1.07 us (1%)
  between operations  0.75 us (1%)
    pallas_call x5, Pallas kernels, run(): pl.pallas_call(kernel, out_shape=tuple(outs), in_specs=[left] * far + [sp...  30.7 us
    all_to_all x1, waiting for transfers between devices, local(): lax.all_to_all(answers.reshape(bricks, capacity, hidden), ('gy', 'gz'), s...  22.5 us
    all_to_all x1, starting transfers between devices, local(): lax.all_to_all(request, ('gy', 'gz'), split_axis=0, concat_axis=0, tiled=...  6.54 us
    all_to_all x1, starting transfers between devices, local(): lax.all_to_all(answers.reshape(bricks, capacity, hidden), ('gy', 'gz'), s...  5.41 us
    ppermute x3, starting transfers between devices, neighbours(): return [lax.ppermute(block, axis, swaps) for axis, swaps in reversed(steps)]  4.23 us
  transfers between devices with their start and end apart: 5, of which 2 were waited for; matrix products, arithmetic and copies ran while one was open for 0% of the time, Pallas kernels for 7%

profile of v5, /device:TPU:9, one launch (start us, length us, event | category | flops | bytes accessed | tf_op | source)
XLA Modules:
  0.0 72.3 jit_solution(1021969530944060023)
XLA Ops:
  0.6 2.3 %shard_map.150 = (bf16[144,512]{1,0:T(8,128)(2,1)}, s32[16,128]{1,0:T(8,128)}, s32[4,128]{1,0:T(4,128)S(1)}) custom-call(s32[1,128]{1,0:T(1,128)} %bitcast.22, s32[1,512]{1,0:T(1,128)} %bitcast.19, s32[1,512]{1,0:T(1,128)} %bitcast.20, bf16[1024,512]{1,0:T(8,128)(2,1)} %refs_3_.3), custom_call_target="tpu_custom_call" | custom-call | tf_op jit(solution)/shard_map/pallas_call | solution.py:217
  2.9 1.3 %collective-permute-start.2 = (bf16[144,512]{1,0:T(8,128)(2,1)}, bf16[144,512]{1,0:T(8,128)(2,1)S(1)}, u32[]{:S(2)}, u32[]{:S(2)}) collective-permute-start(bf16[144,512]{1,0:T(8,128)(2,1)} %get-tuple-element.12), channel_id=1, source_target_pairs={{0,2},{2,0},{4,6},{6,4},{8,10},{10,8},{12,14},{14,12},{1,3},{3,1},... | collective-permute-start | bytes 442376 | tf_op jit(solution)/shard_map/ppermute | solution.py:240
  4.2 1.9 %collective-permute-start.1 = (bf16[144,512]{1,0:T(8,128)(2,1)}, bf16[144,512]{1,0:T(8,128)(2,1)S(1)}, u32[]{:S(2)}, u32[]{:S(2)}) collective-permute-start(bf16[144,512]{1,0:T(8,128)(2,1)} %get-tuple-element.12), channel_id=1, source_target_pairs={{2,4},{4,2},{6,8},{8,6},{10,12},{12,10},{3,5},{5,3},{7,9},{9,7},{1... | collective-permute-start | bytes 442376 | tf_op jit(solution)/shard_map/ppermute | solution.py:240
  6.2 1.0 %collective-permute-start = (bf16[144,512]{1,0:T(8,128)(2,1)}, bf16[144,512]{1,0:T(8,128)(2,1)}, u32[]{:S(2)}, u32[]{:S(2)}) collective-permute-start(bf16[144,512]{1,0:T(8,128)(2,1)} %get-tuple-element.12), channel_id=1, source_target_pairs={{0,1},{1,0},{2,3},{3,2},{4,5},{5,4},{6,7},{7,6},{8,9},{9,8},{10,11... | collective-permute-start | bytes 442376 | tf_op jit(solution)/shard_map/ppermute | solution.py:240
  7.2 6.5 %all-to-all-start = ((s32[16,1,128]{2,1,0:T(1,128)}), s32[16,1,128]{2,1,0:T(1,128)S(1)}, u32[]{:S(2)}, u32[]{:S(2)}) async-start(s32[16,1,128]{2,1,0:T(1,128)} %bitcast.5), calls=%async_computation | async-start | bytes 16384 | tf_op jit(solution)/shard_map/all_to_all | solution.py:286
  13.7 3.6 %shard_map.149 = (bf16[1024,512]{1,0:T(8,128)(2,1)S(1)}, bf16[1024,1024]{1,0:T(8,128)(2,1)S(1)}) custom-call(bf16[1024,512]{1,0:T(8,128)(2,1)} %refs_3_.3, f32[1,512]{1,0:T(1,128)} %bitcast.17, bf16[512,1536]{1,0:T(8,128)(2,1)} %refs_2_.3), custom_call_target="tpu_custom_call" | custom-call | tf_op jit(solution)/shard_map/pallas_call | solution.py:217
  17.3 1.1 %all-to-all-done = s32[16,1,128]{2,1,0:T(1,128)S(1)} async-done(((s32[16,1,128]{2,1,0:T(1,128)}), s32[16,1,128]{2,1,0:T(1,128)S(1)}, u32[]{:S(2)}, u32[]{:S(2)}) %all-to-all-start) | async-done | bytes 8224 | tf_op jit(solution)/shard_map/all_to_all | solution.py:286
  18.4 0.0 collective-permute-done.2.refs_11_
  18.4 0.0 collective-permute-done.1.refs_10_
  18.4 0.0 collective-permute-done.refs_9_
  18.4 21.7 %shard_map.151 = (bf16[1024,512]{1,0:T(8,128)(2,1)}, bf16[1024,512]{1,0:T(8,128)(2,1)}) custom-call(s32[8,8]{1,0:T(8,128)} %refs_0_.3, f32[1,512]{1,0:T(1,128)} %bitcast.18, bf16[512,1536]{1,0:T(8,128)(2,1)} %refs_2_.3, bf16[1024,512]{1,0:T(8,128)(2,1)} %refs_3_.3, bf16[512,512]{1,0:T(8,128)(2,1)} %refs_4_.1, bf16[512,512]{1,0:T(8,128)(2,1)} %refs_5_.1, ...), custom_call_target="tpu_custom_call" | custom-call | tf_op jit(solution)/shard_map/pallas_call | solution.py:217
  40.1 0.0 copy-start
  40.1 0.0 copy-start.2
  40.1 0.0 copy-start.3
  40.2 0.0 copy-start.4
  40.2 0.0 copy-start.5
  40.2 5.4 %all-to-all-start.1 = ((bf16[16,64,512]{2,1,0:T(8,128)(2,1)}), bf16[16,64,512]{2,1,0:T(8,128)(2,1)S(1)}, u32[]{:S(2)}, u32[]{:S(2)}) async-start(bf16[16,64,512]{2,1,0:T(8,128)(2,1)} %bitcast.7), calls=%async_computation.1 | async-start | bytes 2097152 | tf_op jit(solution)/shard_map/all_to_all | solution.py:330
  45.6 0.0 copy-done
  45.6 0.0 copy-done.2
  45.6 0.0 copy-done.3
  45.6 0.0 copy-done.4
  45.6 0.0 copy-start.1
  45.6 1.0 %copy-done.1 = bf16[512,512]{1,0:T(8,128)(2,1)S(1)} copy-done((bf16[512,512]{1,0:T(8,128)(2,1)S(1)}, bf16[512,512]{1,0:T(8,128)(2,1)}, u32[]{:S(2)}) %copy-start.1) | copy-done | bytes 524312
  46.7 1.3 %shard_map.152.part_ref = f32[512,512]{1,0:T(8,128)S(1)} custom-call(s32[4,128]{1,0:T(4,128)S(1)} %bitcast.15, bf16[1024,512]{1,0:T(8,128)(2,1)S(1)} %copy-done, bf16[512,512]{1,0:T(8,128)(2,1)S(1)} %copy-done.1, bf16[512,128]{1,0:T(8,128)(2,1)S(1)} %copy-done.2, bf16[128,512]{1,0:T(8,128)(2,1)S(1)} %copy-done.3), custom_call_target="tpu_custom_call" | custom-call | tf_op jit(solution)/shard_map/pallas_call | solution.py:217
  48.0 22.5 %all-to-all-done.1 = bf16[16,64,512]{2,1,0:T(8,128)(2,1)S(1)} async-done(((bf16[16,64,512]{2,1,0:T(8,128)(2,1)}), bf16[16,64,512]{2,1,0:T(8,128)(2,1)S(1)}, u32[]{:S(2)}, u32[]{:S(2)}) %all-to-all-start.1) | async-done | bytes 1048608 | tf_op jit(solution)/shard_map/all_to_all | solution.py:330
  70.5 0.0 copy-done.5
  70.5 1.8 %shard_map.153 = f32[1,512]{1,0:T(1,128)} custom-call(s32[4,128]{1,0:T(4,128)S(1)} %get-tuple-element.14.place_ref, bf16[1024,512]{1,0:T(8,128)(2,1)S(1)} %bitcast.13, f32[512,512]{1,0:T(8,128)S(1)} %shard_map.152.part_ref, f32[1,512]{1,0:T(1,128)S(1)} %bitcast.16), custom_call_target="tpu_custom_call" | custom-call | tf_op jit(solution)/shard_map/pallas_call | solution.py:217
Async XLA Ops:
  2.9 15.5 %collective-permute-start.2 = (bf16[144,512]{1,0:T(8,128)(2,1)}, bf16[144,512]{1,0:T(8,128)(2,1)S(1)}, u32[]{:S(2)}, u32[]{:S(2)}) collective-permute-start(bf16[144,512]{1,0:T(8,128)(2,1)} %get-tuple-element.12), channel_id=1, source_target_pairs={{0,2},{2,0},{4,6},{6,4},{8,10},{10,8},{12,14},{14,12},{1,3},{3,1},... | collective-permute-start | bytes 442376 | tf_op jit(solution)/shard_map/ppermute | solution.py:240
  4.2 14.2 %collective-permute-start.1 = (bf16[144,512]{1,0:T(8,128)(2,1)}, bf16[144,512]{1,0:T(8,128)(2,1)S(1)}, u32[]{:S(2)}, u32[]{:S(2)}) collective-permute-start(bf16[144,512]{1,0:T(8,128)(2,1)} %get-tuple-element.12), channel_id=1, source_target_pairs={{2,4},{4,2},{6,8},{8,6},{10,12},{12,10},{3,5},{5,3},{7,9},{9,7},{1... | collective-permute-start | bytes 442376 | tf_op jit(solution)/shard_map/ppermute | solution.py:240
  6.2 12.3 %collective-permute-start = (bf16[144,512]{1,0:T(8,128)(2,1)}, bf16[144,512]{1,0:T(8,128)(2,1)}, u32[]{:S(2)}, u32[]{:S(2)}) collective-permute-start(bf16[144,512]{1,0:T(8,128)(2,1)} %get-tuple-element.12), channel_id=1, source_target_pairs={{0,1},{1,0},{2,3},{3,2},{4,5},{5,4},{6,7},{7,6},{8,9},{9,8},{10,11... | collective-permute-start | bytes 442376 | tf_op jit(solution)/shard_map/ppermute | solution.py:240
  7.2 11.2 %all-to-all-start = ((s32[16,1,128]{2,1,0:T(1,128)}), s32[16,1,128]{2,1,0:T(1,128)S(1)}, u32[]{:S(2)}, u32[]{:S(2)}) async-start(s32[16,1,128]{2,1,0:T(1,128)} %bitcast.5), calls=%async_computation | async-start | bytes 16384 | tf_op jit(solution)/shard_map/all_to_all | solution.py:286
  40.1 5.5 %copy-start = (bf16[1024,512]{1,0:T(8,128)(2,1)S(1)}, bf16[1024,512]{1,0:T(8,128)(2,1)}, u32[]{:S(2)}) copy-start(bf16[1024,512]{1,0:T(8,128)(2,1)} %get-tuple-element.7.state_ref) | copy-start | bytes 3145732
  40.1 5.5 %copy-start.2 = (bf16[512,128]{1,0:T(8,128)(2,1)S(1)}, bf16[512,128]{1,0:T(8,128)(2,1)}, u32[]{:S(2)}) copy-start(bf16[512,128]{1,0:T(8,128)(2,1)} %contact_ref.1) | copy-start | bytes 393220
  40.1 5.5 %copy-start.3 = (bf16[128,512]{1,0:T(8,128)(2,1)S(1)}, bf16[128,512]{1,0:T(8,128)(2,1)}, u32[]{:S(2)}) copy-start(bf16[128,512]{1,0:T(8,128)(2,1)} %w_ref.1) | copy-start | bytes 393220
  40.2 5.5 %copy-start.4 = (s32[512]{0:T(512)S(1)}, s32[512]{0:T(512)}, u32[]{:S(2)}) copy-start(s32[512]{0:T(512)} %param.18) | copy-start | bytes 6148
  40.2 30.3 %copy-start.5 = (f32[512]{0:T(512)S(1)}, f32[512]{0:T(512)}, u32[]{:S(2)}) copy-start(f32[512]{0:T(512)} %param.27) | copy-start | bytes 6148
  40.2 30.3 %all-to-all-start.1 = ((bf16[16,64,512]{2,1,0:T(8,128)(2,1)}), bf16[16,64,512]{2,1,0:T(8,128)(2,1)S(1)}, u32[]{:S(2)}, u32[]{:S(2)}) async-start(bf16[16,64,512]{2,1,0:T(8,128)(2,1)} %bitcast.7), calls=%async_computation.1 | async-start | bytes 2097152 | tf_op jit(solution)/shard_map/all_to_all | solution.py:330
  45.6 1.0 %copy-start.1 = (bf16[512,512]{1,0:T(8,128)(2,1)S(1)}, bf16[512,512]{1,0:T(8,128)(2,1)}, u32[]{:S(2)}) copy-start(bf16[512,512]{1,0:T(8,128)(2,1)} %w_source_ref.1) | copy-start | bytes 1572868

commit v6 on v5

--- a/solution.py
+++ b/solution.py
@@ -68,8 +68,10 @@
 
 
 def prepare(*refs, dims):
-    border_ref, request_ref, place_ref, ids_ref, owner_ref, target_ref, nodes_ref, signals = refs[4:]
-    copies = fetch(refs[:4], (ids_ref, owner_ref, target_ref, nodes_ref), signals)
+    border_ref, request_ref, place_ref, nodes_ref, gain_ref, mask_ref, w_ref = refs[7:14]
+    ids_ref, owner_ref, target_ref, signals = refs[14:]
+    places = (ids_ref, owner_ref, target_ref, nodes_ref, gain_ref, mask_ref, w_ref)
+    copies = fetch(refs[:7], places, signals)
     for copy in copies[:3]:
         copy.wait()
     bricks, capacity = dims
@@ -94,40 +96,29 @@
     copies[3].wait()
     border_ref[:border, :] = dot(hot, nodes_ref[...]).astype(BF16)
     border_ref[border:, :] = jnp.ones_like(border_ref[border:, :])
-
-
-def project(*refs):
-    q_ref, kv_ref, nodes_ref, gain_ref, w_ref, signals = refs[3:]
-    copies = fetch(refs[:3], (nodes_ref, gain_ref, w_ref), signals)
+    for copy in copies[4:]:
+        copy.wait()
+
+
+def project(nodes_ref, gain_ref, w_ref, q_ref, kv_ref):
     width = nodes_ref.shape[1]
-    copies[0].wait()
-    copies[1].wait()
     normed = normed_rows(nodes_ref[...], gain_ref[...])
     scale = 1.4426950408889634 / HEAD_DIM**0.5
-    copies[2].wait()
     q_ref[...] = (dot(normed, w_ref[:, :width]) * scale).astype(BF16)
     kv_ref[...] = dot(normed, w_ref[:, width:]).astype(BF16)
 
 
 def attend(*refs, pieces):
-    far_refs = refs[:6]
-    q_ref, kv_ref, request_ref = refs[6:9]
-    halo_refs = refs[9 : 9 + pieces]
-    state_ref, answer_ref, v_ref = refs[9 + pieces : 12 + pieces]
-    mask_ref, gain_ref, w_kv_ref, nodes_ref, w_out_ref, w_target_ref, signals = refs[12 + pieces :]
+    w_out_hbm, w_target_hbm, nodes_ref, gain_ref, mask_ref, w_ref, q_ref, kv_ref = refs[:8]
+    halo_refs = refs[8 : 8 + pieces]
+    state_ref, table_ref, w_out_ref, w_target_ref, v_ref, signals = refs[8 + pieces :]
+    copies = fetch((w_out_hbm, w_target_hbm), (w_out_ref, w_target_ref), signals)
     rows, width = q_ref.shape
-    sources = list(far_refs)
-    sources[2] = far_refs[2].at[:, width:]
-    copies = fetch(
-        sources, (mask_ref, gain_ref, w_kv_ref, nodes_ref, w_out_ref, w_target_ref), signals
-    )
-    for copy in copies[:3]:
-        copy.wait()
     blocks = rows // BLOCK
-    keys = v_ref.shape[1]
+    keys = v_ref.shape[0] // 2
     border = (keys - rows) // pieces
     halo_nodes = jnp.concatenate([ref[:border, :] for ref in halo_refs], 0)
-    halo = dot(normed_rows(halo_nodes, gain_ref[...]), w_kv_ref[...]).astype(BF16)
+    halo = dot(normed_rows(halo_nodes, gain_ref[...]), w_ref[:, width:]).astype(BF16)
     low_keys = iota((keys, PAIR), 1) < HEAD_DIM
     low = iota((rows, PAIR), 1) < HEAD_DIM
 
@@ -147,6 +138,9 @@
     key_block = jnp.concatenate(
         [ones_where(own == iota(own.shape, 1)), ones_where(far == iota(far.shape, 1))], 0
     )
+    key_block = jnp.concatenate([key_block, key_block], 0)
+    v_ref[:keys, PAIR:] = jnp.zeros((keys, PAIR), BF16)
+    v_ref[keys:, :PAIR] = jnp.zeros((keys, PAIR), BF16)
 
     attended = []
     for pair in range(width // PAIR):
@@ -154,35 +148,44 @@
         v_at = slice(width + pair * PAIR, width + (pair + 1) * PAIR)
         values = jnp.concatenate([kv_ref[:, v_at], halo[:, v_at]], 0)
         one = jnp.ones_like(values)
-        v_ref[2 * pair] = jnp.where(low_keys, values, one)
-        v_ref[2 * pair + 1] = jnp.where(low_keys, one, values)
-        q_pair = q_ref[:, at]
+        v_ref[:keys, :PAIR] = jnp.where(low_keys, values, one)
+        v_ref[keys:, PAIR:] = jnp.where(low_keys, one, values)
         k_pair = jnp.concatenate([kv_ref[:, at], halo[:, at]], 0)
+        zero = jnp.zeros_like(k_pair)
+        k_pair = jnp.concatenate(
+            [jnp.where(low_keys, k_pair, zero), jnp.where(low_keys, zero, k_pair)], 0
+        )
         k_pair = jnp.concatenate([k_pair, key_block], 1)
-        mixed = []
-        for half in range(2):
-            q_own = jnp.where(low if half == 0 else ~low, q_pair, jnp.zeros_like(q_pair))
-            scores = dot_nt(jnp.concatenate([q_own, bias], 1), k_pair)
-            fold = scores[:, :128]
+        scores = dot_nt(jnp.concatenate([q_ref[:, at], bias], 1), k_pair)
+        weights = []
+        for half in (scores[:, :keys], scores[:, keys:]):
+            fold = half[:, :128]
             for c in range(128, keys, 128):
-                fold = jnp.maximum(fold, scores[:, c : c + 128])
+                fold = jnp.maximum(fold, half[:, c : c + 128])
             top = jnp.max(fold, axis=1, keepdims=True)
-            weights = jnp.exp2((scores - top).astype(BF16))
-            mixed.append(dot(weights, v_ref[2 * pair + half]))
-        total = pltpu.roll(jnp.where(low, mixed[1], mixed[0]), HEAD_DIM, 1)
-        attended.append((jnp.where(low, mixed[0], mixed[1]) / total).astype(BF16))
-    for copy in copies[3:]:
+            weights.append(jnp.exp2((half - top).astype(BF16)))
+        mixed = dot(jnp.concatenate(weights, 1), v_ref[...])
+        even, odd = mixed[:, :PAIR], mixed[:, PAIR:]
+        total = pltpu.roll(jnp.where(low, odd, even), HEAD_DIM, 1)
+        attended.append((jnp.where(low, even, odd) / total).astype(BF16))
+    for copy in copies:
         copy.wait()
     state = nodes_ref[...].astype(F32) + dot(jnp.concatenate(attended, 1), w_out_ref[...])
     state = state.astype(BF16)
     state_ref[...] = state
-    table = dot(state, w_target_ref[...]).astype(BF16)
+    table_ref[...] = dot(state, w_target_ref[...]).astype(BF16)
+
+
+def answer(table_hbm, request_ref, answer_ref, table_ref, signals):
+    (copy,) = fetch((table_hbm,), (table_ref,), signals)
     bricks = request_ref.shape[0]
     capacity = answer_ref.shape[0] // bricks
     columns = jnp.transpose(request_ref[...])
-    lanes = iota((capacity, rows), 1)
+    lanes = iota((capacity, table_ref.shape[0]), 1)
     hot = [ones_where(columns[:capacity, b : b + 1] == lanes) for b in range(bricks)]
-    answer_ref[...] = dot(jnp.concatenate(hot, 0), table).astype(BF16)
+    hot = jnp.concatenate(hot, 0)
+    copy.wait()
+    answer_ref[...] = dot(hot, table_ref[...]).astype(BF16)
 
 
 def own_part(
@@ -263,69 +266,71 @@
     capacity = max(2 * edges // bricks, 2)
     hidden = w_target.shape[1]
     integer = jnp.int32
-    border, request, place = run(
+    border, request, place, nodes_near, gain, mask, w_near = run(
         functools.partial(prepare, dims=(bricks, capacity)),
         (
             shape((border_count + 16, width), BF16),
             shape((bricks, 128), integer),
             shape((edges // 128, 128), integer),
+            pltpu.VMEM((rows, width), BF16),
+            pltpu.VMEM((1, width), F32),
+            pltpu.VMEM(block_mask.shape, integer),
+            pltpu.VMEM((width, 3 * width), BF16),
         ),
         border_ids.reshape(border_count // 128, 128),
         edge_owner.reshape(1, edges),
         edge_target.reshape(1, edges),
         nodes,
-        far=4,
+        norm_gain.reshape(1, width),
+        block_mask,
+        w_qkv,
+        far=7,
         scratch=[
             pltpu.VMEM((border_count // 128, 128), integer),
             pltpu.VMEM((1, edges), integer),
             pltpu.VMEM((1, edges), integer),
-            pltpu.VMEM((rows, width), BF16),
-            pltpu.SemaphoreType.DMA((4,)),
+            pltpu.SemaphoreType.DMA((7,)),
         ],
     )
     asked = lax.all_to_all(request, ("gy", "gz"), split_axis=0, concat_axis=0, tiled=True)
     halo = neighbours(border)
 
-    gain = norm_gain.reshape(1, width)
     q, kv = run(
         project,
         (pltpu.VMEM((rows, width), BF16), pltpu.VMEM((rows, 2 * width), BF16)),
-        nodes,
+        nodes_near,
         gain,
-        w_qkv,
-        far=3,
-        scratch=[
-            pltpu.VMEM((rows, width), BF16),
-            pltpu.VMEM((1, width), F32),
-            pltpu.VMEM((width, 3 * width), BF16),
-            pltpu.SemaphoreType.DMA((3,)),
-        ],
-    )
-    node_state, answers = run(
+        w_near,
+    )
+    keys = rows + len(halo) * border_count
+    node_state, table = run(
         functools.partial(attend, pieces=len(halo)),
-        (shape((rows, width), BF16), shape((bricks * capacity, hidden), BF16)),
-        block_mask,
-        gain,
-        w_qkv,
-        nodes,
+        (shape((rows, width), BF16), shape((rows, hidden), BF16)),
         w_attn_out,
         w_target,
+        nodes_near,
+        gain,
+        mask,
+        w_near,
         q,
         kv,
-        near(asked),
         *[near(piece) for piece in halo],
-        far=6,
-        mib=32,
+        far=2,
+        mib=40,
         scratch=[
-            pltpu.VMEM((HEADS, rows + len(halo) * border_count, PAIR), BF16),
-            pltpu.VMEM(block_mask.shape, integer),
-            pltpu.VMEM((1, width), F32),
-            pltpu.VMEM((width, 2 * width), BF16),
-            pltpu.VMEM((rows, width), BF16),
             pltpu.VMEM((width, width), BF16),
             pltpu.VMEM((width, hidden), BF16),
-            pltpu.SemaphoreType.DMA((6,)),
+            pltpu.VMEM((2 * keys, 2 * PAIR), BF16),
+            pltpu.SemaphoreType.DMA((2,)),
         ],
+    )
+    (answers,) = run(
+        answer,
+        (shape((bricks * capacity, hidden), BF16),),
+        table,
+        near(asked),
+        far=1,
+        scratch=[pltpu.VMEM((rows, hidden), BF16), pltpu.SemaphoreType.DMA((1,))],
     )
     answers = lax.all_to_all(
         answers.reshape(bricks, capacity, hidden),

time: 72.7 us -> 71 us (0.977)
  Pallas kernels: 30.7 us -> 28.4 us
  waiting for transfers between devices: 23.6 us -> 22.4 us
  local copies, waits for them, and re-layouts: 1.07 us -> 2.03 us
    pallas_call x5 -> x6, Pallas kernels: 30.7 us -> 28.4 us  [run(): pl.pallas_call(kernel, out_shape=tuple(outs), in_specs=[left] * far + [sp...]
    all_to_all x1, waiting for transfers between devices: 1.12 us -> 0.01 us  [local(): lax.all_to_all(request, ('gy', 'gz'), split_axis=0, concat_axis=0, tiled=...]
    unnamed x12 -> x14, local copies, waits for them, and re-layouts: 1.07 us -> 2.03 us
    all_to_all x1, starting transfers between devices: 5.41 us -> 6.16 us  [local(): lax.all_to_all(answers.reshape(bricks, capacity, hidden), ('gy', 'gz'), s...]
  transfers between devices with their start and end apart: 5 -> 5, of which waited for: 2 -> 1; matrix products, arithmetic and copies ran while one was open for 0% -> 0% of each run, Pallas kernels for 7% -> 29%
where the time goes in v6:
time: 71 us; the launch traced here: 70.6 us
  Pallas kernels  28.4 us (40%)
  waiting for transfers between devices  22.4 us (32%)
  starting transfers between devices  16.9 us (24%)
  local copies, waits for them, and re-layouts  2.03 us (3%)
  between operations  0.79 us (1%)
    pallas_call x6, Pallas kernels, run(): pl.pallas_call(kernel, out_shape=tuple(outs), in_specs=[left] * far + [sp...  28.4 us
    all_to_all x1, waiting for transfers between devices, local(): lax.all_to_all(answers.reshape(bricks, capacity, hidden), ('gy', 'gz'), s...  22.4 us
    all_to_all x1, starting transfers between devices, local(): lax.all_to_all(request, ('gy', 'gz'), split_axis=0, concat_axis=0, tiled=...  6.54 us
    all_to_all x1, starting transfers between devices, local(): lax.all_to_all(answers.reshape(bricks, capacity, hidden), ('gy', 'gz'), s...  6.16 us
    ppermute x3, starting transfers between devices, neighbours(): return [lax.ppermute(block, axis, swaps) for axis, swaps in reversed(steps)]  4.23 us
    unnamed x14, local copies, waits for them, and re-layouts  2.03 us
  transfers between devices with their start and end apart: 5, of which 1 were waited for; matrix products, arithmetic and copies ran while one was open for 0% of the time, Pallas kernels for 29%

profile of v6, /device:TPU:9, one launch (start us, length us, event | category | flops | bytes accessed | tf_op | source)
XLA Modules:
  0.0 70.6 jit_solution(2924714401131515663)
XLA Ops:
  0.6 2.5 %shard_map.149 = (bf16[144,512]{1,0:T(8,128)(2,1)S(1)}, s32[16,128]{1,0:T(8,128)}, s32[4,128]{1,0:T(4,128)S(1)}, bf16[1024,512]{1,0:T(8,128)(2,1)S(1)}, f32[1,51...) custom-call(s32[1,128]{1,0:T(1,128)} %bitcast.21, s32[1,512]{1,0:T(1,128)} %bitcast.17, ...), custom_call_target="tpu_custom_call" | custom-call | tf_op jit(solution)/shard_map/pallas_call | solution.py:220
  3.1 1.3 %collective-permute-start.2 = (bf16[144,512]{1,0:T(8,128)(2,1)S(1)}, bf16[144,512]{1,0:T(8,128)(2,1)S(1)}, u32[]{:S(2)}, u32[]{:S(2)}) collective-permute-start(bf16[144,512]{1,0:T(8,128)(2,1)S(1)} %get-tuple-element.19), channel_id=1, source_target_pairs={{0,2},{2,0},{4,6},{6,4},{8,10},{10,8},{12,14},{14,12},{1,3},{3,1},... | collective-permute-start | bytes 442376 | tf_op jit(solution)/shard_map/ppermute | solution.py:243
  4.4 1.9 %collective-permute-start.1 = (bf16[144,512]{1,0:T(8,128)(2,1)S(1)}, bf16[144,512]{1,0:T(8,128)(2,1)S(1)}, u32[]{:S(2)}, u32[]{:S(2)}) collective-permute-start(bf16[144,512]{1,0:T(8,128)(2,1)S(1)} %get-tuple-element.19), channel_id=1, source_target_pairs={{2,4},{4,2},{6,8},{8,6},{10,12},{12,10},{3,5},{5,3},{7,9},{9,7},{1... | collective-permute-start | bytes 442376 | tf_op jit(solution)/shard_map/ppermute | solution.py:243
  6.3 1.0 %collective-permute-start = (bf16[144,512]{1,0:T(8,128)(2,1)S(1)}, bf16[144,512]{1,0:T(8,128)(2,1)S(1)}, u32[]{:S(2)}, u32[]{:S(2)}) collective-permute-start(bf16[144,512]{1,0:T(8,128)(2,1)S(1)} %get-tuple-element.19), channel_id=1, source_target_pairs={{0,1},{1,0},{2,3},{3,2},{4,5},{5,4},{6,7},{7,6},{8,9},{9,8},{10,11... | collective-permute-start | bytes 442376 | tf_op jit(solution)/shard_map/ppermute | solution.py:243
  7.3 6.5 %all-to-all-start = ((s32[16,1,128]{2,1,0:T(1,128)}), s32[16,1,128]{2,1,0:T(1,128)S(1)}, u32[]{:S(2)}, u32[]{:S(2)}) async-start(s32[16,1,128]{2,1,0:T(1,128)} %bitcast.5), calls=%async_computation | async-start | bytes 16384 | tf_op jit(solution)/shard_map/all_to_all | solution.py:295
  13.9 1.9 %shard_map.150 = (bf16[1024,512]{1,0:T(8,128)(2,1)S(1)}, bf16[1024,1024]{1,0:T(8,128)(2,1)S(1)}) custom-call(bf16[1024,512]{1,0:T(8,128)(2,1)S(1)} %get-tuple-element.13.nodes_ref.refs_2_, f32[1,512]{1,0:T(1,128)S(1)} %get-tuple-element.14.gain_ref.refs_3_, bf16[512,1536]{1,0:T(8,128)(2,1)S(1)} %get-tuple-element.16.w_ref.refs_5_), custom_call_target="tpu_custom_call" | custom-call | tf_op jit(solution)/shard_map/pallas_call | solution.py:220
  15.8 0.0 collective-permute-done.2.refs_10_
  15.8 0.0 collective-permute-done.1.refs_9_
  15.8 0.0 collective-permute-done.refs_8_
  15.8 17.5 %shard_map.151 = (bf16[1024,512]{1,0:T(8,128)(2,1)}, bf16[1024,512]{1,0:T(8,128)(2,1)S(1)}) custom-call(bf16[512,512]{1,0:T(8,128)(2,1)} %refs_0_.1, bf16[512,512]{1,0:T(8,128)(2,1)} %refs_1_.1, bf16[1024,512]{1,0:T(8,128)(2,1)S(1)} %get-tuple-element.13.nodes_ref.refs_2_, f32[1,512]{1,0:T(1,128)S(1)} %get-tuple-element.14.gain_ref.refs_3_, ...), custom_call_target="tpu_custom_call" | custom-call | tf_op jit(solution)/shard_map/pallas_call | solution.py:220
  33.3 0.0 copy-start.1
  33.3 1.0 %copy-done.1 = bf16[1024,512]{1,0:T(8,128)(2,1)} copy-done((bf16[1024,512]{1,0:T(8,128)(2,1)}, bf16[1024,512]{1,0:T(8,128)(2,1)S(1)}, u32[]{:S(2)}) %copy-start.1) | copy-done | bytes 1048600
  34.2 0.0 all-to-all-done
  34.3 3.5 %shard_map.152 = bf16[1024,512]{1,0:T(8,128)(2,1)} custom-call(bf16[1024,512]{1,0:T(8,128)(2,1)} %copy-done.1, s32[16,128]{1,0:T(8,128)S(1)} %bitcast.14), custom_call_target="tpu_custom_call" | custom-call | tf_op jit(solution)/shard_map/pallas_call | solution.py:220
  37.7 0.0 copy-start
  37.7 0.0 copy-start.3
  37.8 0.0 copy-start.4
  37.8 0.0 copy-start.5
  37.8 6.2 %all-to-all-start.1 = ((bf16[16,64,512]{2,1,0:T(8,128)(2,1)}), bf16[16,64,512]{2,1,0:T(8,128)(2,1)S(1)}, u32[]{:S(2)}, u32[]{:S(2)}) async-start(bf16[16,64,512]{2,1,0:T(8,128)(2,1)} %bitcast.7), calls=%async_computation.1 | async-start | bytes 2097152 | tf_op jit(solution)/shard_map/all_to_all | solution.py:335
  43.9 0.0 copy-start.6
  43.9 0.0 copy-done
  44.0 0.0 copy-done.3
  44.0 0.0 copy-done.4
  44.0 0.0 copy-done.5
  44.0 0.0 copy-start.2
  44.0 1.0 %copy-done.2 = bf16[512,512]{1,0:T(8,128)(2,1)S(1)} copy-done((bf16[512,512]{1,0:T(8,128)(2,1)S(1)}, bf16[512,512]{1,0:T(8,128)(2,1)}, u32[]{:S(2)}) %copy-start.2) | copy-done | bytes 524312
  45.0 1.3 %shard_map.153.part_ref = f32[512,512]{1,0:T(8,128)S(1)} custom-call(s32[4,128]{1,0:T(4,128)S(1)} %bitcast.15, bf16[1024,512]{1,0:T(8,128)(2,1)S(1)} %copy-done, bf16[512,512]{1,0:T(8,128)(2,1)S(1)} %copy-done.2, bf16[512,128]{1,0:T(8,128)(2,1)S(1)} %copy-done.3, bf16[128,512]{1,0:T(8,128)(2,1)S(1)} %copy-done.4), custom_call_target="tpu_custom_call" | custom-call | tf_op jit(solution)/shard_map/pallas_call | solution.py:220
  46.4 22.4 %all-to-all-done.1 = bf16[16,64,512]{2,1,0:T(8,128)(2,1)S(1)} async-done(((bf16[16,64,512]{2,1,0:T(8,128)(2,1)}), bf16[16,64,512]{2,1,0:T(8,128)(2,1)S(1)}, u32[]{:S(2)}, u32[]{:S(2)}) %all-to-all-start.1) | async-done | bytes 1048608 | tf_op jit(solution)/shard_map/all_to_all | solution.py:335
  68.8 0.0 copy-done.6
  68.8 1.8 %shard_map.154 = f32[1,512]{1,0:T(1,128)} custom-call(s32[4,128]{1,0:T(4,128)S(1)} %get-tuple-element.21.place_ref, bf16[1024,512]{1,0:T(8,128)(2,1)S(1)} %bitcast.13, f32[512,512]{1,0:T(8,128)S(1)} %shard_map.153.part_ref, f32[1,512]{1,0:T(1,128)S(1)} %bitcast.16), custom_call_target="tpu_custom_call" | custom-call | tf_op jit(solution)/shard_map/pallas_call | solution.py:220
Async XLA Ops:
  3.1 12.7 %collective-permute-start.2 = (bf16[144,512]{1,0:T(8,128)(2,1)S(1)}, bf16[144,512]{1,0:T(8,128)(2,1)S(1)}, u32[]{:S(2)}, u32[]{:S(2)}) collective-permute-start(bf16[144,512]{1,0:T(8,128)(2,1)S(1)} %get-tuple-element.19), channel_id=1, source_target_pairs={{0,2},{2,0},{4,6},{6,4},{8,10},{10,8},{12,14},{14,12},{1,3},{3,1},... | collective-permute-start | bytes 442376 | tf_op jit(solution)/shard_map/ppermute | solution.py:243
  4.4 11.4 %collective-permute-start.1 = (bf16[144,512]{1,0:T(8,128)(2,1)S(1)}, bf16[144,512]{1,0:T(8,128)(2,1)S(1)}, u32[]{:S(2)}, u32[]{:S(2)}) collective-permute-start(bf16[144,512]{1,0:T(8,128)(2,1)S(1)} %get-tuple-element.19), channel_id=1, source_target_pairs={{2,4},{4,2},{6,8},{8,6},{10,12},{12,10},{3,5},{5,3},{7,9},{9,7},{1... | collective-permute-start | bytes 442376 | tf_op jit(solution)/shard_map/ppermute | solution.py:243
  6.3 9.5 %collective-permute-start = (bf16[144,512]{1,0:T(8,128)(2,1)S(1)}, bf16[144,512]{1,0:T(8,128)(2,1)S(1)}, u32[]{:S(2)}, u32[]{:S(2)}) collective-permute-start(bf16[144,512]{1,0:T(8,128)(2,1)S(1)} %get-tuple-element.19), channel_id=1, source_target_pairs={{0,1},{1,0},{2,3},{3,2},{4,5},{5,4},{6,7},{7,6},{8,9},{9,8},{10,11... | collective-permute-start | bytes 442376 | tf_op jit(solution)/shard_map/ppermute | solution.py:243
  7.3 26.9 %all-to-all-start = ((s32[16,1,128]{2,1,0:T(1,128)}), s32[16,1,128]{2,1,0:T(1,128)S(1)}, u32[]{:S(2)}, u32[]{:S(2)}) async-start(s32[16,1,128]{2,1,0:T(1,128)} %bitcast.5), calls=%async_computation | async-start | bytes 16384 | tf_op jit(solution)/shard_map/all_to_all | solution.py:295
  33.3 1.0 %copy-start.1 = (bf16[1024,512]{1,0:T(8,128)(2,1)}, bf16[1024,512]{1,0:T(8,128)(2,1)S(1)}, u32[]{:S(2)}) copy-start(bf16[1024,512]{1,0:T(8,128)(2,1)S(1)} %get-tuple-element.22.table_hbm) | copy-start | bytes 3145732
  37.7 6.2 %copy-start = (bf16[1024,512]{1,0:T(8,128)(2,1)S(1)}, bf16[1024,512]{1,0:T(8,128)(2,1)}, u32[]{:S(2)}) copy-start(bf16[1024,512]{1,0:T(8,128)(2,1)} %get-tuple-element.11.state_ref) | copy-start | bytes 3145732
  37.7 6.2 %copy-start.3 = (bf16[512,128]{1,0:T(8,128)(2,1)S(1)}, bf16[512,128]{1,0:T(8,128)(2,1)}, u32[]{:S(2)}) copy-start(bf16[512,128]{1,0:T(8,128)(2,1)} %contact_ref.1) | copy-start | bytes 393220
  37.8 6.2 %copy-start.4 = (bf16[128,512]{1,0:T(8,128)(2,1)S(1)}, bf16[128,512]{1,0:T(8,128)(2,1)}, u32[]{:S(2)}) copy-start(bf16[128,512]{1,0:T(8,128)(2,1)} %w_ref.1) | copy-start | bytes 393220
  37.8 6.2 %copy-start.5 = (s32[512]{0:T(512)S(1)}, s32[512]{0:T(512)}, u32[]{:S(2)}) copy-start(s32[512]{0:T(512)} %param.18) | copy-start | bytes 6148
  37.8 31.0 %all-to-all-start.1 = ((bf16[16,64,512]{2,1,0:T(8,128)(2,1)}), bf16[16,64,512]{2,1,0:T(8,128)(2,1)S(1)}, u32[]{:S(2)}, u32[]{:S(2)}) async-start(bf16[16,64,512]{2,1,0:T(8,128)(2,1)} %bitcast.7), calls=%async_computation.1 | async-start | bytes 2097152 | tf_op jit(solution)/shard_map/all_to_all | solution.py:335
  43.9 24.8 %copy-start.6 = (f32[512]{0:T(512)S(1)}, f32[512]{0:T(512)}, u32[]{:S(2)}) copy-start(f32[512]{0:T(512)} %param.27) | copy-start | bytes 6148
  44.0 1.0 %copy-start.2 = (bf16[512,512]{1,0:T(8,128)(2,1)S(1)}, bf16[512,512]{1,0:T(8,128)(2,1)}, u32[]{:S(2)}) copy-start(bf16[512,512]{1,0:T(8,128)(2,1)} %w_source_ref.1) | copy-start | bytes 1572868

commit v7 on v6

--- a/solution.py
+++ b/solution.py
@@ -109,10 +109,14 @@
 
 
 def attend(*refs, pieces):
-    w_out_hbm, w_target_hbm, nodes_ref, gain_ref, mask_ref, w_ref, q_ref, kv_ref = refs[:8]
+    w_out_hbm, w_target_hbm, nodes_hbm, gain_ref, mask_ref, w_ref, q_ref, kv_ref = refs[:8]
     halo_refs = refs[8 : 8 + pieces]
-    state_ref, table_ref, w_out_ref, w_target_ref, v_ref, signals = refs[8 + pieces :]
-    copies = fetch((w_out_hbm, w_target_hbm), (w_out_ref, w_target_ref), signals)
+    state_hbm, table_ref, w_out_ref, w_target_ref, nodes_ref, v_ref, signals, sent = refs[
+        8 + pieces :
+    ]
+    copies = fetch(
+        (w_out_hbm, w_target_hbm, nodes_hbm), (w_out_ref, w_target_ref, nodes_ref), signals
+    )
     rows, width = q_ref.shape
     blocks = rows // BLOCK
     keys = v_ref.shape[0] // 2
@@ -127,8 +131,8 @@
     seen = dot(mask_ref[...].astype(F32).astype(BF16), ones_where(row == lane))
     seen = jnp.where(row == lane, 1.0, seen)
     for h in range(pieces):
-        sent = halo_refs[h][border : border + 1, :128].astype(F32)
-        seen = jnp.where(lane == blocks + h, sent, seen)
+        marker = halo_refs[h][border : border + 1, :128].astype(F32)
+        seen = jnp.where(lane == blocks + h, marker, seen)
     bias = jnp.where(seen > 0.5, 0.0, -1e30).astype(BF16)
     bias = jnp.concatenate(
         [jnp.broadcast_to(bias[b : b + 1, :], (BLOCK, 128)) for b in range(blocks)], 0
@@ -172,20 +176,34 @@
         copy.wait()
     state = nodes_ref[...].astype(F32) + dot(jnp.concatenate(attended, 1), w_out_ref[...])
     state = state.astype(BF16)
-    state_ref[...] = state
+    nodes_ref[...] = state
+    out = pltpu.make_async_copy(nodes_ref, state_hbm, sent)
+    out.start()
     table_ref[...] = dot(state, w_target_ref[...]).astype(BF16)
-
-
-def answer(table_hbm, request_ref, answer_ref, table_ref, signals):
-    (copy,) = fetch((table_hbm,), (table_ref,), signals)
+    out.wait()
+
+
+def answer(request_ref, table_ref, answer_hbm, answer_ref, sent):
     bricks = request_ref.shape[0]
     capacity = answer_ref.shape[0] // bricks
     columns = jnp.transpose(request_ref[...])
     lanes = iota((capacity, table_ref.shape[0]), 1)
-    hot = [ones_where(columns[:capacity, b : b + 1] == lanes) for b in range(bricks)]
-    hot = jnp.concatenate(hot, 0)
-    copy.wait()
-    answer_ref[...] = dot(hot, table_ref[...]).astype(BF16)
+    copies = []
+    for first in range(0, bricks, bricks // 4):
+        hot = [
+            ones_where(columns[:capacity, b : b + 1] == lanes)
+            for b in range(first, first + bricks // 4)
+        ]
+        at = pl.ds(first * capacity, bricks // 4 * capacity)
+        answer_ref[at, :] = dot(jnp.concatenate(hot, 0), table_ref[...]).astype(BF16)
+        copies.append(
+            pltpu.make_async_copy(
+                answer_ref.at[at], answer_hbm.at[at], sent.at[first // (bricks // 4)]
+            )
+        )
+        copies[-1].start()
+    for copy in copies:
+        copy.wait()
 
 
 def own_part(
@@ -213,7 +231,7 @@
     return pltpu.with_memory_space_constraint(array, pltpu.HBM)
 
 
-def run(kernel, outs, *args, scratch=(), mib=16, far=0):
+def run(kernel, outs, *args, scratch=(), mib=16, far=0, far_outs=0):
     space = pl.BlockSpec(memory_space=pltpu.VMEM)
     left = pl.BlockSpec(memory_space=FAR)
     args = [away(arg) for arg in args[:far]] + list(args[far:])
@@ -221,7 +239,7 @@
         kernel,
         out_shape=tuple(outs),
         in_specs=[left] * far + [space] * (len(args) - far),
-        out_specs=(space,) * len(outs),
+        out_specs=(left,) * far_outs + (space,) * (len(outs) - far_outs),
         scratch_shapes=scratch,
         compiler_params=pltpu.CompilerParams(vmem_limit_bytes=mib * 1024 * 1024),
     )(*args)
@@ -305,32 +323,38 @@
     keys = rows + len(halo) * border_count
     node_state, table = run(
         functools.partial(attend, pieces=len(halo)),
-        (shape((rows, width), BF16), shape((rows, hidden), BF16)),
+        (shape((rows, width), BF16), pltpu.VMEM((rows, hidden), BF16)),
         w_attn_out,
         w_target,
-        nodes_near,
+        nodes,
         gain,
         mask,
         w_near,
         q,
         kv,
         *[near(piece) for piece in halo],
-        far=2,
+        far=3,
         mib=40,
         scratch=[
             pltpu.VMEM((width, width), BF16),
             pltpu.VMEM((width, hidden), BF16),
+            pltpu.VMEM((rows, width), BF16),
             pltpu.VMEM((2 * keys, 2 * PAIR), BF16),
-            pltpu.SemaphoreType.DMA((2,)),
+            pltpu.SemaphoreType.DMA((3,)),
+            pltpu.SemaphoreType.DMA,
         ],
+        far_outs=1,
     )
     (answers,) = run(
         answer,
         (shape((bricks * capacity, hidden), BF16),),
+        near(asked),
         table,
-        near(asked),
-        far=1,
-        scratch=[pltpu.VMEM((rows, hidden), BF16), pltpu.SemaphoreType.DMA((1,))],
+        scratch=[
+            pltpu.VMEM((bricks * capacity, hidden), BF16),
+            pltpu.SemaphoreType.DMA((4,)),
+        ],
+        far_outs=1,
     )
     answers = lax.all_to_all(
         answers.reshape(bricks, capacity, hidden),
@@ -341,7 +365,7 @@
     ).reshape(bricks * capacity, hidden)
     (part,) = run(
         own_part,
-        (shape((edges, hidden), F32),),
+        (pltpu.VMEM((edges, hidden), F32),),
         edge_source.reshape(edges // 128, 128),
         node_state,
         w_source,

time: 71 us -> 68.7 us (0.968)
  Pallas kernels: 28.4 us -> 27.2 us
  local copies, waits for them, and re-layouts: 2.03 us -> 1.07 us
    pallas_call x6, Pallas kernels: 28.4 us -> 27.2 us  [run(): pl.pallas_call(kernel, out_shape=tuple(outs), in_specs=[left] * far + [sp...]
    unnamed x14 -> x12, local copies, waits for them, and re-layouts: 2.03 us -> 1.07 us
  transfers between devices with their start and end apart: 5 -> 5, of which waited for: 1 -> 1; matrix products, arithmetic and copies ran while one was open for 0% -> 0% of each run, Pallas kernels for 29% -> 30%
where the time goes in v7:
time: 68.7 us; the launch traced here: 68.4 us
  Pallas kernels  27.2 us (40%)
  waiting for transfers between devices  22.4 us (33%)
  starting transfers between devices  16.9 us (25%)
  local copies, waits for them, and re-layouts  1.07 us (2%)
  between operations  0.79 us (1%)
    pallas_call x6, Pallas kernels, run(): pl.pallas_call(kernel, out_shape=tuple(outs), in_specs=[left] * far + [sp...  27.2 us
    all_to_all x1, waiting for transfers between devices, local(): lax.all_to_all(answers.reshape(bricks, capacity, hidden), ('gy', 'gz'), s...  22.4 us
    all_to_all x1, starting transfers between devices, local(): lax.all_to_all(request, ('gy', 'gz'), split_axis=0, concat_axis=0, tiled=...  6.54 us
    all_to_all x1, starting transfers between devices, local(): lax.all_to_all(answers.reshape(bricks, capacity, hidden), ('gy', 'gz'), s...  6.16 us
    ppermute x3, starting transfers between devices, neighbours(): return [lax.ppermute(block, axis, swaps) for axis, swaps in reversed(steps)]  4.23 us
  transfers between devices with their start and end apart: 5, of which 1 were waited for; matrix products, arithmetic and copies ran while one was open for 0% of the time, Pallas kernels for 30%

profile of v7, /device:TPU:9, one launch (start us, length us, event | category | flops | bytes accessed | tf_op | source)
XLA Modules:
  0.0 68.4 jit_solution(12786969193281187727)
XLA Ops:
  0.6 2.5 %shard_map.149 = (bf16[144,512]{1,0:T(8,128)(2,1)S(1)}, s32[16,128]{1,0:T(8,128)}, s32[4,128]{1,0:T(4,128)S(1)}, bf16[1024,512]{1,0:T(8,128)(2,1)S(1)}, f32[1,51...) custom-call(s32[1,128]{1,0:T(1,128)} %bitcast.21, s32[1,512]{1,0:T(1,128)} %bitcast.17, ...), custom_call_target="tpu_custom_call" | custom-call | tf_op jit(solution)/shard_map/pallas_call | solution.py:238
  3.1 1.3 %collective-permute-start.2 = (bf16[144,512]{1,0:T(8,128)(2,1)S(1)}, bf16[144,512]{1,0:T(8,128)(2,1)S(1)}, u32[]{:S(2)}, u32[]{:S(2)}) collective-permute-start(bf16[144,512]{1,0:T(8,128)(2,1)S(1)} %get-tuple-element.19), channel_id=1, source_target_pairs={{0,2},{2,0},{4,6},{6,4},{8,10},{10,8},{12,14},{14,12},{1,3},{3,1},... | collective-permute-start | bytes 442376 | tf_op jit(solution)/shard_map/ppermute | solution.py:261
  4.4 1.9 %collective-permute-start.1 = (bf16[144,512]{1,0:T(8,128)(2,1)S(1)}, bf16[144,512]{1,0:T(8,128)(2,1)S(1)}, u32[]{:S(2)}, u32[]{:S(2)}) collective-permute-start(bf16[144,512]{1,0:T(8,128)(2,1)S(1)} %get-tuple-element.19), channel_id=1, source_target_pairs={{2,4},{4,2},{6,8},{8,6},{10,12},{12,10},{3,5},{5,3},{7,9},{9,7},{1... | collective-permute-start | bytes 442376 | tf_op jit(solution)/shard_map/ppermute | solution.py:261
  6.3 1.0 %collective-permute-start = (bf16[144,512]{1,0:T(8,128)(2,1)S(1)}, bf16[144,512]{1,0:T(8,128)(2,1)S(1)}, u32[]{:S(2)}, u32[]{:S(2)}) collective-permute-start(bf16[144,512]{1,0:T(8,128)(2,1)S(1)} %get-tuple-element.19), channel_id=1, source_target_pairs={{0,1},{1,0},{2,3},{3,2},{4,5},{5,4},{6,7},{7,6},{8,9},{9,8},{10,11... | collective-permute-start | bytes 442376 | tf_op jit(solution)/shard_map/ppermute | solution.py:261
  7.3 6.5 %all-to-all-start = ((s32[16,1,128]{2,1,0:T(1,128)}), s32[16,1,128]{2,1,0:T(1,128)S(1)}, u32[]{:S(2)}, u32[]{:S(2)}) async-start(s32[16,1,128]{2,1,0:T(1,128)} %bitcast.5), calls=%async_computation | async-start | bytes 16384 | tf_op jit(solution)/shard_map/all_to_all | solution.py:313
  13.9 1.9 %shard_map.150 = (bf16[1024,512]{1,0:T(8,128)(2,1)S(1)}, bf16[1024,1024]{1,0:T(8,128)(2,1)S(1)}) custom-call(bf16[1024,512]{1,0:T(8,128)(2,1)S(1)} %get-tuple-element.16.nodes_ref, f32[1,512]{1,0:T(1,128)S(1)} %get-tuple-element.13.gain_ref.refs_3_, bf16[512,1536]{1,0:T(8,128)(2,1)S(1)} %get-tuple-element.15.w_ref.refs_5_), custom_call_target="tpu_custom_call" | custom-call | tf_op jit(solution)/shard_map/pallas_call | solution.py:238
  15.8 0.0 collective-permute-done.2.refs_10_
  15.8 0.0 collective-permute-done.1.refs_9_
  15.8 0.0 collective-permute-done.refs_8_
  15.8 17.5 %shard_map.151 = (bf16[1024,512]{1,0:T(8,128)(2,1)}, bf16[1024,512]{1,0:T(8,128)(2,1)S(1)}) custom-call(bf16[512,512]{1,0:T(8,128)(2,1)} %refs_0_.1, bf16[512,512]{1,0:T(8,128)(2,1)} %refs_1_.1, bf16[1024,512]{1,0:T(8,128)(2,1)} %refs_2_.1, f32[1,512]{1,0:T(1,128)S(1)} %get-tuple-element.13.gain_ref.refs_3_, s32[8,8]{1,0:T(8,128)S(1)} %get-tuple-element.14.refs_4_, ...), custom_call_target="tpu_custom_call" | custom-call | tf_op jit(solution)/shard_map/pallas_call | solution.py:238
  33.3 0.0 all-to-all-done
  33.3 2.2 %shard_map.152 = bf16[1024,512]{1,0:T(8,128)(2,1)} custom-call(s32[16,128]{1,0:T(8,128)S(1)} %bitcast.14, bf16[1024,512]{1,0:T(8,128)(2,1)S(1)} %get-tuple-element.23.table_ref), custom_call_target="tpu_custom_call" | custom-call | tf_op jit(solution)/shard_map/pallas_call | solution.py:238
  35.5 0.0 copy-start
  35.5 0.0 copy-start.2
  35.5 0.0 copy-start.3
  35.5 0.0 copy-start.4
  35.5 6.2 %all-to-all-start.1 = ((bf16[16,64,512]{2,1,0:T(8,128)(2,1)}), bf16[16,64,512]{2,1,0:T(8,128)(2,1)S(1)}, u32[]{:S(2)}, u32[]{:S(2)}) async-start(bf16[16,64,512]{2,1,0:T(8,128)(2,1)} %bitcast.7), calls=%async_computation.1 | async-start | bytes 2097152 | tf_op jit(solution)/shard_map/all_to_all | solution.py:359
  41.7 0.0 copy-start.5
  41.7 0.0 copy-done
  41.7 0.0 copy-done.2
  41.7 0.0 copy-done.3
  41.7 0.0 copy-done.4
  41.7 0.0 copy-start.1
  41.8 1.0 %copy-done.1 = bf16[512,512]{1,0:T(8,128)(2,1)S(1)} copy-done((bf16[512,512]{1,0:T(8,128)(2,1)S(1)}, bf16[512,512]{1,0:T(8,128)(2,1)}, u32[]{:S(2)}) %copy-start.1) | copy-done | bytes 524312
  42.8 1.3 %shard_map.153.part_ref = f32[512,512]{1,0:T(8,128)S(1)} custom-call(s32[4,128]{1,0:T(4,128)S(1)} %bitcast.15, bf16[1024,512]{1,0:T(8,128)(2,1)S(1)} %copy-done, bf16[512,512]{1,0:T(8,128)(2,1)S(1)} %copy-done.1, bf16[512,128]{1,0:T(8,128)(2,1)S(1)} %copy-done.2, bf16[128,512]{1,0:T(8,128)(2,1)S(1)} %copy-done.3), custom_call_target="tpu_custom_call" | custom-call | tf_op jit(solution)/shard_map/pallas_call | solution.py:238
  44.1 22.4 %all-to-all-done.1 = bf16[16,64,512]{2,1,0:T(8,128)(2,1)S(1)} async-done(((bf16[16,64,512]{2,1,0:T(8,128)(2,1)}), bf16[16,64,512]{2,1,0:T(8,128)(2,1)S(1)}, u32[]{:S(2)}, u32[]{:S(2)}) %all-to-all-start.1) | async-done | bytes 1048608 | tf_op jit(solution)/shard_map/all_to_all | solution.py:359
  66.5 0.0 copy-done.5
  66.5 1.8 %shard_map.154 = f32[1,512]{1,0:T(1,128)} custom-call(s32[4,128]{1,0:T(4,128)S(1)} %get-tuple-element.21.place_ref, bf16[1024,512]{1,0:T(8,128)(2,1)S(1)} %bitcast.13, f32[512,512]{1,0:T(8,128)S(1)} %shard_map.153.part_ref, f32[1,512]{1,0:T(1,128)S(1)} %bitcast.16), custom_call_target="tpu_custom_call" | custom-call | tf_op jit(solution)/shard_map/pallas_call | solution.py:238
Async XLA Ops:
  3.1 12.7 %collective-permute-start.2 = (bf16[144,512]{1,0:T(8,128)(2,1)S(1)}, bf16[144,512]{1,0:T(8,128)(2,1)S(1)}, u32[]{:S(2)}, u32[]{:S(2)}) collective-permute-start(bf16[144,512]{1,0:T(8,128)(2,1)S(1)} %get-tuple-element.19), channel_id=1, source_target_pairs={{0,2},{2,0},{4,6},{6,4},{8,10},{10,8},{12,14},{14,12},{1,3},{3,1},... | collective-permute-start | bytes 442376 | tf_op jit(solution)/shard_map/ppermute | solution.py:261
  4.4 11.4 %collective-permute-start.1 = (bf16[144,512]{1,0:T(8,128)(2,1)S(1)}, bf16[144,512]{1,0:T(8,128)(2,1)S(1)}, u32[]{:S(2)}, u32[]{:S(2)}) collective-permute-start(bf16[144,512]{1,0:T(8,128)(2,1)S(1)} %get-tuple-element.19), channel_id=1, source_target_pairs={{2,4},{4,2},{6,8},{8,6},{10,12},{12,10},{3,5},{5,3},{7,9},{9,7},{1... | collective-permute-start | bytes 442376 | tf_op jit(solution)/shard_map/ppermute | solution.py:261
  6.3 9.5 %collective-permute-start = (bf16[144,512]{1,0:T(8,128)(2,1)S(1)}, bf16[144,512]{1,0:T(8,128)(2,1)S(1)}, u32[]{:S(2)}, u32[]{:S(2)}) collective-permute-start(bf16[144,512]{1,0:T(8,128)(2,1)S(1)} %get-tuple-element.19), channel_id=1, source_target_pairs={{0,1},{1,0},{2,3},{3,2},{4,5},{5,4},{6,7},{7,6},{8,9},{9,8},{10,11... | collective-permute-start | bytes 442376 | tf_op jit(solution)/shard_map/ppermute | solution.py:261
  7.3 25.9 %all-to-all-start = ((s32[16,1,128]{2,1,0:T(1,128)}), s32[16,1,128]{2,1,0:T(1,128)S(1)}, u32[]{:S(2)}, u32[]{:S(2)}) async-start(s32[16,1,128]{2,1,0:T(1,128)} %bitcast.5), calls=%async_computation | async-start | bytes 16384 | tf_op jit(solution)/shard_map/all_to_all | solution.py:313
  35.5 6.2 %copy-start = (bf16[1024,512]{1,0:T(8,128)(2,1)S(1)}, bf16[1024,512]{1,0:T(8,128)(2,1)}, u32[]{:S(2)}) copy-start(bf16[1024,512]{1,0:T(8,128)(2,1)} %get-tuple-element.11.state_ref) | copy-start | bytes 3145732
  35.5 6.2 %copy-start.2 = (bf16[512,128]{1,0:T(8,128)(2,1)S(1)}, bf16[512,128]{1,0:T(8,128)(2,1)}, u32[]{:S(2)}) copy-start(bf16[512,128]{1,0:T(8,128)(2,1)} %contact_ref.1) | copy-start | bytes 393220
  35.5 6.2 %copy-start.3 = (bf16[128,512]{1,0:T(8,128)(2,1)S(1)}, bf16[128,512]{1,0:T(8,128)(2,1)}, u32[]{:S(2)}) copy-start(bf16[128,512]{1,0:T(8,128)(2,1)} %w_ref.1) | copy-start | bytes 393220
  35.5 6.2 %copy-start.4 = (s32[512]{0:T(512)S(1)}, s32[512]{0:T(512)}, u32[]{:S(2)}) copy-start(s32[512]{0:T(512)} %param.18) | copy-start | bytes 6148
  35.5 31.0 %all-to-all-start.1 = ((bf16[16,64,512]{2,1,0:T(8,128)(2,1)}), bf16[16,64,512]{2,1,0:T(8,128)(2,1)S(1)}, u32[]{:S(2)}, u32[]{:S(2)}) async-start(bf16[16,64,512]{2,1,0:T(8,128)(2,1)} %bitcast.7), calls=%async_computation.1 | async-start | bytes 2097152 | tf_op jit(solution)/shard_map/all_to_all | solution.py:359
  41.7 24.8 %copy-start.5 = (f32[512]{0:T(512)S(1)}, f32[512]{0:T(512)}, u32[]{:S(2)}) copy-start(f32[512]{0:T(512)} %param.27) | copy-start | bytes 6148
  41.7 1.0 %copy-start.1 = (bf16[512,512]{1,0:T(8,128)(2,1)S(1)}, bf16[512,512]{1,0:T(8,128)(2,1)}, u32[]{:S(2)}) copy-start(bf16[512,512]{1,0:T(8,128)(2,1)} %w_source_ref.1) | copy-start | bytes 1572868

commit v8 on v7

--- a/solution.py
+++ b/solution.py
@@ -111,20 +111,20 @@
 def attend(*refs, pieces):
     w_out_hbm, w_target_hbm, nodes_hbm, gain_ref, mask_ref, w_ref, q_ref, kv_ref = refs[:8]
     halo_refs = refs[8 : 8 + pieces]
-    state_hbm, table_ref, w_out_ref, w_target_ref, nodes_ref, v_ref, signals, sent = refs[
-        8 + pieces :
-    ]
+    state_hbm, table_ref, w_out_ref, w_target_ref, nodes_ref = refs[8 + pieces : 13 + pieces]
+    mixed_ref, v_ref, signals, sent = refs[13 + pieces :]
     copies = fetch(
         (w_out_hbm, w_target_hbm, nodes_hbm), (w_out_ref, w_target_ref, nodes_ref), signals
     )
     rows, width = q_ref.shape
     blocks = rows // BLOCK
-    keys = v_ref.shape[0] // 2
+    keys = v_ref.shape[1] // 2
     border = (keys - rows) // pieces
     halo_nodes = jnp.concatenate([ref[:border, :] for ref in halo_refs], 0)
     halo = dot(normed_rows(halo_nodes, gain_ref[...]), w_ref[:, width:]).astype(BF16)
     low_keys = iota((keys, PAIR), 1) < HEAD_DIM
-    low = iota((rows, PAIR), 1) < HEAD_DIM
+    span = rows // 2
+    low = iota((span, PAIR), 1) < HEAD_DIM
 
     lane = iota((blocks, 128), 1)
     row = iota((blocks, 128), 0)
@@ -143,24 +143,33 @@
         [ones_where(own == iota(own.shape, 1)), ones_where(far == iota(far.shape, 1))], 0
     )
     key_block = jnp.concatenate([key_block, key_block], 0)
-    v_ref[:keys, PAIR:] = jnp.zeros((keys, PAIR), BF16)
-    v_ref[keys:, :PAIR] = jnp.zeros((keys, PAIR), BF16)
-
-    attended = []
-    for pair in range(width // PAIR):
+    for buffer in range(2):
+        v_ref[buffer, :keys, PAIR:] = jnp.zeros((keys, PAIR), BF16)
+        v_ref[buffer, keys:, :PAIR] = jnp.zeros((keys, PAIR), BF16)
+
+    def scores_of(pair, part):
         at = slice(pair * PAIR, (pair + 1) * PAIR)
-        v_at = slice(width + pair * PAIR, width + (pair + 1) * PAIR)
-        values = jnp.concatenate([kv_ref[:, v_at], halo[:, v_at]], 0)
-        one = jnp.ones_like(values)
-        v_ref[:keys, :PAIR] = jnp.where(low_keys, values, one)
-        v_ref[keys:, PAIR:] = jnp.where(low_keys, one, values)
+        span_at = slice(part * span, (part + 1) * span)
         k_pair = jnp.concatenate([kv_ref[:, at], halo[:, at]], 0)
         zero = jnp.zeros_like(k_pair)
         k_pair = jnp.concatenate(
             [jnp.where(low_keys, k_pair, zero), jnp.where(low_keys, zero, k_pair)], 0
         )
         k_pair = jnp.concatenate([k_pair, key_block], 1)
-        scores = dot_nt(jnp.concatenate([q_ref[:, at], bias], 1), k_pair)
+        return dot_nt(jnp.concatenate([q_ref[span_at, at], bias[span_at]], 1), k_pair)
+
+    units = [(pair, part) for pair in range(width // PAIR) for part in range(2)]
+    following = scores_of(*units[0])
+    for step, (pair, part) in enumerate(units):
+        scores = following
+        if part == 0:
+            v_at = slice(width + pair * PAIR, width + (pair + 1) * PAIR)
+            values = jnp.concatenate([kv_ref[:, v_at], halo[:, v_at]], 0)
+            one = jnp.ones_like(values)
+            v_ref[pair % 2, :keys, :PAIR] = jnp.where(low_keys, values, one)
+            v_ref[pair % 2, keys:, PAIR:] = jnp.where(low_keys, one, values)
+        if step + 1 < len(units):
+            following = scores_of(*units[step + 1])
         weights = []
         for half in (scores[:, :keys], scores[:, keys:]):
             fold = half[:, :128]
@@ -168,13 +177,15 @@
                 fold = jnp.maximum(fold, half[:, c : c + 128])
             top = jnp.max(fold, axis=1, keepdims=True)
             weights.append(jnp.exp2((half - top).astype(BF16)))
-        mixed = dot(jnp.concatenate(weights, 1), v_ref[...])
+        mixed = dot(jnp.concatenate(weights, 1), v_ref[pair % 2])
         even, odd = mixed[:, :PAIR], mixed[:, PAIR:]
         total = pltpu.roll(jnp.where(low, odd, even), HEAD_DIM, 1)
-        attended.append((jnp.where(low, even, odd) / total).astype(BF16))
+        mixed_ref[part * span : (part + 1) * span, pair * PAIR : (pair + 1) * PAIR] = (
+            jnp.where(low, even, odd) / total
+        ).astype(BF16)
     for copy in copies:
         copy.wait()
-    state = nodes_ref[...].astype(F32) + dot(jnp.concatenate(attended, 1), w_out_ref[...])
+    state = nodes_ref[...].astype(F32) + dot(mixed_ref[...], w_out_ref[...])
     state = state.astype(BF16)
     nodes_ref[...] = state
     out = pltpu.make_async_copy(nodes_ref, state_hbm, sent)
@@ -339,7 +350,8 @@
             pltpu.VMEM((width, width), BF16),
             pltpu.VMEM((width, hidden), BF16),
             pltpu.VMEM((rows, width), BF16),
-            pltpu.VMEM((2 * keys, 2 * PAIR), BF16),
+            pltpu.VMEM((rows, width), BF16),
+            pltpu.VMEM((2, 2 * keys, 2 * PAIR), BF16),
             pltpu.SemaphoreType.DMA((3,)),
             pltpu.SemaphoreType.DMA,
         ],

time: 68.7 us -> 67.5 us (0.983)
  Pallas kernels: 27.2 us -> 25.9 us
    pallas_call x6, Pallas kernels: 27.2 us -> 25.9 us  [run(): pl.pallas_call(kernel, out_shape=tuple(outs), in_specs=[left] * far + [sp...]
  transfers between devices with their start and end apart: 5 -> 5, of which waited for: 1 -> 1; matrix products, arithmetic and copies ran while one was open for 0% -> 0% of each run, Pallas kernels for 30% -> 29%
where the time goes in v8:
time: 67.5 us; the launch traced here: 67.1 us
  Pallas kernels  25.9 us (38%)
  waiting for transfers between devices  22.4 us (33%)
  starting transfers between devices  16.9 us (25%)
  local copies, waits for them, and re-layouts  1.07 us (2%)
  between operations  0.79 us (1%)
    pallas_call x6, Pallas kernels, run(): pl.pallas_call(kernel, out_shape=tuple(outs), in_specs=[left] * far + [sp...  25.9 us
    all_to_all x1, waiting for transfers between devices, local(): lax.all_to_all(answers.reshape(bricks, capacity, hidden), ('gy', 'gz'), s...  22.4 us
    all_to_all x1, starting transfers between devices, local(): lax.all_to_all(request, ('gy', 'gz'), split_axis=0, concat_axis=0, tiled=...  6.54 us
    all_to_all x1, starting transfers between devices, local(): lax.all_to_all(answers.reshape(bricks, capacity, hidden), ('gy', 'gz'), s...  6.16 us
    ppermute x3, starting transfers between devices, neighbours(): return [lax.ppermute(block, axis, swaps) for axis, swaps in reversed(steps)]  4.23 us
  transfers between devices with their start and end apart: 5, of which 1 were waited for; matrix products, arithmetic and copies ran while one was open for 0% of the time, Pallas kernels for 29%

profile of v8, /device:TPU:9, one launch (start us, length us, event | category | flops | bytes accessed | tf_op | source)
XLA Modules:
  0.0 67.1 jit_solution(3876295392186669567)
XLA Ops:
  0.6 2.5 %shard_map.149 = (bf16[144,512]{1,0:T(8,128)(2,1)S(1)}, s32[16,128]{1,0:T(8,128)}, s32[4,128]{1,0:T(4,128)S(1)}, bf16[1024,512]{1,0:T(8,128)(2,1)S(1)}, f32[1,51...) custom-call(s32[1,128]{1,0:T(1,128)} %bitcast.21, s32[1,512]{1,0:T(1,128)} %bitcast.17, ...), custom_call_target="tpu_custom_call" | custom-call | tf_op jit(solution)/shard_map/pallas_call | solution.py:249
  3.1 1.3 %collective-permute-start.2 = (bf16[144,512]{1,0:T(8,128)(2,1)S(1)}, bf16[144,512]{1,0:T(8,128)(2,1)S(1)}, u32[]{:S(2)}, u32[]{:S(2)}) collective-permute-start(bf16[144,512]{1,0:T(8,128)(2,1)S(1)} %get-tuple-element.19), channel_id=1, source_target_pairs={{0,2},{2,0},{4,6},{6,4},{8,10},{10,8},{12,14},{14,12},{1,3},{3,1},... | collective-permute-start | bytes 442376 | tf_op jit(solution)/shard_map/ppermute | solution.py:272
  4.4 1.9 %collective-permute-start.1 = (bf16[144,512]{1,0:T(8,128)(2,1)S(1)}, bf16[144,512]{1,0:T(8,128)(2,1)S(1)}, u32[]{:S(2)}, u32[]{:S(2)}) collective-permute-start(bf16[144,512]{1,0:T(8,128)(2,1)S(1)} %get-tuple-element.19), channel_id=1, source_target_pairs={{2,4},{4,2},{6,8},{8,6},{10,12},{12,10},{3,5},{5,3},{7,9},{9,7},{1... | collective-permute-start | bytes 442376 | tf_op jit(solution)/shard_map/ppermute | solution.py:272
  6.3 1.0 %collective-permute-start = (bf16[144,512]{1,0:T(8,128)(2,1)S(1)}, bf16[144,512]{1,0:T(8,128)(2,1)S(1)}, u32[]{:S(2)}, u32[]{:S(2)}) collective-permute-start(bf16[144,512]{1,0:T(8,128)(2,1)S(1)} %get-tuple-element.19), channel_id=1, source_target_pairs={{0,1},{1,0},{2,3},{3,2},{4,5},{5,4},{6,7},{7,6},{8,9},{9,8},{10,11... | collective-permute-start | bytes 442376 | tf_op jit(solution)/shard_map/ppermute | solution.py:272
  7.3 6.5 %all-to-all-start = ((s32[16,1,128]{2,1,0:T(1,128)}), s32[16,1,128]{2,1,0:T(1,128)S(1)}, u32[]{:S(2)}, u32[]{:S(2)}) async-start(s32[16,1,128]{2,1,0:T(1,128)} %bitcast.5), calls=%async_computation | async-start | bytes 16384 | tf_op jit(solution)/shard_map/all_to_all | solution.py:324
  13.9 1.9 %shard_map.150 = (bf16[1024,512]{1,0:T(8,128)(2,1)S(1)}, bf16[1024,1024]{1,0:T(8,128)(2,1)S(1)}) custom-call(bf16[1024,512]{1,0:T(8,128)(2,1)S(1)} %get-tuple-element.16.nodes_ref, f32[1,512]{1,0:T(1,128)S(1)} %get-tuple-element.13.gain_ref.refs_3_, bf16[512,1536]{1,0:T(8,128)(2,1)S(1)} %get-tuple-element.15.w_ref.refs_5_), custom_call_target="tpu_custom_call" | custom-call | tf_op jit(solution)/shard_map/pallas_call | solution.py:249
  15.8 0.0 collective-permute-done.2.refs_10_
  15.8 0.0 collective-permute-done.1.refs_9_
  15.8 0.0 collective-permute-done.refs_8_
  15.8 16.2 %shard_map.151 = (bf16[1024,512]{1,0:T(8,128)(2,1)}, bf16[1024,512]{1,0:T(8,128)(2,1)S(1)}) custom-call(bf16[512,512]{1,0:T(8,128)(2,1)} %refs_0_.1, bf16[512,512]{1,0:T(8,128)(2,1)} %refs_1_.1, bf16[1024,512]{1,0:T(8,128)(2,1)} %refs_2_.1, f32[1,512]{1,0:T(1,128)S(1)} %get-tuple-element.13.gain_ref.refs_3_, s32[8,8]{1,0:T(8,128)S(1)} %get-tuple-element.14.refs_4_, ...), custom_call_target="tpu_custom_call" | custom-call | tf_op jit(solution)/shard_map/pallas_call | solution.py:249
  32.0 0.0 all-to-all-done
  32.0 2.2 %shard_map.152 = bf16[1024,512]{1,0:T(8,128)(2,1)} custom-call(s32[16,128]{1,0:T(8,128)S(1)} %bitcast.14, bf16[1024,512]{1,0:T(8,128)(2,1)S(1)} %get-tuple-element.23.table_ref), custom_call_target="tpu_custom_call" | custom-call | tf_op jit(solution)/shard_map/pallas_call | solution.py:249
  34.2 0.0 copy-start
  34.2 0.0 copy-start.2
  34.2 0.0 copy-start.3
  34.3 0.0 copy-start.4
  34.3 6.2 %all-to-all-start.1 = ((bf16[16,64,512]{2,1,0:T(8,128)(2,1)}), bf16[16,64,512]{2,1,0:T(8,128)(2,1)S(1)}, u32[]{:S(2)}, u32[]{:S(2)}) async-start(bf16[16,64,512]{2,1,0:T(8,128)(2,1)} %bitcast.7), calls=%async_computation.1 | async-start | bytes 2097152 | tf_op jit(solution)/shard_map/all_to_all | solution.py:371
  40.4 0.0 copy-start.5
  40.4 0.0 copy-done
  40.5 0.0 copy-done.2
  40.5 0.0 copy-done.3
  40.5 0.0 copy-done.4
  40.5 0.0 copy-start.1
  40.5 1.0 %copy-done.1 = bf16[512,512]{1,0:T(8,128)(2,1)S(1)} copy-done((bf16[512,512]{1,0:T(8,128)(2,1)S(1)}, bf16[512,512]{1,0:T(8,128)(2,1)}, u32[]{:S(2)}) %copy-start.1) | copy-done | bytes 524312
  41.5 1.3 %shard_map.153.part_ref = f32[512,512]{1,0:T(8,128)S(1)} custom-call(s32[4,128]{1,0:T(4,128)S(1)} %bitcast.15, bf16[1024,512]{1,0:T(8,128)(2,1)S(1)} %copy-done, bf16[512,512]{1,0:T(8,128)(2,1)S(1)} %copy-done.1, bf16[512,128]{1,0:T(8,128)(2,1)S(1)} %copy-done.2, bf16[128,512]{1,0:T(8,128)(2,1)S(1)} %copy-done.3), custom_call_target="tpu_custom_call" | custom-call | tf_op jit(solution)/shard_map/pallas_call | solution.py:249
  42.9 22.4 %all-to-all-done.1 = bf16[16,64,512]{2,1,0:T(8,128)(2,1)S(1)} async-done(((bf16[16,64,512]{2,1,0:T(8,128)(2,1)}), bf16[16,64,512]{2,1,0:T(8,128)(2,1)S(1)}, u32[]{:S(2)}, u32[]{:S(2)}) %all-to-all-start.1) | async-done | bytes 1048608 | tf_op jit(solution)/shard_map/all_to_all | solution.py:371
  65.3 0.0 copy-done.5
  65.3 1.8 %shard_map.154 = f32[1,512]{1,0:T(1,128)} custom-call(s32[4,128]{1,0:T(4,128)S(1)} %get-tuple-element.21.place_ref, bf16[1024,512]{1,0:T(8,128)(2,1)S(1)} %bitcast.13, f32[512,512]{1,0:T(8,128)S(1)} %shard_map.153.part_ref, f32[1,512]{1,0:T(1,128)S(1)} %bitcast.16), custom_call_target="tpu_custom_call" | custom-call | tf_op jit(solution)/shard_map/pallas_call | solution.py:249
Async XLA Ops:
  3.1 12.7 %collective-permute-start.2 = (bf16[144,512]{1,0:T(8,128)(2,1)S(1)}, bf16[144,512]{1,0:T(8,128)(2,1)S(1)}, u32[]{:S(2)}, u32[]{:S(2)}) collective-permute-start(bf16[144,512]{1,0:T(8,128)(2,1)S(1)} %get-tuple-element.19), channel_id=1, source_target_pairs={{0,2},{2,0},{4,6},{6,4},{8,10},{10,8},{12,14},{14,12},{1,3},{3,1},... | collective-permute-start | bytes 442376 | tf_op jit(solution)/shard_map/ppermute | solution.py:272
  4.4 11.4 %collective-permute-start.1 = (bf16[144,512]{1,0:T(8,128)(2,1)S(1)}, bf16[144,512]{1,0:T(8,128)(2,1)S(1)}, u32[]{:S(2)}, u32[]{:S(2)}) collective-permute-start(bf16[144,512]{1,0:T(8,128)(2,1)S(1)} %get-tuple-element.19), channel_id=1, source_target_pairs={{2,4},{4,2},{6,8},{8,6},{10,12},{12,10},{3,5},{5,3},{7,9},{9,7},{1... | collective-permute-start | bytes 442376 | tf_op jit(solution)/shard_map/ppermute | solution.py:272
  6.3 9.5 %collective-permute-start = (bf16[144,512]{1,0:T(8,128)(2,1)S(1)}, bf16[144,512]{1,0:T(8,128)(2,1)S(1)}, u32[]{:S(2)}, u32[]{:S(2)}) collective-permute-start(bf16[144,512]{1,0:T(8,128)(2,1)S(1)} %get-tuple-element.19), channel_id=1, source_target_pairs={{0,1},{1,0},{2,3},{3,2},{4,5},{5,4},{6,7},{7,6},{8,9},{9,8},{10,11... | collective-permute-start | bytes 442376 | tf_op jit(solution)/shard_map/ppermute | solution.py:272
  7.3 24.7 %all-to-all-start = ((s32[16,1,128]{2,1,0:T(1,128)}), s32[16,1,128]{2,1,0:T(1,128)S(1)}, u32[]{:S(2)}, u32[]{:S(2)}) async-start(s32[16,1,128]{2,1,0:T(1,128)} %bitcast.5), calls=%async_computation | async-start | bytes 16384 | tf_op jit(solution)/shard_map/all_to_all | solution.py:324
  34.2 6.2 %copy-start = (bf16[1024,512]{1,0:T(8,128)(2,1)S(1)}, bf16[1024,512]{1,0:T(8,128)(2,1)}, u32[]{:S(2)}) copy-start(bf16[1024,512]{1,0:T(8,128)(2,1)} %get-tuple-element.11.state_ref) | copy-start | bytes 3145732
  34.2 6.2 %copy-start.2 = (bf16[512,128]{1,0:T(8,128)(2,1)S(1)}, bf16[512,128]{1,0:T(8,128)(2,1)}, u32[]{:S(2)}) copy-start(bf16[512,128]{1,0:T(8,128)(2,1)} %contact_ref.1) | copy-start | bytes 393220
  34.2 6.2 %copy-start.3 = (bf16[128,512]{1,0:T(8,128)(2,1)S(1)}, bf16[128,512]{1,0:T(8,128)(2,1)}, u32[]{:S(2)}) copy-start(bf16[128,512]{1,0:T(8,128)(2,1)} %w_ref.1) | copy-start | bytes 393220
  34.3 6.2 %copy-start.4 = (s32[512]{0:T(512)S(1)}, s32[512]{0:T(512)}, u32[]{:S(2)}) copy-start(s32[512]{0:T(512)} %param.18) | copy-start | bytes 6148
  34.3 31.0 %all-to-all-start.1 = ((bf16[16,64,512]{2,1,0:T(8,128)(2,1)}), bf16[16,64,512]{2,1,0:T(8,128)(2,1)S(1)}, u32[]{:S(2)}, u32[]{:S(2)}) async-start(bf16[16,64,512]{2,1,0:T(8,128)(2,1)} %bitcast.7), calls=%async_computation.1 | async-start | bytes 2097152 | tf_op jit(solution)/shard_map/all_to_all | solution.py:371
  40.4 24.8 %copy-start.5 = (f32[512]{0:T(512)S(1)}, f32[512]{0:T(512)}, u32[]{:S(2)}) copy-start(f32[512]{0:T(512)} %param.27) | copy-start | bytes 6148
  40.5 1.0 %copy-start.1 = (bf16[512,512]{1,0:T(8,128)(2,1)S(1)}, bf16[512,512]{1,0:T(8,128)(2,1)}, u32[]{:S(2)}) copy-start(bf16[512,512]{1,0:T(8,128)(2,1)} %w_source_ref.1) | copy-start | bytes 1572868

commit v9 on v8

--- a/solution.py
+++ b/solution.py
@@ -199,18 +199,15 @@
     capacity = answer_ref.shape[0] // bricks
     columns = jnp.transpose(request_ref[...])
     lanes = iota((capacity, table_ref.shape[0]), 1)
+    hot = [ones_where(columns[:capacity, b : b + 1] == lanes) for b in range(bricks)]
+    hot = jnp.concatenate(hot, 0)
+    half = table_ref.shape[1] // 2
     copies = []
-    for first in range(0, bricks, bricks // 4):
-        hot = [
-            ones_where(columns[:capacity, b : b + 1] == lanes)
-            for b in range(first, first + bricks // 4)
-        ]
-        at = pl.ds(first * capacity, bricks // 4 * capacity)
-        answer_ref[at, :] = dot(jnp.concatenate(hot, 0), table_ref[...]).astype(BF16)
+    for part in range(2):
+        at = pl.ds(part * half, half)
+        answer_ref[:, at] = dot(hot, table_ref[:, at]).astype(BF16)
         copies.append(
-            pltpu.make_async_copy(
-                answer_ref.at[at], answer_hbm.at[at], sent.at[first // (bricks // 4)]
-            )
+            pltpu.make_async_copy(answer_ref.at[:, at], answer_hbm.at[:, at], sent.at[part])
         )
         copies[-1].start()
     for copy in copies:
@@ -226,11 +223,15 @@
 
 
 def score(place_ref, answers_ref, part_ref, w_ref, out_ref):
-    pre = part_ref[...] + picked(place_ref[...], answers_ref[...])
-    weighted = jax.nn.gelu(pre) * w_ref[...]
-    folded = weighted[:, :128]
-    for at in range(128, weighted.shape[1], 128):
-        folded = folded + weighted[:, at : at + 128]
+    hot = hot_rows(place_ref[...], answers_ref.shape[0])
+    half = answers_ref.shape[1] // 2
+    folded = jnp.zeros((part_ref.shape[0], 128), F32)
+    found = [dot(hot, answers_ref[:, at : at + half]) for at in (0, half)]
+    for part in range(2):
+        at = slice(part * half, (part + 1) * half)
+        weighted = jax.nn.gelu(part_ref[:, at] + found[part]) * w_ref[:, at]
+        for c in range(0, half, 128):
+            folded = folded + weighted[:, c : c + 128]
     out_ref[...] = jnp.sum(jnp.transpose(folded), axis=0, keepdims=True)
 
 
@@ -364,7 +365,7 @@
         table,
         scratch=[
             pltpu.VMEM((bricks * capacity, hidden), BF16),
-            pltpu.SemaphoreType.DMA((4,)),
+            pltpu.SemaphoreType.DMA((2,)),
         ],
         far_outs=1,
     )

time: 67.5 us -> 67.7 us (level)
  no operation moved by 1% of the time
where the time goes in v9:
time: 67.7 us; the launch traced here: 67.3 us
  Pallas kernels  26.1 us (39%)
  waiting for transfers between devices  22.4 us (33%)
  starting transfers between devices  16.9 us (25%)
  local copies, waits for them, and re-layouts  1.07 us (2%)
  between operations  0.79 us (1%)
    pallas_call x6, Pallas kernels, run(): pl.pallas_call(kernel, out_shape=tuple(outs), in_specs=[left] * far + [sp...  26.1 us
    all_to_all x1, waiting for transfers between devices, local(): lax.all_to_all(answers.reshape(bricks, capacity, hidden), ('gy', 'gz'), s...  22.4 us
    all_to_all x1, starting transfers between devices, local(): lax.all_to_all(request, ('gy', 'gz'), split_axis=0, concat_axis=0, tiled=...  6.54 us
    all_to_all x1, starting transfers between devices, local(): lax.all_to_all(answers.reshape(bricks, capacity, hidden), ('gy', 'gz'), s...  6.16 us
    ppermute x3, starting transfers between devices, neighbours(): return [lax.ppermute(block, axis, swaps) for axis, swaps in reversed(steps)]  4.23 us
  transfers between devices with their start and end apart: 5, of which 1 were waited for; matrix products, arithmetic and copies ran while one was open for 0% of the time, Pallas kernels for 29%

profile of v9, /device:TPU:9, one launch (start us, length us, event | category | flops | bytes accessed | tf_op | source)
XLA Modules:
  0.0 67.3 jit_solution(5507578498143117029)
XLA Ops:
  0.6 2.5 %shard_map.149 = (bf16[144,512]{1,0:T(8,128)(2,1)S(1)}, s32[16,128]{1,0:T(8,128)}, s32[4,128]{1,0:T(4,128)S(1)}, bf16[1024,512]{1,0:T(8,128)(2,1)S(1)}, f32[1,51...) custom-call(s32[1,128]{1,0:T(1,128)} %bitcast.21, s32[1,512]{1,0:T(1,128)} %bitcast.17, ...), custom_call_target="tpu_custom_call" | custom-call | tf_op jit(solution)/shard_map/pallas_call | solution.py:250
  3.1 1.3 %collective-permute-start.2 = (bf16[144,512]{1,0:T(8,128)(2,1)S(1)}, bf16[144,512]{1,0:T(8,128)(2,1)S(1)}, u32[]{:S(2)}, u32[]{:S(2)}) collective-permute-start(bf16[144,512]{1,0:T(8,128)(2,1)S(1)} %get-tuple-element.19), channel_id=1, source_target_pairs={{0,2},{2,0},{4,6},{6,4},{8,10},{10,8},{12,14},{14,12},{1,3},{3,1},... | collective-permute-start | bytes 442376 | tf_op jit(solution)/shard_map/ppermute | solution.py:273
  4.4 1.9 %collective-permute-start.1 = (bf16[144,512]{1,0:T(8,128)(2,1)S(1)}, bf16[144,512]{1,0:T(8,128)(2,1)S(1)}, u32[]{:S(2)}, u32[]{:S(2)}) collective-permute-start(bf16[144,512]{1,0:T(8,128)(2,1)S(1)} %get-tuple-element.19), channel_id=1, source_target_pairs={{2,4},{4,2},{6,8},{8,6},{10,12},{12,10},{3,5},{5,3},{7,9},{9,7},{1... | collective-permute-start | bytes 442376 | tf_op jit(solution)/shard_map/ppermute | solution.py:273
  6.3 1.0 %collective-permute-start = (bf16[144,512]{1,0:T(8,128)(2,1)S(1)}, bf16[144,512]{1,0:T(8,128)(2,1)S(1)}, u32[]{:S(2)}, u32[]{:S(2)}) collective-permute-start(bf16[144,512]{1,0:T(8,128)(2,1)S(1)} %get-tuple-element.19), channel_id=1, source_target_pairs={{0,1},{1,0},{2,3},{3,2},{4,5},{5,4},{6,7},{7,6},{8,9},{9,8},{10,11... | collective-permute-start | bytes 442376 | tf_op jit(solution)/shard_map/ppermute | solution.py:273
  7.3 6.5 %all-to-all-start = ((s32[16,1,128]{2,1,0:T(1,128)}), s32[16,1,128]{2,1,0:T(1,128)S(1)}, u32[]{:S(2)}, u32[]{:S(2)}) async-start(s32[16,1,128]{2,1,0:T(1,128)} %bitcast.5), calls=%async_computation | async-start | bytes 16384 | tf_op jit(solution)/shard_map/all_to_all | solution.py:325
  13.9 1.9 %shard_map.150 = (bf16[1024,512]{1,0:T(8,128)(2,1)S(1)}, bf16[1024,1024]{1,0:T(8,128)(2,1)S(1)}) custom-call(bf16[1024,512]{1,0:T(8,128)(2,1)S(1)} %get-tuple-element.16.nodes_ref, f32[1,512]{1,0:T(1,128)S(1)} %get-tuple-element.13.gain_ref.refs_3_, bf16[512,1536]{1,0:T(8,128)(2,1)S(1)} %get-tuple-element.15.w_ref.refs_5_), custom_call_target="tpu_custom_call" | custom-call | tf_op jit(solution)/shard_map/pallas_call | solution.py:250
  15.8 0.0 collective-permute-done.2.refs_10_
  15.8 0.0 collective-permute-done.1.refs_9_
  15.8 0.0 collective-permute-done.refs_8_
  15.8 16.2 %shard_map.151 = (bf16[1024,512]{1,0:T(8,128)(2,1)}, bf16[1024,512]{1,0:T(8,128)(2,1)S(1)}) custom-call(bf16[512,512]{1,0:T(8,128)(2,1)} %refs_0_.1, bf16[512,512]{1,0:T(8,128)(2,1)} %refs_1_.1, bf16[1024,512]{1,0:T(8,128)(2,1)} %refs_2_.1, f32[1,512]{1,0:T(1,128)S(1)} %get-tuple-element.13.gain_ref.refs_3_, s32[8,8]{1,0:T(8,128)S(1)} %get-tuple-element.14.refs_4_, ...), custom_call_target="tpu_custom_call" | custom-call | tf_op jit(solution)/shard_map/pallas_call | solution.py:250
  32.0 0.0 all-to-all-done
  32.0 2.4 %shard_map.152 = bf16[1024,512]{1,0:T(8,128)(2,1)} custom-call(s32[16,128]{1,0:T(8,128)S(1)} %bitcast.14, bf16[1024,512]{1,0:T(8,128)(2,1)S(1)} %get-tuple-element.23.table_ref), custom_call_target="tpu_custom_call" | custom-call | tf_op jit(solution)/shard_map/pallas_call | solution.py:250
  34.4 0.0 copy-start
  34.4 0.0 copy-start.2
  34.4 0.0 copy-start.3
  34.5 0.0 copy-start.4
  34.5 6.2 %all-to-all-start.1 = ((bf16[16,64,512]{2,1,0:T(8,128)(2,1)}), bf16[16,64,512]{2,1,0:T(8,128)(2,1)S(1)}, u32[]{:S(2)}, u32[]{:S(2)}) async-start(bf16[16,64,512]{2,1,0:T(8,128)(2,1)} %bitcast.7), calls=%async_computation.1 | async-start | bytes 2097152 | tf_op jit(solution)/shard_map/all_to_all | solution.py:372
  40.6 0.0 copy-start.5
  40.6 0.0 copy-done
  40.7 0.0 copy-done.2
  40.7 0.0 copy-done.3
  40.7 0.0 copy-done.4
  40.7 0.0 copy-start.1
  40.7 1.0 %copy-done.1 = bf16[512,512]{1,0:T(8,128)(2,1)S(1)} copy-done((bf16[512,512]{1,0:T(8,128)(2,1)S(1)}, bf16[512,512]{1,0:T(8,128)(2,1)}, u32[]{:S(2)}) %copy-start.1) | copy-done | bytes 524312
  41.7 1.3 %shard_map.153.part_ref = f32[512,512]{1,0:T(8,128)S(1)} custom-call(s32[4,128]{1,0:T(4,128)S(1)} %bitcast.15, bf16[1024,512]{1,0:T(8,128)(2,1)S(1)} %copy-done, bf16[512,512]{1,0:T(8,128)(2,1)S(1)} %copy-done.1, bf16[512,128]{1,0:T(8,128)(2,1)S(1)} %copy-done.2, bf16[128,512]{1,0:T(8,128)(2,1)S(1)} %copy-done.3), custom_call_target="tpu_custom_call" | custom-call | tf_op jit(solution)/shard_map/pallas_call | solution.py:250
  43.1 22.4 %all-to-all-done.1 = bf16[16,64,512]{2,1,0:T(8,128)(2,1)S(1)} async-done(((bf16[16,64,512]{2,1,0:T(8,128)(2,1)}), bf16[16,64,512]{2,1,0:T(8,128)(2,1)S(1)}, u32[]{:S(2)}, u32[]{:S(2)}) %all-to-all-start.1) | async-done | bytes 1048608 | tf_op jit(solution)/shard_map/all_to_all | solution.py:372
  65.5 0.0 copy-done.5
  65.5 1.8 %shard_map.154 = f32[1,512]{1,0:T(1,128)} custom-call(s32[4,128]{1,0:T(4,128)S(1)} %get-tuple-element.21.place_ref, bf16[1024,512]{1,0:T(8,128)(2,1)S(1)} %bitcast.13, f32[512,512]{1,0:T(8,128)S(1)} %shard_map.153.part_ref, f32[1,512]{1,0:T(1,128)S(1)} %bitcast.16), custom_call_target="tpu_custom_call" | custom-call | tf_op jit(solution)/shard_map/pallas_call | solution.py:250
Async XLA Ops:
  3.1 12.7 %collective-permute-start.2 = (bf16[144,512]{1,0:T(8,128)(2,1)S(1)}, bf16[144,512]{1,0:T(8,128)(2,1)S(1)}, u32[]{:S(2)}, u32[]{:S(2)}) collective-permute-start(bf16[144,512]{1,0:T(8,128)(2,1)S(1)} %get-tuple-element.19), channel_id=1, source_target_pairs={{0,2},{2,0},{4,6},{6,4},{8,10},{10,8},{12,14},{14,12},{1,3},{3,1},... | collective-permute-start | bytes 442376 | tf_op jit(solution)/shard_map/ppermute | solution.py:273
  4.4 11.4 %collective-permute-start.1 = (bf16[144,512]{1,0:T(8,128)(2,1)S(1)}, bf16[144,512]{1,0:T(8,128)(2,1)S(1)}, u32[]{:S(2)}, u32[]{:S(2)}) collective-permute-start(bf16[144,512]{1,0:T(8,128)(2,1)S(1)} %get-tuple-element.19), channel_id=1, source_target_pairs={{2,4},{4,2},{6,8},{8,6},{10,12},{12,10},{3,5},{5,3},{7,9},{9,7},{1... | collective-permute-start | bytes 442376 | tf_op jit(solution)/shard_map/ppermute | solution.py:273
  6.3 9.5 %collective-permute-start = (bf16[144,512]{1,0:T(8,128)(2,1)S(1)}, bf16[144,512]{1,0:T(8,128)(2,1)S(1)}, u32[]{:S(2)}, u32[]{:S(2)}) collective-permute-start(bf16[144,512]{1,0:T(8,128)(2,1)S(1)} %get-tuple-element.19), channel_id=1, source_target_pairs={{0,1},{1,0},{2,3},{3,2},{4,5},{5,4},{6,7},{7,6},{8,9},{9,8},{10,11... | collective-permute-start | bytes 442376 | tf_op jit(solution)/shard_map/ppermute | solution.py:273
  7.3 24.7 %all-to-all-start = ((s32[16,1,128]{2,1,0:T(1,128)}), s32[16,1,128]{2,1,0:T(1,128)S(1)}, u32[]{:S(2)}, u32[]{:S(2)}) async-start(s32[16,1,128]{2,1,0:T(1,128)} %bitcast.5), calls=%async_computation | async-start | bytes 16384 | tf_op jit(solution)/shard_map/all_to_all | solution.py:325
  34.4 6.2 %copy-start = (bf16[1024,512]{1,0:T(8,128)(2,1)S(1)}, bf16[1024,512]{1,0:T(8,128)(2,1)}, u32[]{:S(2)}) copy-start(bf16[1024,512]{1,0:T(8,128)(2,1)} %get-tuple-element.11.state_ref) | copy-start | bytes 3145732
  34.4 6.2 %copy-start.2 = (bf16[512,128]{1,0:T(8,128)(2,1)S(1)}, bf16[512,128]{1,0:T(8,128)(2,1)}, u32[]{:S(2)}) copy-start(bf16[512,128]{1,0:T(8,128)(2,1)} %contact_ref.1) | copy-start | bytes 393220
  34.4 6.2 %copy-start.3 = (bf16[128,512]{1,0:T(8,128)(2,1)S(1)}, bf16[128,512]{1,0:T(8,128)(2,1)}, u32[]{:S(2)}) copy-start(bf16[128,512]{1,0:T(8,128)(2,1)} %w_ref.1) | copy-start | bytes 393220
  34.5 6.2 %copy-start.4 = (s32[512]{0:T(512)S(1)}, s32[512]{0:T(512)}, u32[]{:S(2)}) copy-start(s32[512]{0:T(512)} %param.18) | copy-start | bytes 6148
  34.5 31.0 %all-to-all-start.1 = ((bf16[16,64,512]{2,1,0:T(8,128)(2,1)}), bf16[16,64,512]{2,1,0:T(8,128)(2,1)S(1)}, u32[]{:S(2)}, u32[]{:S(2)}) async-start(bf16[16,64,512]{2,1,0:T(8,128)(2,1)} %bitcast.7), calls=%async_computation.1 | async-start | bytes 2097152 | tf_op jit(solution)/shard_map/all_to_all | solution.py:372
  40.6 24.8 %copy-start.5 = (f32[512]{0:T(512)S(1)}, f32[512]{0:T(512)}, u32[]{:S(2)}) copy-start(f32[512]{0:T(512)} %param.27) | copy-start | bytes 6148
  40.7 1.0 %copy-start.1 = (bf16[512,512]{1,0:T(8,128)(2,1)S(1)}, bf16[512,512]{1,0:T(8,128)(2,1)}, u32[]{:S(2)}) copy-start(bf16[512,512]{1,0:T(8,128)(2,1)} %w_source_ref.1) | copy-start | bytes 1572868

commit v10 on v8

--- a/solution.py
+++ b/solution.py
@@ -158,6 +158,17 @@
         k_pair = jnp.concatenate([k_pair, key_block], 1)
         return dot_nt(jnp.concatenate([q_ref[span_at, at], bias[span_at]], 1), k_pair)
 
+    def finish(part):
+        at = pl.ds(part * span, span)
+        state = nodes_ref[at, :].astype(F32) + dot(mixed_ref[at, :], w_out_ref[...])
+        state = state.astype(BF16)
+        nodes_ref[at, :] = state
+        out = pltpu.make_async_copy(nodes_ref.at[at], state_hbm.at[at], sent.at[part])
+        out.start()
+        table_ref[at, :] = dot(state, w_target_ref[...]).astype(BF16)
+        return out
+
+    outs = []
     units = [(pair, part) for pair in range(width // PAIR) for part in range(2)]
     following = scores_of(*units[0])
     for step, (pair, part) in enumerate(units):
@@ -170,6 +181,10 @@
             v_ref[pair % 2, keys:, PAIR:] = jnp.where(low_keys, one, values)
         if step + 1 < len(units):
             following = scores_of(*units[step + 1])
+        else:
+            for copy in copies:
+                copy.wait()
+            outs.append(finish(0))
         weights = []
         for half in (scores[:, :keys], scores[:, keys:]):
             fold = half[:, :128]
@@ -183,15 +198,9 @@
         mixed_ref[part * span : (part + 1) * span, pair * PAIR : (pair + 1) * PAIR] = (
             jnp.where(low, even, odd) / total
         ).astype(BF16)
-    for copy in copies:
-        copy.wait()
-    state = nodes_ref[...].astype(F32) + dot(mixed_ref[...], w_out_ref[...])
-    state = state.astype(BF16)
-    nodes_ref[...] = state
-    out = pltpu.make_async_copy(nodes_ref, state_hbm, sent)
-    out.start()
-    table_ref[...] = dot(state, w_target_ref[...]).astype(BF16)
-    out.wait()
+    outs.append(finish(1))
+    for out in outs:
+        out.wait()
 
 
 def answer(request_ref, table_ref, answer_hbm, answer_ref, sent):
@@ -353,7 +362,7 @@
             pltpu.VMEM((rows, width), BF16),
             pltpu.VMEM((2, 2 * keys, 2 * PAIR), BF16),
             pltpu.SemaphoreType.DMA((3,)),
-            pltpu.SemaphoreType.DMA,
+            pltpu.SemaphoreType.DMA((2,)),
         ],
         far_outs=1,
     )

time: 67.5 us -> 70.7 us (1.047)
  Pallas kernels: 25.9 us -> 29.1 us
    pallas_call x6, Pallas kernels: 25.9 us -> 29.1 us  [run(): pl.pallas_call(kernel, out_shape=tuple(outs), in_specs=[left] * far + [sp...]
  transfers between devices with their start and end apart: 5 -> 5, of which waited for: 1 -> 1; matrix products, arithmetic and copies ran while one was open for 0% -> 0% of each run, Pallas kernels for 29% -> 32%
where the time goes in v10:
time: 70.7 us; the launch traced here: 70.3 us
  Pallas kernels  29.1 us (41%)
  waiting for transfers between devices  22.4 us (32%)
  starting transfers between devices  16.9 us (24%)
  local copies, waits for them, and re-layouts  1.07 us (2%)
  between operations  0.79 us (1%)
    pallas_call x6, Pallas kernels, run(): pl.pallas_call(kernel, out_shape=tuple(outs), in_specs=[left] * far + [sp...  29.1 us
    all_to_all x1, waiting for transfers between devices, local(): lax.all_to_all(answers.reshape(bricks, capacity, hidden), ('gy', 'gz'), s...  22.4 us
    all_to_all x1, starting transfers between devices, local(): lax.all_to_all(request, ('gy', 'gz'), split_axis=0, concat_axis=0, tiled=...  6.54 us
    all_to_all x1, starting transfers between devices, local(): lax.all_to_all(answers.reshape(bricks, capacity, hidden), ('gy', 'gz'), s...  6.16 us
    ppermute x3, starting transfers between devices, neighbours(): return [lax.ppermute(block, axis, swaps) for axis, swaps in reversed(steps)]  4.23 us
  transfers between devices with their start and end apart: 5, of which 1 were waited for; matrix products, arithmetic and copies ran while one was open for 0% of the time, Pallas kernels for 32%

profile of v10, /device:TPU:9, one launch (start us, length us, event | category | flops | bytes accessed | tf_op | source)
XLA Modules:
  0.0 70.3 jit_solution(12574115793124330876)
XLA Ops:
  0.6 2.5 %shard_map.149 = (bf16[144,512]{1,0:T(8,128)(2,1)S(1)}, s32[16,128]{1,0:T(8,128)}, s32[4,128]{1,0:T(4,128)S(1)}, bf16[1024,512]{1,0:T(8,128)(2,1)S(1)}, f32[1,51...) custom-call(s32[1,128]{1,0:T(1,128)} %bitcast.21, s32[1,512]{1,0:T(1,128)} %bitcast.17, ...), custom_call_target="tpu_custom_call" | custom-call | tf_op jit(solution)/shard_map/pallas_call | solution.py:258
  3.1 1.3 %collective-permute-start.2 = (bf16[144,512]{1,0:T(8,128)(2,1)S(1)}, bf16[144,512]{1,0:T(8,128)(2,1)S(1)}, u32[]{:S(2)}, u32[]{:S(2)}) collective-permute-start(bf16[144,512]{1,0:T(8,128)(2,1)S(1)} %get-tuple-element.19), channel_id=1, source_target_pairs={{0,2},{2,0},{4,6},{6,4},{8,10},{10,8},{12,14},{14,12},{1,3},{3,1},... | collective-permute-start | bytes 442376 | tf_op jit(solution)/shard_map/ppermute | solution.py:281
  4.4 1.9 %collective-permute-start.1 = (bf16[144,512]{1,0:T(8,128)(2,1)S(1)}, bf16[144,512]{1,0:T(8,128)(2,1)S(1)}, u32[]{:S(2)}, u32[]{:S(2)}) collective-permute-start(bf16[144,512]{1,0:T(8,128)(2,1)S(1)} %get-tuple-element.19), channel_id=1, source_target_pairs={{2,4},{4,2},{6,8},{8,6},{10,12},{12,10},{3,5},{5,3},{7,9},{9,7},{1... | collective-permute-start | bytes 442376 | tf_op jit(solution)/shard_map/ppermute | solution.py:281
  6.3 1.0 %collective-permute-start = (bf16[144,512]{1,0:T(8,128)(2,1)S(1)}, bf16[144,512]{1,0:T(8,128)(2,1)S(1)}, u32[]{:S(2)}, u32[]{:S(2)}) collective-permute-start(bf16[144,512]{1,0:T(8,128)(2,1)S(1)} %get-tuple-element.19), channel_id=1, source_target_pairs={{0,1},{1,0},{2,3},{3,2},{4,5},{5,4},{6,7},{7,6},{8,9},{9,8},{10,11... | collective-permute-start | bytes 442376 | tf_op jit(solution)/shard_map/ppermute | solution.py:281
  7.3 6.5 %all-to-all-start = ((s32[16,1,128]{2,1,0:T(1,128)}), s32[16,1,128]{2,1,0:T(1,128)S(1)}, u32[]{:S(2)}, u32[]{:S(2)}) async-start(s32[16,1,128]{2,1,0:T(1,128)} %bitcast.5), calls=%async_computation | async-start | bytes 16384 | tf_op jit(solution)/shard_map/all_to_all | solution.py:333
  13.9 1.9 %shard_map.150 = (bf16[1024,512]{1,0:T(8,128)(2,1)S(1)}, bf16[1024,1024]{1,0:T(8,128)(2,1)S(1)}) custom-call(bf16[1024,512]{1,0:T(8,128)(2,1)S(1)} %get-tuple-element.16.nodes_ref, f32[1,512]{1,0:T(1,128)S(1)} %get-tuple-element.13.gain_ref.refs_3_, bf16[512,1536]{1,0:T(8,128)(2,1)S(1)} %get-tuple-element.15.w_ref.refs_5_), custom_call_target="tpu_custom_call" | custom-call | tf_op jit(solution)/shard_map/pallas_call | solution.py:258
  15.8 0.0 collective-permute-done.2.refs_10_
  15.8 0.0 collective-permute-done.1.refs_9_
  15.8 0.0 collective-permute-done.refs_8_
  15.8 19.4 %shard_map.151 = (bf16[1024,512]{1,0:T(8,128)(2,1)}, bf16[1024,512]{1,0:T(8,128)(2,1)S(1)}) custom-call(bf16[512,512]{1,0:T(8,128)(2,1)} %refs_0_.1, bf16[512,512]{1,0:T(8,128)(2,1)} %refs_1_.1, bf16[1024,512]{1,0:T(8,128)(2,1)} %refs_2_.1, f32[1,512]{1,0:T(1,128)S(1)} %get-tuple-element.13.gain_ref.refs_3_, s32[8,8]{1,0:T(8,128)S(1)} %get-tuple-element.14.refs_4_, ...), custom_call_target="tpu_custom_call" | custom-call | tf_op jit(solution)/shard_map/pallas_call | solution.py:258
  35.2 0.0 all-to-all-done
  35.2 2.2 %shard_map.152 = bf16[1024,512]{1,0:T(8,128)(2,1)} custom-call(s32[16,128]{1,0:T(8,128)S(1)} %bitcast.14, bf16[1024,512]{1,0:T(8,128)(2,1)S(1)} %get-tuple-element.23.table_ref), custom_call_target="tpu_custom_call" | custom-call | tf_op jit(solution)/shard_map/pallas_call | solution.py:258
  37.4 0.0 copy-start
  37.4 0.0 copy-start.2
  37.5 0.0 copy-start.3
  37.5 0.0 copy-start.4
  37.5 6.2 %all-to-all-start.1 = ((bf16[16,64,512]{2,1,0:T(8,128)(2,1)}), bf16[16,64,512]{2,1,0:T(8,128)(2,1)S(1)}, u32[]{:S(2)}, u32[]{:S(2)}) async-start(bf16[16,64,512]{2,1,0:T(8,128)(2,1)} %bitcast.7), calls=%async_computation.1 | async-start | bytes 2097152 | tf_op jit(solution)/shard_map/all_to_all | solution.py:380
  43.6 0.0 copy-start.5
  43.6 0.0 copy-done
  43.7 0.0 copy-done.2
  43.7 0.0 copy-done.3
  43.7 0.0 copy-done.4
  43.7 0.0 copy-start.1
  43.7 1.0 %copy-done.1 = bf16[512,512]{1,0:T(8,128)(2,1)S(1)} copy-done((bf16[512,512]{1,0:T(8,128)(2,1)S(1)}, bf16[512,512]{1,0:T(8,128)(2,1)}, u32[]{:S(2)}) %copy-start.1) | copy-done | bytes 524312
  44.7 1.3 %shard_map.153.part_ref = f32[512,512]{1,0:T(8,128)S(1)} custom-call(s32[4,128]{1,0:T(4,128)S(1)} %bitcast.15, bf16[1024,512]{1,0:T(8,128)(2,1)S(1)} %copy-done, bf16[512,512]{1,0:T(8,128)(2,1)S(1)} %copy-done.1, bf16[512,128]{1,0:T(8,128)(2,1)S(1)} %copy-done.2, bf16[128,512]{1,0:T(8,128)(2,1)S(1)} %copy-done.3), custom_call_target="tpu_custom_call" | custom-call | tf_op jit(solution)/shard_map/pallas_call | solution.py:258
  46.1 22.4 %all-to-all-done.1 = bf16[16,64,512]{2,1,0:T(8,128)(2,1)S(1)} async-done(((bf16[16,64,512]{2,1,0:T(8,128)(2,1)}), bf16[16,64,512]{2,1,0:T(8,128)(2,1)S(1)}, u32[]{:S(2)}, u32[]{:S(2)}) %all-to-all-start.1) | async-done | bytes 1048608 | tf_op jit(solution)/shard_map/all_to_all | solution.py:380
  68.5 0.0 copy-done.5
  68.5 1.8 %shard_map.154 = f32[1,512]{1,0:T(1,128)} custom-call(s32[4,128]{1,0:T(4,128)S(1)} %get-tuple-element.21.place_ref, bf16[1024,512]{1,0:T(8,128)(2,1)S(1)} %bitcast.13, f32[512,512]{1,0:T(8,128)S(1)} %shard_map.153.part_ref, f32[1,512]{1,0:T(1,128)S(1)} %bitcast.16), custom_call_target="tpu_custom_call" | custom-call | tf_op jit(solution)/shard_map/pallas_call | solution.py:258
Async XLA Ops:
  3.1 12.7 %collective-permute-start.2 = (bf16[144,512]{1,0:T(8,128)(2,1)S(1)}, bf16[144,512]{1,0:T(8,128)(2,1)S(1)}, u32[]{:S(2)}, u32[]{:S(2)}) collective-permute-start(bf16[144,512]{1,0:T(8,128)(2,1)S(1)} %get-tuple-element.19), channel_id=1, source_target_pairs={{0,2},{2,0},{4,6},{6,4},{8,10},{10,8},{12,14},{14,12},{1,3},{3,1},... | collective-permute-start | bytes 442376 | tf_op jit(solution)/shard_map/ppermute | solution.py:281
  4.4 11.4 %collective-permute-start.1 = (bf16[144,512]{1,0:T(8,128)(2,1)S(1)}, bf16[144,512]{1,0:T(8,128)(2,1)S(1)}, u32[]{:S(2)}, u32[]{:S(2)}) collective-permute-start(bf16[144,512]{1,0:T(8,128)(2,1)S(1)} %get-tuple-element.19), channel_id=1, source_target_pairs={{2,4},{4,2},{6,8},{8,6},{10,12},{12,10},{3,5},{5,3},{7,9},{9,7},{1... | collective-permute-start | bytes 442376 | tf_op jit(solution)/shard_map/ppermute | solution.py:281
  6.3 9.5 %collective-permute-start = (bf16[144,512]{1,0:T(8,128)(2,1)S(1)}, bf16[144,512]{1,0:T(8,128)(2,1)S(1)}, u32[]{:S(2)}, u32[]{:S(2)}) collective-permute-start(bf16[144,512]{1,0:T(8,128)(2,1)S(1)} %get-tuple-element.19), channel_id=1, source_target_pairs={{0,1},{1,0},{2,3},{3,2},{4,5},{5,4},{6,7},{7,6},{8,9},{9,8},{10,11... | collective-permute-start | bytes 442376 | tf_op jit(solution)/shard_map/ppermute | solution.py:281
  7.3 27.9 %all-to-all-start = ((s32[16,1,128]{2,1,0:T(1,128)}), s32[16,1,128]{2,1,0:T(1,128)S(1)}, u32[]{:S(2)}, u32[]{:S(2)}) async-start(s32[16,1,128]{2,1,0:T(1,128)} %bitcast.5), calls=%async_computation | async-start | bytes 16384 | tf_op jit(solution)/shard_map/all_to_all | solution.py:333
  37.4 6.2 %copy-start = (bf16[1024,512]{1,0:T(8,128)(2,1)S(1)}, bf16[1024,512]{1,0:T(8,128)(2,1)}, u32[]{:S(2)}) copy-start(bf16[1024,512]{1,0:T(8,128)(2,1)} %get-tuple-element.11.state_ref) | copy-start | bytes 3145732
  37.4 6.2 %copy-start.2 = (bf16[512,128]{1,0:T(8,128)(2,1)S(1)}, bf16[512,128]{1,0:T(8,128)(2,1)}, u32[]{:S(2)}) copy-start(bf16[512,128]{1,0:T(8,128)(2,1)} %contact_ref.1) | copy-start | bytes 393220
  37.5 6.2 %copy-start.3 = (bf16[128,512]{1,0:T(8,128)(2,1)S(1)}, bf16[128,512]{1,0:T(8,128)(2,1)}, u32[]{:S(2)}) copy-start(bf16[128,512]{1,0:T(8,128)(2,1)} %w_ref.1) | copy-start | bytes 393220
  37.5 6.2 %copy-start.4 = (s32[512]{0:T(512)S(1)}, s32[512]{0:T(512)}, u32[]{:S(2)}) copy-start(s32[512]{0:T(512)} %param.18) | copy-start | bytes 6148
  37.5 31.0 %all-to-all-start.1 = ((bf16[16,64,512]{2,1,0:T(8,128)(2,1)}), bf16[16,64,512]{2,1,0:T(8,128)(2,1)S(1)}, u32[]{:S(2)}, u32[]{:S(2)}) async-start(bf16[16,64,512]{2,1,0:T(8,128)(2,1)} %bitcast.7), calls=%async_computation.1 | async-start | bytes 2097152 | tf_op jit(solution)/shard_map/all_to_all | solution.py:380
  43.6 24.8 %copy-start.5 = (f32[512]{0:T(512)S(1)}, f32[512]{0:T(512)}, u32[]{:S(2)}) copy-start(f32[512]{0:T(512)} %param.27) | copy-start | bytes 6148
  43.7 1.0 %copy-start.1 = (bf16[512,512]{1,0:T(8,128)(2,1)S(1)}, bf16[512,512]{1,0:T(8,128)(2,1)}, u32[]{:S(2)}) copy-start(bf16[512,512]{1,0:T(8,128)(2,1)} %w_source_ref.1) | copy-start | bytes 1572868

commit v11 on v8

--- a/solution.py
+++ b/solution.py
@@ -158,6 +158,8 @@
         k_pair = jnp.concatenate([k_pair, key_block], 1)
         return dot_nt(jnp.concatenate([q_ref[span_at, at], bias[span_at]], 1), k_pair)
 
+    copies[0].wait()
+    copies[1].wait()
     units = [(pair, part) for pair in range(width // PAIR) for part in range(2)]
     following = scores_of(*units[0])
     for step, (pair, part) in enumerate(units):
@@ -183,9 +185,9 @@
         mixed_ref[part * span : (part + 1) * span, pair * PAIR : (pair + 1) * PAIR] = (
             jnp.where(low, even, odd) / total
         ).astype(BF16)
-    for copy in copies:
-        copy.wait()
-    state = nodes_ref[...].astype(F32) + dot(mixed_ref[...], w_out_ref[...])
+    update = dot(mixed_ref[...], w_out_ref[...])
+    copies[2].wait()
+    state = nodes_ref[...].astype(F32) + update
     state = state.astype(BF16)
     nodes_ref[...] = state
     out = pltpu.make_async_copy(nodes_ref, state_hbm, sent)

time: 67.5 us -> 68.7 us (1.018)
  Pallas kernels: 25.9 us -> 27.2 us
    pallas_call x6, Pallas kernels: 25.9 us -> 27.2 us  [run(): pl.pallas_call(kernel, out_shape=tuple(outs), in_specs=[left] * far + [sp...]
  transfers between devices with their start and end apart: 5 -> 5, of which waited for: 1 -> 1; matrix products, arithmetic and copies ran while one was open for 0% -> 0% of each run, Pallas kernels for 29% -> 30%
where the time goes in v11:
time: 68.7 us; the launch traced here: 68.4 us
  Pallas kernels  27.2 us (40%)
  waiting for transfers between devices  22.4 us (33%)
  starting transfers between devices  16.9 us (25%)
  local copies, waits for them, and re-layouts  1.07 us (2%)
  between operations  0.79 us (1%)
    pallas_call x6, Pallas kernels, run(): pl.pallas_call(kernel, out_shape=tuple(outs), in_specs=[left] * far + [sp...  27.2 us
    all_to_all x1, waiting for transfers between devices, local(): lax.all_to_all(answers.reshape(bricks, capacity, hidden), ('gy', 'gz'), s...  22.4 us
    all_to_all x1, starting transfers between devices, local(): lax.all_to_all(request, ('gy', 'gz'), split_axis=0, concat_axis=0, tiled=...  6.54 us
    all_to_all x1, starting transfers between devices, local(): lax.all_to_all(answers.reshape(bricks, capacity, hidden), ('gy', 'gz'), s...  6.16 us
    ppermute x3, starting transfers between devices, neighbours(): return [lax.ppermute(block, axis, swaps) for axis, swaps in reversed(steps)]  4.23 us
  transfers between devices with their start and end apart: 5, of which 1 were waited for; matrix products, arithmetic and copies ran while one was open for 0% of the time, Pallas kernels for 30%

profile of v11, /device:TPU:9, one launch (start us, length us, event | category | flops | bytes accessed | tf_op | source)
XLA Modules:
  0.0 68.4 jit_solution(17600514403561318009)
XLA Ops:
  0.6 2.5 %shard_map.149 = (bf16[144,512]{1,0:T(8,128)(2,1)S(1)}, s32[16,128]{1,0:T(8,128)}, s32[4,128]{1,0:T(4,128)S(1)}, bf16[1024,512]{1,0:T(8,128)(2,1)S(1)}, f32[1,51...) custom-call(s32[1,128]{1,0:T(1,128)} %bitcast.21, s32[1,512]{1,0:T(1,128)} %bitcast.17, ...), custom_call_target="tpu_custom_call" | custom-call | tf_op jit(solution)/shard_map/pallas_call | solution.py:251
  3.1 1.3 %collective-permute-start.2 = (bf16[144,512]{1,0:T(8,128)(2,1)S(1)}, bf16[144,512]{1,0:T(8,128)(2,1)S(1)}, u32[]{:S(2)}, u32[]{:S(2)}) collective-permute-start(bf16[144,512]{1,0:T(8,128)(2,1)S(1)} %get-tuple-element.19), channel_id=1, source_target_pairs={{0,2},{2,0},{4,6},{6,4},{8,10},{10,8},{12,14},{14,12},{1,3},{3,1},... | collective-permute-start | bytes 442376 | tf_op jit(solution)/shard_map/ppermute | solution.py:274
  4.4 1.9 %collective-permute-start.1 = (bf16[144,512]{1,0:T(8,128)(2,1)S(1)}, bf16[144,512]{1,0:T(8,128)(2,1)S(1)}, u32[]{:S(2)}, u32[]{:S(2)}) collective-permute-start(bf16[144,512]{1,0:T(8,128)(2,1)S(1)} %get-tuple-element.19), channel_id=1, source_target_pairs={{2,4},{4,2},{6,8},{8,6},{10,12},{12,10},{3,5},{5,3},{7,9},{9,7},{1... | collective-permute-start | bytes 442376 | tf_op jit(solution)/shard_map/ppermute | solution.py:274
  6.3 1.0 %collective-permute-start = (bf16[144,512]{1,0:T(8,128)(2,1)S(1)}, bf16[144,512]{1,0:T(8,128)(2,1)S(1)}, u32[]{:S(2)}, u32[]{:S(2)}) collective-permute-start(bf16[144,512]{1,0:T(8,128)(2,1)S(1)} %get-tuple-element.19), channel_id=1, source_target_pairs={{0,1},{1,0},{2,3},{3,2},{4,5},{5,4},{6,7},{7,6},{8,9},{9,8},{10,11... | collective-permute-start | bytes 442376 | tf_op jit(solution)/shard_map/ppermute | solution.py:274
  7.3 6.5 %all-to-all-start = ((s32[16,1,128]{2,1,0:T(1,128)}), s32[16,1,128]{2,1,0:T(1,128)S(1)}, u32[]{:S(2)}, u32[]{:S(2)}) async-start(s32[16,1,128]{2,1,0:T(1,128)} %bitcast.5), calls=%async_computation | async-start | bytes 16384 | tf_op jit(solution)/shard_map/all_to_all | solution.py:326
  13.9 1.9 %shard_map.150 = (bf16[1024,512]{1,0:T(8,128)(2,1)S(1)}, bf16[1024,1024]{1,0:T(8,128)(2,1)S(1)}) custom-call(bf16[1024,512]{1,0:T(8,128)(2,1)S(1)} %get-tuple-element.16.nodes_ref, f32[1,512]{1,0:T(1,128)S(1)} %get-tuple-element.13.gain_ref.refs_3_, bf16[512,1536]{1,0:T(8,128)(2,1)S(1)} %get-tuple-element.15.w_ref.refs_5_), custom_call_target="tpu_custom_call" | custom-call | tf_op jit(solution)/shard_map/pallas_call | solution.py:251
  15.8 0.0 collective-permute-done.2.refs_10_
  15.8 0.0 collective-permute-done.1.refs_9_
  15.8 0.0 collective-permute-done.refs_8_
  15.8 17.5 %shard_map.151 = (bf16[1024,512]{1,0:T(8,128)(2,1)}, bf16[1024,512]{1,0:T(8,128)(2,1)S(1)}) custom-call(bf16[512,512]{1,0:T(8,128)(2,1)} %refs_0_.1, bf16[512,512]{1,0:T(8,128)(2,1)} %refs_1_.1, bf16[1024,512]{1,0:T(8,128)(2,1)} %refs_2_.1, f32[1,512]{1,0:T(1,128)S(1)} %get-tuple-element.13.gain_ref.refs_3_, s32[8,8]{1,0:T(8,128)S(1)} %get-tuple-element.14.refs_4_, ...), custom_call_target="tpu_custom_call" | custom-call | tf_op jit(solution)/shard_map/pallas_call | solution.py:251
  33.3 0.0 all-to-all-done
  33.3 2.2 %shard_map.152 = bf16[1024,512]{1,0:T(8,128)(2,1)} custom-call(s32[16,128]{1,0:T(8,128)S(1)} %bitcast.14, bf16[1024,512]{1,0:T(8,128)(2,1)S(1)} %get-tuple-element.23.table_ref), custom_call_target="tpu_custom_call" | custom-call | tf_op jit(solution)/shard_map/pallas_call | solution.py:251
  35.5 0.0 copy-start
  35.5 0.0 copy-start.2
  35.5 0.0 copy-start.3
  35.5 0.0 copy-start.4
  35.5 6.2 %all-to-all-start.1 = ((bf16[16,64,512]{2,1,0:T(8,128)(2,1)}), bf16[16,64,512]{2,1,0:T(8,128)(2,1)S(1)}, u32[]{:S(2)}, u32[]{:S(2)}) async-start(bf16[16,64,512]{2,1,0:T(8,128)(2,1)} %bitcast.7), calls=%async_computation.1 | async-start | bytes 2097152 | tf_op jit(solution)/shard_map/all_to_all | solution.py:373
  41.7 0.0 copy-start.5
  41.7 0.0 copy-done
  41.7 0.0 copy-done.2
  41.7 0.0 copy-done.3
  41.7 0.0 copy-done.4
  41.8 0.0 copy-start.1
  41.8 1.0 %copy-done.1 = bf16[512,512]{1,0:T(8,128)(2,1)S(1)} copy-done((bf16[512,512]{1,0:T(8,128)(2,1)S(1)}, bf16[512,512]{1,0:T(8,128)(2,1)}, u32[]{:S(2)}) %copy-start.1) | copy-done | bytes 524312
  42.8 1.3 %shard_map.153.part_ref = f32[512,512]{1,0:T(8,128)S(1)} custom-call(s32[4,128]{1,0:T(4,128)S(1)} %bitcast.15, bf16[1024,512]{1,0:T(8,128)(2,1)S(1)} %copy-done, bf16[512,512]{1,0:T(8,128)(2,1)S(1)} %copy-done.1, bf16[512,128]{1,0:T(8,128)(2,1)S(1)} %copy-done.2, bf16[128,512]{1,0:T(8,128)(2,1)S(1)} %copy-done.3), custom_call_target="tpu_custom_call" | custom-call | tf_op jit(solution)/shard_map/pallas_call | solution.py:251
  44.1 22.4 %all-to-all-done.1 = bf16[16,64,512]{2,1,0:T(8,128)(2,1)S(1)} async-done(((bf16[16,64,512]{2,1,0:T(8,128)(2,1)}), bf16[16,64,512]{2,1,0:T(8,128)(2,1)S(1)}, u32[]{:S(2)}, u32[]{:S(2)}) %all-to-all-start.1) | async-done | bytes 1048608 | tf_op jit(solution)/shard_map/all_to_all | solution.py:373
  66.5 0.0 copy-done.5
  66.6 1.9 %shard_map.154 = f32[1,512]{1,0:T(1,128)} custom-call(s32[4,128]{1,0:T(4,128)S(1)} %get-tuple-element.21.place_ref, bf16[1024,512]{1,0:T(8,128)(2,1)S(1)} %bitcast.13, f32[512,512]{1,0:T(8,128)S(1)} %shard_map.153.part_ref, f32[1,512]{1,0:T(1,128)S(1)} %bitcast.16), custom_call_target="tpu_custom_call" | custom-call | tf_op jit(solution)/shard_map/pallas_call | solution.py:251
Async XLA Ops:
  3.1 12.7 %collective-permute-start.2 = (bf16[144,512]{1,0:T(8,128)(2,1)S(1)}, bf16[144,512]{1,0:T(8,128)(2,1)S(1)}, u32[]{:S(2)}, u32[]{:S(2)}) collective-permute-start(bf16[144,512]{1,0:T(8,128)(2,1)S(1)} %get-tuple-element.19), channel_id=1, source_target_pairs={{0,2},{2,0},{4,6},{6,4},{8,10},{10,8},{12,14},{14,12},{1,3},{3,1},... | collective-permute-start | bytes 442376 | tf_op jit(solution)/shard_map/ppermute | solution.py:274
  4.4 11.4 %collective-permute-start.1 = (bf16[144,512]{1,0:T(8,128)(2,1)S(1)}, bf16[144,512]{1,0:T(8,128)(2,1)S(1)}, u32[]{:S(2)}, u32[]{:S(2)}) collective-permute-start(bf16[144,512]{1,0:T(8,128)(2,1)S(1)} %get-tuple-element.19), channel_id=1, source_target_pairs={{2,4},{4,2},{6,8},{8,6},{10,12},{12,10},{3,5},{5,3},{7,9},{9,7},{1... | collective-permute-start | bytes 442376 | tf_op jit(solution)/shard_map/ppermute | solution.py:274
  6.3 9.5 %collective-permute-start = (bf16[144,512]{1,0:T(8,128)(2,1)S(1)}, bf16[144,512]{1,0:T(8,128)(2,1)S(1)}, u32[]{:S(2)}, u32[]{:S(2)}) collective-permute-start(bf16[144,512]{1,0:T(8,128)(2,1)S(1)} %get-tuple-element.19), channel_id=1, source_target_pairs={{0,1},{1,0},{2,3},{3,2},{4,5},{5,4},{6,7},{7,6},{8,9},{9,8},{10,11... | collective-permute-start | bytes 442376 | tf_op jit(solution)/shard_map/ppermute | solution.py:274
  7.3 25.9 %all-to-all-start = ((s32[16,1,128]{2,1,0:T(1,128)}), s32[16,1,128]{2,1,0:T(1,128)S(1)}, u32[]{:S(2)}, u32[]{:S(2)}) async-start(s32[16,1,128]{2,1,0:T(1,128)} %bitcast.5), calls=%async_computation | async-start | bytes 16384 | tf_op jit(solution)/shard_map/all_to_all | solution.py:326
  35.5 6.2 %copy-start = (bf16[1024,512]{1,0:T(8,128)(2,1)S(1)}, bf16[1024,512]{1,0:T(8,128)(2,1)}, u32[]{:S(2)}) copy-start(bf16[1024,512]{1,0:T(8,128)(2,1)} %get-tuple-element.11.state_ref) | copy-start | bytes 3145732
  35.5 6.2 %copy-start.2 = (bf16[512,128]{1,0:T(8,128)(2,1)S(1)}, bf16[512,128]{1,0:T(8,128)(2,1)}, u32[]{:S(2)}) copy-start(bf16[512,128]{1,0:T(8,128)(2,1)} %contact_ref.1) | copy-start | bytes 393220
  35.5 6.2 %copy-start.3 = (bf16[128,512]{1,0:T(8,128)(2,1)S(1)}, bf16[128,512]{1,0:T(8,128)(2,1)}, u32[]{:S(2)}) copy-start(bf16[128,512]{1,0:T(8,128)(2,1)} %w_ref.1) | copy-start | bytes 393220
  35.5 6.2 %copy-start.4 = (s32[512]{0:T(512)S(1)}, s32[512]{0:T(512)}, u32[]{:S(2)}) copy-start(s32[512]{0:T(512)} %param.18) | copy-start | bytes 6148
  35.5 31.0 %all-to-all-start.1 = ((bf16[16,64,512]{2,1,0:T(8,128)(2,1)}), bf16[16,64,512]{2,1,0:T(8,128)(2,1)S(1)}, u32[]{:S(2)}, u32[]{:S(2)}) async-start(bf16[16,64,512]{2,1,0:T(8,128)(2,1)} %bitcast.7), calls=%async_computation.1 | async-start | bytes 2097152 | tf_op jit(solution)/shard_map/all_to_all | solution.py:373
  41.7 24.8 %copy-start.5 = (f32[512]{0:T(512)S(1)}, f32[512]{0:T(512)}, u32[]{:S(2)}) copy-start(f32[512]{0:T(512)} %param.27) | copy-start | bytes 6148
  41.8 1.0 %copy-start.1 = (bf16[512,512]{1,0:T(8,128)(2,1)S(1)}, bf16[512,512]{1,0:T(8,128)(2,1)}, u32[]{:S(2)}) copy-start(bf16[512,512]{1,0:T(8,128)(2,1)} %w_source_ref.1) | copy-start | bytes 1572868

commit v12 on v8

--- a/solution.py
+++ b/solution.py
@@ -200,16 +200,16 @@
     columns = jnp.transpose(request_ref[...])
     lanes = iota((capacity, table_ref.shape[0]), 1)
     copies = []
-    for first in range(0, bricks, bricks // 4):
+    for first in range(0, bricks, bricks // 2):
         hot = [
             ones_where(columns[:capacity, b : b + 1] == lanes)
-            for b in range(first, first + bricks // 4)
+            for b in range(first, first + bricks // 2)
         ]
-        at = pl.ds(first * capacity, bricks // 4 * capacity)
+        at = pl.ds(first * capacity, bricks // 2 * capacity)
         answer_ref[at, :] = dot(jnp.concatenate(hot, 0), table_ref[...]).astype(BF16)
         copies.append(
             pltpu.make_async_copy(
-                answer_ref.at[at], answer_hbm.at[at], sent.at[first // (bricks // 4)]
+                answer_ref.at[at], answer_hbm.at[at], sent.at[first // (bricks // 2)]
             )
         )
         copies[-1].start()

time: 67.5 us -> 67.5 us (level)
  no operation moved by 1% of the time
where the time goes in v12:
time: 67.5 us; the launch traced here: 67.2 us
  Pallas kernels  25.9 us (38%)
  waiting for transfers between devices  22.4 us (33%)
  starting transfers between devices  16.9 us (25%)
  local copies, waits for them, and re-layouts  1.07 us (2%)
  between operations  0.79 us (1%)
    pallas_call x6, Pallas kernels, run(): pl.pallas_call(kernel, out_shape=tuple(outs), in_specs=[left] * far + [sp...  25.9 us
    all_to_all x1, waiting for transfers between devices, local(): lax.all_to_all(answers.reshape(bricks, capacity, hidden), ('gy', 'gz'), s...  22.4 us
    all_to_all x1, starting transfers between devices, local(): lax.all_to_all(request, ('gy', 'gz'), split_axis=0, concat_axis=0, tiled=...  6.54 us
    all_to_all x1, starting transfers between devices, local(): lax.all_to_all(answers.reshape(bricks, capacity, hidden), ('gy', 'gz'), s...  6.16 us
    ppermute x3, starting transfers between devices, neighbours(): return [lax.ppermute(block, axis, swaps) for axis, swaps in reversed(steps)]  4.23 us
  transfers between devices with their start and end apart: 5, of which 1 were waited for; matrix products, arithmetic and copies ran while one was open for 0% of the time, Pallas kernels for 29%

profile of v12, /device:TPU:9, one launch (start us, length us, event | category | flops | bytes accessed | tf_op | source)
XLA Modules:
  0.0 67.2 jit_solution(16032137364034093205)
XLA Ops:
  0.6 2.5 %shard_map.149 = (bf16[144,512]{1,0:T(8,128)(2,1)S(1)}, s32[16,128]{1,0:T(8,128)}, s32[4,128]{1,0:T(4,128)S(1)}, bf16[1024,512]{1,0:T(8,128)(2,1)S(1)}, f32[1,51...) custom-call(s32[1,128]{1,0:T(1,128)} %bitcast.21, s32[1,512]{1,0:T(1,128)} %bitcast.17, ...), custom_call_target="tpu_custom_call" | custom-call | tf_op jit(solution)/shard_map/pallas_call | solution.py:249
  3.1 1.3 %collective-permute-start.2 = (bf16[144,512]{1,0:T(8,128)(2,1)S(1)}, bf16[144,512]{1,0:T(8,128)(2,1)S(1)}, u32[]{:S(2)}, u32[]{:S(2)}) collective-permute-start(bf16[144,512]{1,0:T(8,128)(2,1)S(1)} %get-tuple-element.19), channel_id=1, source_target_pairs={{0,2},{2,0},{4,6},{6,4},{8,10},{10,8},{12,14},{14,12},{1,3},{3,1},... | collective-permute-start | bytes 442376 | tf_op jit(solution)/shard_map/ppermute | solution.py:272
  4.4 1.9 %collective-permute-start.1 = (bf16[144,512]{1,0:T(8,128)(2,1)S(1)}, bf16[144,512]{1,0:T(8,128)(2,1)S(1)}, u32[]{:S(2)}, u32[]{:S(2)}) collective-permute-start(bf16[144,512]{1,0:T(8,128)(2,1)S(1)} %get-tuple-element.19), channel_id=1, source_target_pairs={{2,4},{4,2},{6,8},{8,6},{10,12},{12,10},{3,5},{5,3},{7,9},{9,7},{1... | collective-permute-start | bytes 442376 | tf_op jit(solution)/shard_map/ppermute | solution.py:272
  6.3 1.0 %collective-permute-start = (bf16[144,512]{1,0:T(8,128)(2,1)S(1)}, bf16[144,512]{1,0:T(8,128)(2,1)S(1)}, u32[]{:S(2)}, u32[]{:S(2)}) collective-permute-start(bf16[144,512]{1,0:T(8,128)(2,1)S(1)} %get-tuple-element.19), channel_id=1, source_target_pairs={{0,1},{1,0},{2,3},{3,2},{4,5},{5,4},{6,7},{7,6},{8,9},{9,8},{10,11... | collective-permute-start | bytes 442376 | tf_op jit(solution)/shard_map/ppermute | solution.py:272
  7.3 6.5 %all-to-all-start = ((s32[16,1,128]{2,1,0:T(1,128)}), s32[16,1,128]{2,1,0:T(1,128)S(1)}, u32[]{:S(2)}, u32[]{:S(2)}) async-start(s32[16,1,128]{2,1,0:T(1,128)} %bitcast.5), calls=%async_computation | async-start | bytes 16384 | tf_op jit(solution)/shard_map/all_to_all | solution.py:324
  13.9 1.9 %shard_map.150 = (bf16[1024,512]{1,0:T(8,128)(2,1)S(1)}, bf16[1024,1024]{1,0:T(8,128)(2,1)S(1)}) custom-call(bf16[1024,512]{1,0:T(8,128)(2,1)S(1)} %get-tuple-element.16.nodes_ref, f32[1,512]{1,0:T(1,128)S(1)} %get-tuple-element.13.gain_ref.refs_3_, bf16[512,1536]{1,0:T(8,128)(2,1)S(1)} %get-tuple-element.15.w_ref.refs_5_), custom_call_target="tpu_custom_call" | custom-call | tf_op jit(solution)/shard_map/pallas_call | solution.py:249
  15.8 0.0 collective-permute-done.2.refs_10_
  15.8 0.0 collective-permute-done.1.refs_9_
  15.8 0.0 collective-permute-done.refs_8_
  15.8 16.2 %shard_map.151 = (bf16[1024,512]{1,0:T(8,128)(2,1)}, bf16[1024,512]{1,0:T(8,128)(2,1)S(1)}) custom-call(bf16[512,512]{1,0:T(8,128)(2,1)} %refs_0_.1, bf16[512,512]{1,0:T(8,128)(2,1)} %refs_1_.1, bf16[1024,512]{1,0:T(8,128)(2,1)} %refs_2_.1, f32[1,512]{1,0:T(1,128)S(1)} %get-tuple-element.13.gain_ref.refs_3_, s32[8,8]{1,0:T(8,128)S(1)} %get-tuple-element.14.refs_4_, ...), custom_call_target="tpu_custom_call" | custom-call | tf_op jit(solution)/shard_map/pallas_call | solution.py:249
  32.0 0.0 all-to-all-done
  32.0 2.2 %shard_map.152 = bf16[1024,512]{1,0:T(8,128)(2,1)} custom-call(s32[16,128]{1,0:T(8,128)S(1)} %bitcast.14, bf16[1024,512]{1,0:T(8,128)(2,1)S(1)} %get-tuple-element.23.table_ref), custom_call_target="tpu_custom_call" | custom-call | tf_op jit(solution)/shard_map/pallas_call | solution.py:249
  34.3 0.0 copy-start
  34.3 0.0 copy-start.2
  34.3 0.0 copy-start.3
  34.3 0.0 copy-start.4
  34.3 6.2 %all-to-all-start.1 = ((bf16[16,64,512]{2,1,0:T(8,128)(2,1)}), bf16[16,64,512]{2,1,0:T(8,128)(2,1)S(1)}, u32[]{:S(2)}, u32[]{:S(2)}) async-start(bf16[16,64,512]{2,1,0:T(8,128)(2,1)} %bitcast.7), calls=%async_computation.1 | async-start | bytes 2097152 | tf_op jit(solution)/shard_map/all_to_all | solution.py:371
  40.5 0.0 copy-start.5
  40.5 0.0 copy-done
  40.5 0.0 copy-done.2
  40.5 0.0 copy-done.3
  40.5 0.0 copy-done.4
  40.5 0.0 copy-start.1
  40.5 1.0 %copy-done.1 = bf16[512,512]{1,0:T(8,128)(2,1)S(1)} copy-done((bf16[512,512]{1,0:T(8,128)(2,1)S(1)}, bf16[512,512]{1,0:T(8,128)(2,1)}, u32[]{:S(2)}) %copy-start.1) | copy-done | bytes 524312
  41.6 1.3 %shard_map.153.part_ref = f32[512,512]{1,0:T(8,128)S(1)} custom-call(s32[4,128]{1,0:T(4,128)S(1)} %bitcast.15, bf16[1024,512]{1,0:T(8,128)(2,1)S(1)} %copy-done, bf16[512,512]{1,0:T(8,128)(2,1)S(1)} %copy-done.1, bf16[512,128]{1,0:T(8,128)(2,1)S(1)} %copy-done.2, bf16[128,512]{1,0:T(8,128)(2,1)S(1)} %copy-done.3), custom_call_target="tpu_custom_call" | custom-call | tf_op jit(solution)/shard_map/pallas_call | solution.py:249
  42.9 22.4 %all-to-all-done.1 = bf16[16,64,512]{2,1,0:T(8,128)(2,1)S(1)} async-done(((bf16[16,64,512]{2,1,0:T(8,128)(2,1)}), bf16[16,64,512]{2,1,0:T(8,128)(2,1)S(1)}, u32[]{:S(2)}, u32[]{:S(2)}) %all-to-all-start.1) | async-done | bytes 1048608 | tf_op jit(solution)/shard_map/all_to_all | solution.py:371
  65.3 0.0 copy-done.5
  65.3 1.8 %shard_map.154 = f32[1,512]{1,0:T(1,128)} custom-call(s32[4,128]{1,0:T(4,128)S(1)} %get-tuple-element.21.place_ref, bf16[1024,512]{1,0:T(8,128)(2,1)S(1)} %bitcast.13, f32[512,512]{1,0:T(8,128)S(1)} %shard_map.153.part_ref, f32[1,512]{1,0:T(1,128)S(1)} %bitcast.16), custom_call_target="tpu_custom_call" | custom-call | tf_op jit(solution)/shard_map/pallas_call | solution.py:249
Async XLA Ops:
  3.1 12.7 %collective-permute-start.2 = (bf16[144,512]{1,0:T(8,128)(2,1)S(1)}, bf16[144,512]{1,0:T(8,128)(2,1)S(1)}, u32[]{:S(2)}, u32[]{:S(2)}) collective-permute-start(bf16[144,512]{1,0:T(8,128)(2,1)S(1)} %get-tuple-element.19), channel_id=1, source_target_pairs={{0,2},{2,0},{4,6},{6,4},{8,10},{10,8},{12,14},{14,12},{1,3},{3,1},... | collective-permute-start | bytes 442376 | tf_op jit(solution)/shard_map/ppermute | solution.py:272
  4.4 11.4 %collective-permute-start.1 = (bf16[144,512]{1,0:T(8,128)(2,1)S(1)}, bf16[144,512]{1,0:T(8,128)(2,1)S(1)}, u32[]{:S(2)}, u32[]{:S(2)}) collective-permute-start(bf16[144,512]{1,0:T(8,128)(2,1)S(1)} %get-tuple-element.19), channel_id=1, source_target_pairs={{2,4},{4,2},{6,8},{8,6},{10,12},{12,10},{3,5},{5,3},{7,9},{9,7},{1... | collective-permute-start | bytes 442376 | tf_op jit(solution)/shard_map/ppermute | solution.py:272
  6.3 9.5 %collective-permute-start = (bf16[144,512]{1,0:T(8,128)(2,1)S(1)}, bf16[144,512]{1,0:T(8,128)(2,1)S(1)}, u32[]{:S(2)}, u32[]{:S(2)}) collective-permute-start(bf16[144,512]{1,0:T(8,128)(2,1)S(1)} %get-tuple-element.19), channel_id=1, source_target_pairs={{0,1},{1,0},{2,3},{3,2},{4,5},{5,4},{6,7},{7,6},{8,9},{9,8},{10,11... | collective-permute-start | bytes 442376 | tf_op jit(solution)/shard_map/ppermute | solution.py:272
  7.3 24.7 %all-to-all-start = ((s32[16,1,128]{2,1,0:T(1,128)}), s32[16,1,128]{2,1,0:T(1,128)S(1)}, u32[]{:S(2)}, u32[]{:S(2)}) async-start(s32[16,1,128]{2,1,0:T(1,128)} %bitcast.5), calls=%async_computation | async-start | bytes 16384 | tf_op jit(solution)/shard_map/all_to_all | solution.py:324
  34.3 6.2 %copy-start = (bf16[1024,512]{1,0:T(8,128)(2,1)S(1)}, bf16[1024,512]{1,0:T(8,128)(2,1)}, u32[]{:S(2)}) copy-start(bf16[1024,512]{1,0:T(8,128)(2,1)} %get-tuple-element.11.state_ref) | copy-start | bytes 3145732
  34.3 6.2 %copy-start.2 = (bf16[512,128]{1,0:T(8,128)(2,1)S(1)}, bf16[512,128]{1,0:T(8,128)(2,1)}, u32[]{:S(2)}) copy-start(bf16[512,128]{1,0:T(8,128)(2,1)} %contact_ref.1) | copy-start | bytes 393220
  34.3 6.2 %copy-start.3 = (bf16[128,512]{1,0:T(8,128)(2,1)S(1)}, bf16[128,512]{1,0:T(8,128)(2,1)}, u32[]{:S(2)}) copy-start(bf16[128,512]{1,0:T(8,128)(2,1)} %w_ref.1) | copy-start | bytes 393220
  34.3 6.2 %copy-start.4 = (s32[512]{0:T(512)S(1)}, s32[512]{0:T(512)}, u32[]{:S(2)}) copy-start(s32[512]{0:T(512)} %param.18) | copy-start | bytes 6148
  34.3 31.0 %all-to-all-start.1 = ((bf16[16,64,512]{2,1,0:T(8,128)(2,1)}), bf16[16,64,512]{2,1,0:T(8,128)(2,1)S(1)}, u32[]{:S(2)}, u32[]{:S(2)}) async-start(bf16[16,64,512]{2,1,0:T(8,128)(2,1)} %bitcast.7), calls=%async_computation.1 | async-start | bytes 2097152 | tf_op jit(solution)/shard_map/all_to_all | solution.py:371
  40.5 24.8 %copy-start.5 = (f32[512]{0:T(512)S(1)}, f32[512]{0:T(512)}, u32[]{:S(2)}) copy-start(f32[512]{0:T(512)} %param.27) | copy-start | bytes 6148
  40.5 1.0 %copy-start.1 = (bf16[512,512]{1,0:T(8,128)(2,1)S(1)}, bf16[512,512]{1,0:T(8,128)(2,1)}, u32[]{:S(2)}) copy-start(bf16[512,512]{1,0:T(8,128)(2,1)} %w_source_ref.1) | copy-start | bytes 1572868
